TPU v7x, 128 devices: a whole 4x4x4 slice. The times are simulated.
128 devices in a mesh: row: 8 (over y, x_lo), col: 16 (over z, x_hi, core).
Axes of the slice: x: 4 (x_hi: 2, x_lo: 2; x = x_hi * 2 + x_lo), y: 4, z: 4, core: 2. Of those that a mesh axis runs over, the one named last changes fastest.
Arguments:
- context_heads: bfloat16 [16384, 8192], P('row', 'col'), may hold values from -6 to 6
- teacher_proj: bfloat16 [8192, 4096], P('col', 'row'), may hold values from -0.0625 to 0.0625
- teacher_resid: bfloat16 [16384, 4096], P(('row', 'col')), may hold values from -6 to 6
- student_in: bfloat16 [16384, 1024], P(('row', 'col')), may hold values from -24 to 24
- norm_gain: bfloat16 [1024], replicated, may hold values from 0.099609375 to 1.8984375
- qkv_weight: bfloat16 [1024, 3072], replicated
- out_weight: bfloat16 [1024, 1024], replicated, may hold values from -0.1875 to 0.1875
- head_weight: bfloat16 [1024, 4096], replicated, may hold values from -0.1875 to 0.1875
- token_ids: int32 [16384], P(('row', 'col')), may hold values from 0 to 128255, as said below
- doc_ids: int32 [16384], P('row'), may hold values from 0 to 63, never falling along the last dimension, each value on 1 to 1024 neighbouring positions
Outputs:
- target: bfloat16 [16384, 4096], P(('row', 'col'))
- prediction: float32 [16384, 4096], P(('row', 'col'))
- head_grad: float32 [1024, 4096], P(('row', 'col'))
Inputs may be any that keep to these rules, and one draw needn't show every extreme that they name: `token_ids`: ids of 128000 and above are special tokens that the loss skips. `doc_ids`: document numbers never fall along the whole array; a document holds at most half of 2048 positions.
All inputs are finite; a program needn't handle non-finite values.
Results may differ from a plain program's by a relative error of at most 0.012.
The roundings to bfloat16 on the way count: a program that leaves them out, or rounds other values in their place, can miss the bound.
Values may be sent and summed in bfloat16 or wider, within the bound.
No kernel may reach another device: no remote copies, remote signals or barrier semaphores. Data moves between devices by JAX's collectives and lax.ppermute only.
A program may use at most 128 MiB of HBM per device.

v0:
```python
import math

import jax
import jax.numpy as jnp
from jax import lax
from jax.experimental import pallas as pl
from jax.experimental.pallas import tpu as pltpu
from jax.sharding import Mesh
from jax.sharding import PartitionSpec as P

HEADS = 16
HEAD_DIM = 64
SPECIAL = 128000

AXES = ("y", "xl", "z", "xh", "core")
SIZES = (4, 2, 4, 2, 2)
COL = ("z", "xh", "core")
CHUNKS = 2


def exchange(blocks, axes):
    return lax.all_to_all(blocks, axes, 0, 0, tiled=True)


def shift(array, axis, step):
    size = lax.axis_size(axis)
    return lax.ppermute(array, axis, [(i, (i + step) % size) for i in range(size)])


def flip(array, *axes):
    last = 2 ** len(axes) - 1
    return lax.ppermute(array, axes, [(i, last - i) for i in range(last + 1)])


def partial_kernel(slot_ref, *refs):
    heads, weights, outs = refs[:4], refs[4:12], refs[12:20]
    sorted_ref, total_ref = refs[20:]
    width = outs[0].shape[1]

    @pl.when(pl.program_id(0) == 0)
    def _():
        for step in range(4):
            for near in range(2):
                slot = slot_ref[step * 2 + near]
                lanes = pl.ds(pl.multiple_of((slot % 2) * width, width), width)
                for side in range(2):
                    for half in range(2):
                        sorted_ref[slot // 2, side, half, :, lanes] = weights[side * 4 + step][
                            near, half
                        ]

    def step(far, carry):
        total = None
        for side in range(2):
            for half in range(2):
                term = jnp.dot(
                    heads[half * 2 + side][...],
                    sorted_ref[far, side, half],
                    preferred_element_type=jnp.float32,
                ).astype(jnp.bfloat16)
                term = term.astype(jnp.float32)
                total = term if total is None else total + term
        total_ref[far] = total.astype(jnp.bfloat16)
        return carry

    lax.fori_loop(0, 4, step, 0)
    for far in range(4):
        for side in range(2):
            outs[far * 2 + side][...] = total_ref[far, :, side * width : (side + 1) * width]


def teacher_partials(slots, heads, own, other):
    tokens, depth = heads[0].shape
    width = own[0].shape[3]
    rows = 256
    weight_spec = pl.BlockSpec(own[0].shape, lambda i, _: (0, 0, 0, 0))
    return pl.pallas_call(
        partial_kernel,
        out_shape=[jax.ShapeDtypeStruct((tokens, width), jnp.bfloat16)] * 8,
        grid_spec=pltpu.PrefetchScalarGridSpec(
            num_scalar_prefetch=1,
            grid=(tokens // rows,),
            in_specs=[pl.BlockSpec((rows, depth), lambda i, _: (i, 0))] * 4 + [weight_spec] * 8,
            out_specs=[pl.BlockSpec((rows, width), lambda i, _: (i, 0))] * 8,
            scratch_shapes=[
                pltpu.VMEM((4, 2, 2, depth, 2 * width), jnp.bfloat16),
                pltpu.VMEM((4, rows, 2 * width), jnp.bfloat16),
            ],
        ),
        compiler_params=pltpu.CompilerParams(vmem_limit_bytes=48 * 1024 * 1024),
        name="teacher_partials",
    )(slots, *heads, *own, *other)


def pack_kernel(*refs):
    pieces, outs = refs[:4], refs[4:]
    width = outs[0].shape[3]
    for chunk, out_ref in enumerate(outs):
        for i in range(4):
            out_ref[i // 2, i % 2] = pieces[i][:, chunk * width : (chunk + 1) * width]


def pack(pieces):
    depth, wide = pieces[0].shape
    shape = (2, 2, depth, wide // CHUNKS)
    return pl.pallas_call(
        pack_kernel,
        out_shape=[jax.ShapeDtypeStruct(shape, pieces[0].dtype)] * CHUNKS,
        name="pack",
    )(*pieces)


def regroup_kernel(*refs):
    for i, out_ref in enumerate(refs[4:]):
        for far in range(4):
            out_ref[far] = refs[far][i // 2, i % 2]


def regroup(pieces):
    shape = (4, *pieces[0].shape[2:])
    return pl.pallas_call(
        regroup_kernel,
        out_shape=[jax.ShapeDtypeStruct(shape, pieces[0].dtype)] * 4,
        name="regroup",
    )(*pieces)


def gradient_kernel(place_ref, *refs):
    kept, parts = refs[:8], refs[8:16]
    weight_ref, resid_ref = refs[16:18]
    targets, product_ref = refs[18:22], refs[22]
    rows = resid_ref.shape[1]
    for far in range(4):
        for side in range(2):
            tokens = kept[far * 2 + side][...].reshape(2 * rows, -1)
            wanted = []
            for half in range(2):
                block = place_ref[(far * 2 + half) * 2 + side]
                start = pl.multiple_of((block // 2) * rows, rows)
                total = None
                for source in range(4):
                    term = parts[source * 2 + side][pl.ds(start, rows), :].astype(jnp.float32)
                    total = term if total is None else total + term
                target = (resid_ref[block].astype(jnp.float32) + total).astype(jnp.bfloat16)
                targets[far][half, side] = target
                wanted.append(target)
            predicted = jnp.dot(tokens, weight_ref[...], preferred_element_type=jnp.float32)
            error = (predicted - jnp.concatenate(wanted).astype(jnp.float32)).astype(jnp.bfloat16)
            term = lax.dot_general(
                tokens, error, (((0,), (0,)), ((), ())), preferred_element_type=jnp.float32
            )
            if far == 0 and side == 0:
                product_ref[...] = term
            else:
                product_ref[...] += term


def gradient_term(places, kept, parts, weight, resid, chunk):
    rows = resid.shape[1]
    width = weight.shape[1]
    piece = (2, 2, rows, width)
    *targets, product = pl.pallas_call(
        gradient_kernel,
        out_shape=(
            *[jax.ShapeDtypeStruct(piece, jnp.bfloat16)] * 4,
            jax.ShapeDtypeStruct(weight.shape, jnp.float32),
        ),
        grid_spec=pltpu.PrefetchScalarGridSpec(
            num_scalar_prefetch=1,
            grid=(1,),
            in_specs=[
                pl.BlockSpec(x.shape, lambda i, _, n=x.ndim: (0,) * n)
                for x in (*kept, *parts, weight)
            ]
            + [pl.BlockSpec((16, rows, width), lambda i, _: (0, 0, chunk))],
            out_specs=(
                *[pl.BlockSpec(piece, lambda i, _: (0, 0, 0, 0))] * 4,
                pl.BlockSpec(weight.shape, lambda i, _: (0, 0)),
            ),
        ),
        compiler_params=pltpu.CompilerParams(vmem_limit_bytes=48 * 1024 * 1024),
        name="gradient_term",
    )(places, *kept, *parts, weight, resid)
    return targets, product


def place_kernel(column_ref, *refs):
    out_ref = refs[-1]
    for i, ref in enumerate(refs[:-1]):
        for far in range(4):
            column = pl.multiple_of(column_ref[i * 4 + far], 128)
            out_ref[:, pl.ds(column, ref.shape[2])] = ref[far]


def place_columns(columns, pieces, out_width):
    rows = pieces[0].shape[1]
    return pl.pallas_call(
        place_kernel,
        out_shape=jax.ShapeDtypeStruct((rows, out_width), pieces[0].dtype),
        grid_spec=pltpu.PrefetchScalarGridSpec(
            num_scalar_prefetch=1,
            grid=(1,),
            in_specs=[pl.BlockSpec(x.shape, lambda i, _: (0, 0, 0)) for x in pieces],
            out_specs=pl.BlockSpec((rows, out_width), lambda i, _: (0, 0)),
        ),
        name="place_columns",
    )(columns, *pieces)


def sum_kernel(scale, *refs):
    out_ref = refs[-1]
    count, _, width = refs[0].shape
    groups = 16
    for chunk, ref in enumerate(refs[:-1]):
        for place in range(groups):
            z, xh, core = place // 4, place // 2 % 2, place % 2
            total = ref[place]
            for i in range(1, count // groups):
                total = total + ref[i * groups + place]
            column = ((z * 4 + core * 2 + xh) * (len(refs) - 1) + chunk) * width
            out_ref[:, column : column + width] = total * scale


def sum_rows(pieces, out_width, scale):
    rows = pieces[0].shape[1]
    return pl.pallas_call(
        lambda *refs: sum_kernel(scale, *refs),
        out_shape=jax.ShapeDtypeStruct((rows, out_width), jnp.float32),
        name="sum_rows",
    )(*pieces)


def neighbours(array):
    size = math.prod(lax.axis_size(axis) for axis in COL)
    up = [(i, (i + 1) % size) for i in range(size)]
    down = [(i, (i - 1) % size) for i in range(size)]
    return lax.ppermute(array, COL, up), lax.ppermute(array, COL, down)


def student_hidden(student_in, norm_gain, qkv_weight, out_weight, doc_ids):
    tok_rows, student_width = student_in.shape
    student_f = student_in.astype(jnp.float32)
    mean_sq = jnp.mean(student_f * student_f, axis=-1, keepdims=True)
    normed = (student_f * lax.rsqrt(mean_sq + 1e-05) * norm_gain.astype(jnp.float32)).astype(
        jnp.bfloat16
    )
    projected = jnp.dot(normed, qkv_weight, preferred_element_type=jnp.float32).astype(jnp.bfloat16)
    queries = projected[:, :student_width].reshape(tok_rows, HEADS, HEAD_DIM)
    keyvals = projected[:, student_width:]
    before, after = neighbours(keyvals)
    widened = jnp.concatenate([before, keyvals, after], axis=0)
    keys_all = widened[:, :student_width].reshape(3 * tok_rows, HEADS, HEAD_DIM)
    values_all = widened[:, student_width:].reshape(3 * tok_rows, HEADS, HEAD_DIM)
    first_pos = lax.axis_index(COL) * tok_rows
    query_pos = first_pos + jnp.arange(tok_rows, dtype=jnp.int32)
    key_pos = first_pos - tok_rows + jnp.arange(3 * tok_rows, dtype=jnp.int32)
    filler = jnp.full((tok_rows,), -1, jnp.int32)
    padded_docs = jnp.concatenate([filler, doc_ids, filler])
    query_docs = lax.dynamic_slice_in_dim(doc_ids, first_pos, tok_rows)
    key_docs = lax.dynamic_slice_in_dim(padded_docs, first_pos, 3 * tok_rows)
    allowed = (query_docs[:, None] == key_docs[None, :]) & (
        jnp.abs(query_pos[:, None] - key_pos[None, :]) <= tok_rows
    )
    scores = jnp.einsum("qhd,khd->hqk", queries, keys_all, preferred_element_type=jnp.float32) * (
        1.0 / math.sqrt(HEAD_DIM)
    )
    scores = jnp.where(allowed[None], scores, -jnp.inf)
    row_max = jnp.max(scores, axis=-1, keepdims=True)
    exp_scores = jnp.exp(scores - row_max)
    weights = (exp_scores / jnp.sum(exp_scores, axis=-1, keepdims=True)).astype(jnp.bfloat16)
    attended = jnp.einsum("hqk,khd->qhd", weights, values_all, preferred_element_type=jnp.float32)
    attended = attended.reshape(tok_rows, student_width).astype(jnp.bfloat16)
    return (student_f + jnp.dot(attended, out_weight, preferred_element_type=jnp.float32)).astype(
        jnp.bfloat16
    )


def body(
    context_heads,
    teacher_proj,
    teacher_resid,
    student_in,
    norm_gain,
    qkv_weight,
    out_weight,
    head_weight,
    token_ids,
    doc_ids,
):
    tok_rows, student_width = student_in.shape
    row_tokens, depth = context_heads.shape
    out_width = teacher_resid.shape[1]
    half_width = teacher_proj.shape[1] // 2
    width = half_width // CHUNKS
    y, xl, z, xh, core = (lax.axis_index(axis).astype(jnp.int32) for axis in AXES)

    keep = lax.dynamic_slice_in_dim(teacher_proj, xh * half_width, half_width, axis=1)
    give = lax.dynamic_slice_in_dim(teacher_proj, (1 - xh) * half_width, half_width, axis=1)
    across = (keep, flip(give, "xh"), flip(keep, "xl"), flip(give, "xl", "xh"))
    own, other = [], []
    for near in pack(across):
        along_y = [near] + [shift(near, "y", -step) for step in (1, 3, 2)]
        along_y = [along_y[i] for i in (0, 1, 3, 2)]
        own.append(along_y)
        other.append([flip(piece, "core") for piece in along_y])

    by_core = context_heads.reshape(row_tokens // (2 * tok_rows), 2, tok_rows, depth)
    here, there = (
        lax.dynamic_index_in_dim(by_core, i, 1, keepdims=False).reshape(row_tokens // 2, depth)
        for i in (core, 1 - core)
    )
    heads = (here, flip(there, "core"), flip(here, "xh"), flip(there, "xh", "core"))

    by_owner = teacher_resid.reshape(tok_rows, 4, 2, 2, half_width).transpose(1, 3, 2, 0, 4)
    resid_cols = exchange(by_owner.reshape(16, tok_rows, half_width), COL)

    hidden = student_hidden(student_in, norm_gain, qkv_weight, out_weight, doc_ids)
    prediction = jnp.dot(hidden, head_weight, preferred_element_type=jnp.float32)
    kept = jnp.where((token_ids < SPECIAL)[:, None], hidden, jnp.zeros_like(hidden))
    kept = jnp.stack([kept, flip(kept, "xh")])
    kept_all = []
    for far in range(4):
        piece = kept if far == 0 else shift(kept, "z", far)
        kept_all += [piece, flip(piece, "core")]

    steps = jnp.arange(4, dtype=jnp.int32)
    pair = jnp.arange(2, dtype=jnp.int32)
    slots = (
        ((y + steps - z) % 4)[:, None] * 2 + jnp.bitwise_xor(jnp.bitwise_xor(xl, core), pair)[None]
    ).reshape(8)
    places = (
        ((z - steps) % 4)[:, None, None] * 4
        + jnp.bitwise_xor(xh, pair)[None, :, None] * 2
        + jnp.bitwise_xor(core, pair)[None, None, :]
    ).reshape(16)
    block = z * 4 + core * 2 + xh
    sent = [teacher_partials(slots, heads, own[i], other[i]) for i in range(CHUNKS)]
    everyone = math.prod(SIZES)
    target_pieces, columns, grad_pieces = [], [], []
    for chunk in range(CHUNKS):
        parts = []
        for far in range(4):
            for side in range(2):
                part = sent[chunk][far * 2 + side]
                if far and side:
                    moves = [(i, (i // 2 + far) % 4 * 2 + 1 - i % 2) for i in range(8)]
                    part = lax.ppermute(part, ("z", "core"), moves)
                elif far:
                    part = shift(part, "z", far)
                elif side:
                    part = flip(part, "core")
                parts.append(part)
        weight = lax.dynamic_slice_in_dim(
            head_weight, block * half_width + chunk * width, width, axis=1
        )
        targets, product = gradient_term(places, kept_all, parts, weight, resid_cols, chunk)
        grad_pieces.append(
            exchange(product.reshape(everyone, student_width // everyone, width), AXES)
        )
        targets = [targets[0]] + [shift(targets[far], "z", -far) for far in (1, 2, 3)]
        grouped = regroup(targets)
        for i, piece in enumerate(grouped):
            axes = ("xh",) * (i // 2) + ("core",) * (i % 2)
            target_pieces.append(flip(piece, *axes) if axes else piece)
            source = ((z + steps) % 4) * 4 + (core ^ (i % 2)) * 2 + (xh ^ (i // 2))
            columns.append(source * half_width + chunk * width)
    target = place_columns(jnp.concatenate(columns), target_pieces, out_width)
    head_grad = sum_rows(grad_pieces, out_width, 1.0 / row_tokens)
    return (target, prediction, head_grad)


def solution(mesh):
    fine = Mesh(mesh.devices.reshape(SIZES), AXES)
    row, col, whole = (("y", "xl"), COL, AXES)
    return jax.shard_map(
        body,
        mesh=fine,
        in_specs=(
            P(row, col),
            P(col, row),
            P(whole, None),
            P(whole, None),
            P(),
            P(),
            P(),
            P(),
            P(whole),
            P(row),
        ),
        out_specs=(P(whole, None), P(whole, None), P(whole, None)),
        check_vma=False,
    )
```

profile of v0, /device:TPU:0, one launch (start us, length us, event | category | flops | bytes accessed | tf_op | source)
XLA Modules:
  0.0 295.4 jit_solution(8806452288102169187)
XLA Ops:
  2.6 4.0 %convolution_convert_fusion = bf16[128,3072]{1,0:T(8,128)(2,1)S(1)} fusion(bf16[1024,3072]{1,0:T(8,128)(2,1)} %param.15, bf16[128,1024]{1,0:T(8,128)(2,1)} %param.13, f32[1024]{0:T(1024)S(1)} %convert_element_type.28, f32[128]{0:T(128)S(1)} %add_rsqrt_fusion), kind=kOutput, calls=%fused_computation.1 | convolution fusion | flops 806223872 | bytes 7344640 | tf_op jit(solution)/shard_map/dot_general | solution.py:247
  6.6 6.1 %collective-permute-start.1 = (bf16[128,2048]{1,0:T(8,128)(2,1)S(1)}, bf16[128,2048]{1,0:T(8,128)(2,1)}, u32[]{:S(2)}, u32[]{:S(2)}) collective-permute-start(bf16[128,2048]{1,0:T(8,128)(2,1)S(1)} %slice.16), channel_id=1, source_target_pairs={{0,15},{1,0},{2,1},{3,2},{4,3},{5,4},{6,5},{7,6},{8,7},{9,8},{10,9... | collective-permute-start | bytes 1572872 | tf_op jit(solution)/shard_map/ppermute | solution.py:237
  14.6 3.3 %collective-permute-start.15 = (bf16[512,256]{1,0:T(8,128)(2,1)}, bf16[512,256]{1,0:T(8,128)(2,1)}, u32[]{:S(2)}, u32[]{:S(2)}) collective-permute-start(bf16[512,256]{1,0:T(8,128)(2,1)} %get-tuple-element.89), channel_id=1, source_target_pairs={{0,18},{2,16},{16,2},{18,0},{1,19},{3,17},{17,3},{19,1},{4,22},{6,... | collective-permute-start | bytes 786440 | tf_op jit(solution)/shard_map/ppermute | solution.py:32
  20.9 9.3 %collective-permute-done.13.refs_1_ = bf16[512,256]{1,0:T(8,128)(2,1)} collective-permute-done((bf16[512,256]{1,0:T(8,128)(2,1)}, bf16[512,256]{1,0:T(8,128)(2,1)}, u32[]{:S(2)}, u32[]{:S(2)}) %collective-permute-start.13) | collective-permute-done | bytes 262176 | tf_op jit(solution)/shard_map/ppermute | solution.py:32
  30.2 4.6 %collective-permute-done.14.refs_2_ = bf16[512,256]{1,0:T(8,128)(2,1)} collective-permute-done((bf16[512,256]{1,0:T(8,128)(2,1)}, bf16[512,256]{1,0:T(8,128)(2,1)}, u32[]{:S(2)}, u32[]{:S(2)}) %collective-permute-start.14) | collective-permute-done | bytes 262176 | tf_op jit(solution)/shard_map/ppermute | solution.py:32
  34.8 2.4 pack.1
  37.2 3.0 %collective-permute-start.16 = (bf16[2,2,512,128]{3,2,1,0:T(8,128)(2,1)}, bf16[2,2,512,128]{3,2,1,0:T(8,128)(2,1)}, u32[]{:S(2)}, u32[]{:S(2)}) collective-permute-start(bf16[2,2,512,128]{3,2,1,0:T(8,128)(2,1)} %get-tuple-element.39.refs_4_), channel_id=1, source_target_pairs={{0,96},{32,0},{64,32},{96,64},{1,97},{33,1},{65,33},{97,65},{2,98}... | collective-permute-start | bytes 1572872 | tf_op jit(solution)/shard_map/ppermute | solution.py:27
  44.2 2.3 copy.19
  47.6 4.0 %fusion.28 = (f32[16,128]{1,0:T(8,128)S(1)}, f32[16,128,384]{2,1,0:T(8,128)}) fusion(pred[128,384]{1,0:T(8,128)(4,1)S(1)} %fusion.16, bf16[128,16,64]{0,2,1:T(8,128)(2,1)S(1)} %bitcast.42, bf16[384,16,64]{0,2,1:T(8,128)(2,1)} %bitcast.41), kind=kOutput, calls=%fused_computation.73 | convolution fusion | flops 103809408 | bytes 4251648 | tf_op jit(solution)/shard_map/sub | solution.py:269
  51.6 2.8 fusion.6
  55.6 2.1 collective-permute-start.2
  59.5 6.3 %collective-permute-done.2 = bf16[128,1024]{1,0:T(8,128)(2,1)S(1)} collective-permute-done((bf16[128,1024]{1,0:T(8,128)(2,1)S(1)}, bf16[128,1024]{1,0:T(8,128)(2,1)S(1)}, u32[]{:S(2)}, u32[]{:S(2)}) %collective-permute-start.2) | collective-permute-done | bytes 262176 | tf_op jit(solution)/shard_map/ppermute | solution.py:32
  65.9 2.3 collective-permute-start.36
  69.8 2.2 collective-permute-start.11
  73.2 17.2 %collective-permute-done.36.refs_5_ = bf16[2,2,512,128]{3,2,1,0:T(8,128)(2,1)S(1)} collective-permute-done((bf16[2,2,512,128]{3,2,1,0:T(8,128)(2,1)S(1)}, bf16[2,2,512,128]{3,2,1,0:T(8,128)(2,1)S(1)}, u32[]{:S(2)}, u32[]{:S(2)}) %collective-permute-start.36) | collective-permute-done | bytes 524320 | tf_op jit(solution)/shard_map/ppermute | solution.py:27
  90.4 2.1 collective-permute-start.38
  92.5 8.8 %collective-permute-done.38.refs_7_ = bf16[2,2,512,128]{3,2,1,0:T(8,128)(2,1)} collective-permute-done((bf16[2,2,512,128]{3,2,1,0:T(8,128)(2,1)S(1)}, bf16[2,2,512,128]{3,2,1,0:T(8,128)(2,1)}, u32[]{:S(2)}, u32[]{:S(2)}) %collective-permute-start.38) | collective-permute-done | bytes 524320 | tf_op jit(solution)/shard_map/ppermute | solution.py:27
  103.6 15.3 %collective-permute-done.12.refs_3_ = bf16[1024,512]{1,0:T(8,128)(2,1)S(1)} collective-permute-done((bf16[1024,512]{1,0:T(8,128)(2,1)S(1)}, bf16[1024,512]{1,0:T(8,128)(2,1)S(1)}, u32[]{:S(2)}, u32[]{:S(2)}) %collective-permute-start.12) | collective-permute-done | bytes 1048608 | tf_op jit(solution)/shard_map/ppermute | solution.py:32
  119.2 2.9 collective-permute-start.6
  125.7 2.6 reshape.212
  128.4 2.6 copy.24
  130.9 6.1 %all-to-all-start = ((bf16[16,128,256]{2,1,0:T(8,128)(2,1)}), bf16[16,128,256]{2,1,0:T(8,128)(2,1)}, u32[]{:S(2)}, u32[]{:S(2)}) async-start(bf16[16,128,256]{2,1,0:T(8,128)(2,1)} %bitcast.35), calls=%async_computation | async-start | bytes 2097152 | tf_op jit(solution)/shard_map/all_to_all | solution.py:22
  140.4 11.0 %teacher_partials.2 = (bf16[1024,128]{1,0:T(8,128)(2,1)S(1)}, bf16[1024,128]{1,0:T(8,128)(2,1)S(1)}, bf16[1024,128]{1,0:T(8,128)(2,1)S(1)}, bf16[1024,128]{1,0:T...) custom-call(s32[8]{0:T(128)S(1)} %add.302.slot_ref, ...), custom_call_target="tpu_custom_call" | custom-call | tf_op jit(solution)/shard_map/teacher_partials/pallas_call | solution.py:77
  154.7 2.5 collective-permute-start.26
  160.5 2.8 collective-permute-done.24.refs_10_
  164.0 1.9 collective-permute-done.25.refs_11_
  168.0 7.4 %collective-permute-done.26.refs_12_ = bf16[1024,128]{1,0:T(8,128)(2,1)S(1)} collective-permute-done((bf16[1024,128]{1,0:T(8,128)(2,1)S(1)}, bf16[1024,128]{1,0:T(8,128)(2,1)S(1)}, u32[]{:S(2)}, u32[]{:S(2)}) %collective-permute-start.26) | collective-permute-done | bytes 262176 | tf_op jit(solution)/shard_map/ppermute | solution.py:27
  176.2 2.3 collective-permute-done.27.refs_13_
  180.4 11.7 %teacher_partials.3 = (bf16[1024,128]{1,0:T(8,128)(2,1)S(1)}, bf16[1024,128]{1,0:T(8,128)(2,1)}, bf16[1024,128]{1,0:T(8,128)(2,1)}, bf16[1024,128]{1,0:T(8,128)(...) custom-call(s32[8]{0:T(128)S(1)} %add.302.slot_ref, ...), custom_call_target="tpu_custom_call" | custom-call | tf_op jit(solution)/shard_map/teacher_partials/pallas_call | solution.py:77
  197.1 4.1 %collective-permute-start.46 = (bf16[1024,128]{1,0:T(8,128)(2,1)}, bf16[1024,128]{1,0:T(8,128)(2,1)}, u32[]{:S(2)}, u32[]{:S(2)}) collective-permute-start(bf16[1024,128]{1,0:T(8,128)(2,1)} %copy-done.37), channel_id=1, source_target_pairs={{0,8},{4,12},{8,0},{12,4},{1,9},{5,13},{9,1},{13,5},{2,10},{6,14},... | collective-permute-start | bytes 786440 | tf_op jit(solution)/shard_map/ppermute | solution.py:27
  209.2 4.9 %gradient_term.2 = (bf16[2,2,128,128]{3,2,1,0:T(8,128)(2,1)S(1)}, bf16[2,2,128,128]{3,2,1,0:T(8,128)(2,1)S(1)}, bf16[2,2,128,128]{3,2,1,0:T(8,128)(2,1)S(1)}, bf...) custom-call(s32[16]{0:T(128)S(1)} %add.284.place_ref, bf16[2,128,1024]{2,1,0:T(8,128)(2,1)S(1)} %pad_maximum_fusion.1.refs_0_, ...), custom_call_target="tpu_custom_call" | custom-call | tf_op jit(solution)/shard_map/gradient_term/pallas_call | solution.py:162
  216.8 9.0 %all-to-all-start.1 = ((f32[128,8,128]{2,1,0:T(8,128)}), f32[128,8,128]{2,1,0:T(8,128)}, u32[]{:S(2)}, u32[]{:S(2)}) async-start(f32[128,8,128]{2,1,0:T(8,128)} %bitcast.30), calls=%async_computation.1 | async-start | bytes 1048576 | tf_op jit(solution)/shard_map/all_to_all | solution.py:22
  225.8 2.8 collective-permute-start.48
  229.3 2.9 collective-permute-start.31
  232.2 7.5 %collective-permute-done.48.refs_14_ = bf16[1024,128]{1,0:T(8,128)(2,1)S(1)} collective-permute-done((bf16[1024,128]{1,0:T(8,128)(2,1)}, bf16[1024,128]{1,0:T(8,128)(2,1)S(1)}, u32[]{:S(2)}, u32[]{:S(2)}) %collective-permute-start.48) | collective-permute-done | bytes 262176 | tf_op jit(solution)/shard_map/ppermute | solution.py:27
  239.7 4.5 %collective-permute-done.49.refs_15_ = bf16[1024,128]{1,0:T(8,128)(2,1)S(1)} collective-permute-done((bf16[1024,128]{1,0:T(8,128)(2,1)}, bf16[1024,128]{1,0:T(8,128)(2,1)S(1)}, u32[]{:S(2)}, u32[]{:S(2)}) %collective-permute-start.49) | collective-permute-done | bytes 262176 | tf_op jit(solution)/shard_map/ppermute | solution.py:347
  246.9 5.5 %gradient_term.3 = (bf16[2,2,128,128]{3,2,1,0:T(8,128)(2,1)S(1)}, bf16[2,2,128,128]{3,2,1,0:T(8,128)(2,1)}, bf16[2,2,128,128]{3,2,1,0:T(8,128)(2,1)}, bf16[2,2,128,128]{3,2,1,0:T(8,128)(2,1)}, f32[1024,128]{1,0:T(8,128)S(1)}) custom-call(s32[16]{0:T(128)S(1)} %add.284.place_ref, bf16[2,128,1024]{2,1,0:T(8,128)(2,1)S(1)} %pad_maximum_fusion.1.refs_0_, ...), custom_call_target="tpu_custom_call" | custom-call | tf_op jit(solution)/shard_map/gradient_term/pallas_call | solution.py:162
  253.8 3.2 %collective-permute-start.50 = (bf16[2,2,128,128]{3,2,1,0:T(8,128)(2,1)}, bf16[2,2,128,128]{3,2,1,0:T(8,128)(2,1)S(1)}, u32[]{:S(2)}, u32[]{:S(2)}) collective-permute-start(bf16[2,2,128,128]{3,2,1,0:T(8,128)(2,1)} %get-tuple-element.66), channel_id=1, source_target_pairs={{0,12},{4,0},{8,4},{12,8},{1,13},{5,1},{9,5},{13,9},{2,14},{6,2},{... | collective-permute-start | bytes 393224 | tf_op jit(solution)/shard_map/ppermute | solution.py:27
  258.4 1.9 regroup.2
  261.0 2.7 collective-permute-start.34
  267.5 1.9 regroup.3
  269.5 2.3 collective-permute-start.54
  271.8 6.5 %all-to-all-start.2 = ((f32[128,8,128]{2,1,0:T(8,128)}), f32[128,8,128]{2,1,0:T(8,128)S(1)}, u32[]{:S(2)}, u32[]{:S(2)}) async-start(f32[128,8,128]{2,1,0:T(8,128)} %bitcast.31), calls=%async_computation.2 | async-start | bytes 1048576 | tf_op jit(solution)/shard_map/all_to_all | solution.py:22
  278.3 2.3 collective-permute-start.55
  280.5 6.2 %fusion.29 = f32[128,4096]{1,0:T(8,128)} fusion(bf16[128,1024]{1,0:T(8,128)(2,1)} %get-tuple-element.94, bf16[1024,4096]{1,0:T(8,128)(2,1)} %param.17), kind=kOutput, calls=%fused_computation.74 | convolution fusion | flops 1073741824 | bytes 10747904 | tf_op jit(solution)/shard_map/dot_general | solution.py:318
  286.8 2.1 collective-permute-done.55.refs_7_
  289.5 3.2 %place_columns.1 = bf16[128,4096]{1,0:T(8,128)(2,1)} custom-call(s32[32]{0:T(128)} %concatenate.9.column_ref, bf16[4,128,128]{2,1,0:T(8,128)(2,1)} %get-tuple-element.52.refs_0_, bf16[4,128,128]{2,1,0:T(8,128)(2,1)} %copy-done.50, bf16[4,128,128]{2,1,0:T(8,128)(2,1)} %copy-done.51, bf16[4,128,128]{2,1,0:T(8,128)(2,1)} %copy-done.52, ...), custom_call_target="tpu_custom_call" | custom-call | tf_op jit(solution)/shard_map/place_columns/pallas_call | solution.py:197
  293.5 1.9 sum_rows.1
  (240 shorter events, 67.2 us)
Async XLA Ops:
  6.6 35.2 %collective-permute-start.1 = (bf16[128,2048]{1,0:T(8,128)(2,1)S(1)}, bf16[128,2048]{1,0:T(8,128)(2,1)}, u32[]{:S(2)}, u32[]{:S(2)}) collective-permute-start(bf16[128,2048]{1,0:T(8,128)(2,1)S(1)} %slice.16), channel_id=1, source_target_pairs={{0,15},{1,0},{2,1},{3,2},{4,3},{5,4},{6,5},{7,6},{8,7},{9,8},{10,9... | collective-permute-start | bytes 1572872 | tf_op jit(solution)/shard_map/ppermute | solution.py:237
  12.7 29.1 %collective-permute-start = (bf16[128,2048]{1,0:T(8,128)(2,1)S(1)}, bf16[128,2048]{1,0:T(8,128)(2,1)}, u32[]{:S(2)}, u32[]{:S(2)}) collective-permute-start(bf16[128,2048]{1,0:T(8,128)(2,1)S(1)} %slice.16), channel_id=1, source_target_pairs={{0,1},{1,2},{2,3},{3,4},{4,5},{5,6},{6,7},{7,8},{8,9},{9,10},{10,1... | collective-permute-start | bytes 1572872 | tf_op jit(solution)/shard_map/ppermute | solution.py:237
  14.6 15.6 %collective-permute-start.13 = (bf16[512,256]{1,0:T(8,128)(2,1)}, bf16[512,256]{1,0:T(8,128)(2,1)}, u32[]{:S(2)}, u32[]{:S(2)}) collective-permute-start(bf16[512,256]{1,0:T(8,128)(2,1)} %get-tuple-element.89), channel_id=1, source_target_pairs={{0,2},{2,0},{1,3},{3,1},{4,6},{6,4},{5,7},{7,5},{8,10},{10,8},{9,1... | collective-permute-start | bytes 786440 | tf_op jit(solution)/shard_map/ppermute | solution.py:32
  14.6 20.3 %collective-permute-start.15 = (bf16[512,256]{1,0:T(8,128)(2,1)}, bf16[512,256]{1,0:T(8,128)(2,1)}, u32[]{:S(2)}, u32[]{:S(2)}) collective-permute-start(bf16[512,256]{1,0:T(8,128)(2,1)} %get-tuple-element.89), channel_id=1, source_target_pairs={{0,18},{2,16},{16,2},{18,0},{1,19},{3,17},{17,3},{19,1},{4,22},{6,... | collective-permute-start | bytes 786440 | tf_op jit(solution)/shard_map/ppermute | solution.py:32
  17.8 17.0 %collective-permute-start.14 = (bf16[512,256]{1,0:T(8,128)(2,1)}, bf16[512,256]{1,0:T(8,128)(2,1)}, u32[]{:S(2)}, u32[]{:S(2)}) collective-permute-start(bf16[512,256]{1,0:T(8,128)(2,1)} %get-tuple-element.90.refs_0_), channel_id=1, source_target_pairs={{0,16},{16,0},{1,17},{17,1},{2,18},{18,2},{3,19},{19,3},{4,20},{20... | collective-permute-start | bytes 786440 | tf_op jit(solution)/shard_map/ppermute | solution.py:32
  37.2 30.9 %collective-permute-start.16 = (bf16[2,2,512,128]{3,2,1,0:T(8,128)(2,1)}, bf16[2,2,512,128]{3,2,1,0:T(8,128)(2,1)}, u32[]{:S(2)}, u32[]{:S(2)}) collective-permute-start(bf16[2,2,512,128]{3,2,1,0:T(8,128)(2,1)} %get-tuple-element.39.refs_4_), channel_id=1, source_target_pairs={{0,96},{32,0},{64,32},{96,64},{1,97},{33,1},{65,33},{97,65},{2,98}... | collective-permute-start | bytes 1572872 | tf_op jit(solution)/shard_map/ppermute | solution.py:27
  40.2 29.6 %collective-permute-start.17 = (bf16[2,2,512,128]{3,2,1,0:T(8,128)(2,1)}, bf16[2,2,512,128]{3,2,1,0:T(8,128)(2,1)}, u32[]{:S(2)}, u32[]{:S(2)}) collective-permute-start(bf16[2,2,512,128]{3,2,1,0:T(8,128)(2,1)} %get-tuple-element.39.refs_4_), channel_id=1, source_target_pairs={{0,64},{32,96},{64,0},{96,32},{1,65},{33,97},{65,1},{97,33},{2,66}... | collective-permute-start | bytes 1572872 | tf_op jit(solution)/shard_map/ppermute | solution.py:27
  40.9 29.0 %collective-permute-start.18 = (bf16[2,2,512,128]{3,2,1,0:T(8,128)(2,1)}, bf16[2,2,512,128]{3,2,1,0:T(8,128)(2,1)}, u32[]{:S(2)}, u32[]{:S(2)}) collective-permute-start(bf16[2,2,512,128]{3,2,1,0:T(8,128)(2,1)} %get-tuple-element.39.refs_4_), channel_id=1, source_target_pairs={{0,32},{32,64},{64,96},{96,0},{1,33},{33,65},{65,97},{97,1},{2,34}... | collective-permute-start | bytes 1572872 | tf_op jit(solution)/shard_map/ppermute | solution.py:27
  41.8 30.2 %collective-permute-start.19 = (bf16[2,2,512,128]{3,2,1,0:T(8,128)(2,1)}, bf16[2,2,512,128]{3,2,1,0:T(8,128)(2,1)}, u32[]{:S(2)}, u32[]{:S(2)}) collective-permute-start(bf16[2,2,512,128]{3,2,1,0:T(8,128)(2,1)} %get-tuple-element.39.refs_4_), channel_id=1, source_target_pairs={{0,1},{1,0},{2,3},{3,2},{4,5},{5,4},{6,7},{7,6},{8,9},{9,8},{10,11... | collective-permute-start | bytes 1572872 | tf_op jit(solution)/shard_map/ppermute | solution.py:32
  65.9 24.5 %collective-permute-start.36 = (bf16[2,2,512,128]{3,2,1,0:T(8,128)(2,1)S(1)}, bf16[2,2,512,128]{3,2,1,0:T(8,128)(2,1)S(1)}, u32[]{:S(2)}, u32[]{:S(2)}) collective-permute-start(bf16[2,2,512,128]{3,2,1,0:T(8,128)(2,1)S(1)} %copy-done.2), channel_id=1, source_target_pairs={{0,96},{32,0},{64,32},{96,64},{1,97},{33,1},{65,33},{97,65},{2,98}... | collective-permute-start | bytes 1572872 | tf_op jit(solution)/shard_map/ppermute | solution.py:27
  68.1 24.3 %collective-permute-start.37 = (bf16[2,2,512,128]{3,2,1,0:T(8,128)(2,1)S(1)}, bf16[2,2,512,128]{3,2,1,0:T(8,128)(2,1)}, u32[]{:S(2)}, u32[]{:S(2)}) collective-permute-start(bf16[2,2,512,128]{3,2,1,0:T(8,128)(2,1)S(1)} %copy-done.2), channel_id=1, source_target_pairs={{0,64},{32,96},{64,0},{96,32},{1,65},{33,97},{65,1},{97,33},{2,66}... | collective-permute-start | bytes 1572872 | tf_op jit(solution)/shard_map/ppermute | solution.py:27
  69.8 33.2 %collective-permute-start.10 = (bf16[1024,512]{1,0:T(8,128)(2,1)S(1)}, bf16[1024,512]{1,0:T(8,128)(2,1)S(1)}, u32[]{:S(2)}, u32[]{:S(2)}) collective-permute-start(bf16[1024,512]{1,0:T(8,128)(2,1)S(1)} %bitcast.37), channel_id=1, source_target_pairs={{0,1},{1,0},{2,3},{3,2},{4,5},{5,4},{6,7},{7,6},{8,9},{9,8},{10,11... | collective-permute-start | bytes 3145736 | tf_op jit(solution)/shard_map/ppermute | solution.py:32
  69.8 33.4 %collective-permute-start.11 = (bf16[1024,512]{1,0:T(8,128)(2,1)S(1)}, bf16[1024,512]{1,0:T(8,128)(2,1)S(1)}, u32[]{:S(2)}, u32[]{:S(2)}) collective-permute-start(bf16[1024,512]{1,0:T(8,128)(2,1)S(1)} %bitcast.32), channel_id=1, source_target_pairs={{0,2},{2,0},{1,3},{3,1},{4,6},{6,4},{5,7},{7,5},{8,10},{10,8},{9,1... | collective-permute-start | bytes 3145736 | tf_op jit(solution)/shard_map/ppermute | solution.py:32
  72.1 46.8 %collective-permute-start.12 = (bf16[1024,512]{1,0:T(8,128)(2,1)S(1)}, bf16[1024,512]{1,0:T(8,128)(2,1)S(1)}, u32[]{:S(2)}, u32[]{:S(2)}) collective-permute-start(bf16[1024,512]{1,0:T(8,128)(2,1)S(1)} %bitcast.38), channel_id=1, source_target_pairs={{0,3},{1,2},{2,1},{3,0},{4,7},{5,6},{6,5},{7,4},{8,11},{9,10},{10,... | collective-permute-start | bytes 3145736 | tf_op jit(solution)/shard_map/ppermute | solution.py:32
  101.3 17.9 %collective-permute-start.3 = (bf16[2,128,1024]{2,1,0:T(8,128)(2,1)S(1)}, bf16[2,128,1024]{2,1,0:T(8,128)(2,1)S(1)}, u32[]{:S(2)}, u32[]{:S(2)}) collective-permute-start(bf16[2,128,1024]{2,1,0:T(8,128)(2,1)S(1)} %pad_maximum_fusion.1.refs_0_), channel_id=1, source_target_pairs={{0,1},{1,0},{2,3},{3,2},{4,5},{5,4},{6,7},{7,6},{8,9},{9,8},{10,11... | collective-permute-start | bytes 1572872 | tf_op jit(solution)/shard_map/ppermute | solution.py:32
  102.1 20.0 %collective-permute-start.4 = (bf16[2,128,1024]{2,1,0:T(8,128)(2,1)S(1)}, bf16[2,128,1024]{2,1,0:T(8,128)(2,1)S(1)}, u32[]{:S(2)}, u32[]{:S(2)}) collective-permute-start(bf16[2,128,1024]{2,1,0:T(8,128)(2,1)S(1)} %pad_maximum_fusion.1.refs_0_), channel_id=1, source_target_pairs={{0,4},{4,8},{8,12},{12,0},{1,5},{5,9},{9,13},{13,1},{2,6},{6,10},{... | collective-permute-start | bytes 1572872 | tf_op jit(solution)/shard_map/ppermute | solution.py:27
  103.0 19.8 %collective-permute-start.20 = (bf16[2,2,512,128]{3,2,1,0:T(8,128)(2,1)}, bf16[2,2,512,128]{3,2,1,0:T(8,128)(2,1)S(1)}, u32[]{:S(2)}, u32[]{:S(2)}) collective-permute-start(bf16[2,2,512,128]{3,2,1,0:T(8,128)(2,1)} %collective-permute-done.16.refs_5_), channel_id=1, source_target_pairs={{0,1},{1,0},{2,3},{3,2},{4,5},{5,4},{6,7},{7,6},{8,9},{9,8},{10,11... | collective-permute-start | bytes 1572872 | tf_op jit(solution)/shard_map/ppermute | solution.py:32
  103.3 20.3 %collective-permute-start.21 = (bf16[2,2,512,128]{3,2,1,0:T(8,128)(2,1)}, bf16[2,2,512,128]{3,2,1,0:T(8,128)(2,1)S(1)}, u32[]{:S(2)}, u32[]{:S(2)}) collective-permute-start(bf16[2,2,512,128]{3,2,1,0:T(8,128)(2,1)} %collective-permute-done.17.refs_6_), channel_id=1, source_target_pairs={{0,1},{1,0},{2,3},{3,2},{4,5},{5,4},{6,7},{7,6},{8,9},{9,8},{10,11... | collective-permute-start | bytes 1572872 | tf_op jit(solution)/shard_map/ppermute | solution.py:32
  119.2 32.2 %collective-permute-start.6 = (bf16[2,128,1024]{2,1,0:T(8,128)(2,1)S(1)}, bf16[2,128,1024]{2,1,0:T(8,128)(2,1)S(1)}, u32[]{:S(2)}, u32[]{:S(2)}) collective-permute-start(bf16[2,128,1024]{2,1,0:T(8,128)(2,1)S(1)} %pad_maximum_fusion.1.refs_0_), channel_id=1, source_target_pairs={{0,8},{4,12},{8,0},{12,4},{1,9},{5,13},{9,1},{13,5},{2,10},{6,14},... | collective-permute-start | bytes 1572872 | tf_op jit(solution)/shard_map/ppermute | solution.py:27
  122.1 30.8 %collective-permute-start.8 = (bf16[2,128,1024]{2,1,0:T(8,128)(2,1)S(1)}, bf16[2,128,1024]{2,1,0:T(8,128)(2,1)}, u32[]{:S(2)}, u32[]{:S(2)}) collective-permute-start(bf16[2,128,1024]{2,1,0:T(8,128)(2,1)S(1)} %pad_maximum_fusion.1.refs_0_), channel_id=1, source_target_pairs={{0,12},{4,0},{8,4},{12,8},{1,13},{5,1},{9,5},{13,9},{2,14},{6,2},{... | collective-permute-start | bytes 1572872 | tf_op jit(solution)/shard_map/ppermute | solution.py:27
  123.6 30.0 %collective-permute-start.40 = (bf16[2,2,512,128]{3,2,1,0:T(8,128)(2,1)S(1)}, bf16[2,2,512,128]{3,2,1,0:T(8,128)(2,1)}, u32[]{:S(2)}, u32[]{:S(2)}) collective-permute-start(bf16[2,2,512,128]{3,2,1,0:T(8,128)(2,1)S(1)} %collective-permute-done.36.refs_5_), channel_id=1, source_target_pairs={{0,1},{1,0},{2,3},{3,2},{4,5},{5,4},{6,7},{7,6},{8,9},{9,8},{10,11... | collective-permute-start | bytes 1572872 | tf_op jit(solution)/shard_map/ppermute | solution.py:32
  124.4 30.3 %collective-permute-start.41 = (bf16[2,2,512,128]{3,2,1,0:T(8,128)(2,1)}, bf16[2,2,512,128]{3,2,1,0:T(8,128)(2,1)}, u32[]{:S(2)}, u32[]{:S(2)}) collective-permute-start(bf16[2,2,512,128]{3,2,1,0:T(8,128)(2,1)} %collective-permute-done.37.refs_6_), channel_id=1, source_target_pairs={{0,1},{1,0},{2,3},{3,2},{4,5},{5,4},{6,7},{7,6},{8,9},{9,8},{10,11... | collective-permute-start | bytes 1572872 | tf_op jit(solution)/shard_map/ppermute | solution.py:32
  125.7 31.5 %collective-permute-start.42 = (bf16[2,2,512,128]{3,2,1,0:T(8,128)(2,1)}, bf16[2,2,512,128]{3,2,1,0:T(8,128)(2,1)}, u32[]{:S(2)}, u32[]{:S(2)}) collective-permute-start(bf16[2,2,512,128]{3,2,1,0:T(8,128)(2,1)} %collective-permute-done.38.refs_7_), channel_id=1, source_target_pairs={{0,1},{1,0},{2,3},{3,2},{4,5},{5,4},{6,7},{7,6},{8,9},{9,8},{10,11... | collective-permute-start | bytes 1572872 | tf_op jit(solution)/shard_map/ppermute | solution.py:32
  130.9 71.6 %all-to-all-start = ((bf16[16,128,256]{2,1,0:T(8,128)(2,1)}), bf16[16,128,256]{2,1,0:T(8,128)(2,1)}, u32[]{:S(2)}, u32[]{:S(2)}) async-start(bf16[16,128,256]{2,1,0:T(8,128)(2,1)} %bitcast.35), calls=%async_computation | async-start | bytes 2097152 | tf_op jit(solution)/shard_map/all_to_all | solution.py:22
  154.7 20.8 %collective-permute-start.26 = (bf16[1024,128]{1,0:T(8,128)(2,1)S(1)}, bf16[1024,128]{1,0:T(8,128)(2,1)S(1)}, u32[]{:S(2)}, u32[]{:S(2)}) collective-permute-start(bf16[1024,128]{1,0:T(8,128)(2,1)S(1)} %get-tuple-element.44), channel_id=1, source_target_pairs={{0,8},{4,12},{8,0},{12,4},{1,9},{5,13},{9,1},{13,5},{2,10},{6,14},... | collective-permute-start | bytes 786440 | tf_op jit(solution)/shard_map/ppermute | solution.py:27
  157.2 21.3 %collective-permute-start.27 = (bf16[1024,128]{1,0:T(8,128)(2,1)S(1)}, bf16[1024,128]{1,0:T(8,128)(2,1)S(1)}, u32[]{:S(2)}, u32[]{:S(2)}) collective-permute-start(bf16[1024,128]{1,0:T(8,128)(2,1)S(1)} %get-tuple-element.45), channel_id=1, source_target_pairs={{0,9},{1,8},{4,13},{5,12},{8,1},{9,0},{12,5},{13,4},{2,11},{3,10},... | collective-permute-start | bytes 786440 | tf_op jit(solution)/shard_map/ppermute | solution.py:347
  158.7 36.3 %collective-permute-start.28 = (bf16[1024,128]{1,0:T(8,128)(2,1)S(1)}, bf16[1024,128]{1,0:T(8,128)(2,1)S(1)}, u32[]{:S(2)}, u32[]{:S(2)}) collective-permute-start(bf16[1024,128]{1,0:T(8,128)(2,1)S(1)} %get-tuple-element.46), channel_id=1, source_target_pairs={{0,12},{4,0},{8,4},{12,8},{1,13},{5,1},{9,5},{13,9},{2,14},{6,2},{... | collective-permute-start | bytes 786440 | tf_op jit(solution)/shard_map/ppermute | solution.py:27
  164.0 31.8 %collective-permute-start.29 = (bf16[1024,128]{1,0:T(8,128)(2,1)S(1)}, bf16[1024,128]{1,0:T(8,128)(2,1)S(1)}, u32[]{:S(2)}, u32[]{:S(2)}) collective-permute-start(bf16[1024,128]{1,0:T(8,128)(2,1)S(1)} %get-tuple-element.47), channel_id=1, source_target_pairs={{0,13},{1,12},{4,1},{5,0},{8,5},{9,4},{12,9},{13,8},{2,15},{3,14},... | collective-permute-start | bytes 786440 | tf_op jit(solution)/shard_map/ppermute | solution.py:347
  166.6 30.0 %collective-permute-start.5 = (bf16[2,128,1024]{2,1,0:T(8,128)(2,1)S(1)}, bf16[2,128,1024]{2,1,0:T(8,128)(2,1)S(1)}, u32[]{:S(2)}, u32[]{:S(2)}) collective-permute-start(bf16[2,128,1024]{2,1,0:T(8,128)(2,1)S(1)} %collective-permute-done.4.refs_2_), channel_id=1, source_target_pairs={{0,1},{1,0},{2,3},{3,2},{4,5},{5,4},{6,7},{7,6},{8,9},{9,8},{10,11... | collective-permute-start | bytes 1572872 | tf_op jit(solution)/shard_map/ppermute | solution.py:32
  176.2 20.9 %collective-permute-start.7 = (bf16[2,128,1024]{2,1,0:T(8,128)(2,1)S(1)}, bf16[2,128,1024]{2,1,0:T(8,128)(2,1)}, u32[]{:S(2)}, u32[]{:S(2)}) collective-permute-start(bf16[2,128,1024]{2,1,0:T(8,128)(2,1)S(1)} %collective-permute-done.6.refs_4_), channel_id=1, source_target_pairs={{0,1},{1,0},{2,3},{3,2},{4,5},{5,4},{6,7},{7,6},{8,9},{9,8},{10,11... | collective-permute-start | bytes 1572872 | tf_op jit(solution)/shard_map/ppermute | solution.py:32
  179.2 22.0 %collective-permute-start.9 = (bf16[2,128,1024]{2,1,0:T(8,128)(2,1)}, bf16[2,128,1024]{2,1,0:T(8,128)(2,1)}, u32[]{:S(2)}, u32[]{:S(2)}) collective-permute-start(bf16[2,128,1024]{2,1,0:T(8,128)(2,1)} %collective-permute-done.8.refs_6_), channel_id=1, source_target_pairs={{0,1},{1,0},{2,3},{3,2},{4,5},{5,4},{6,7},{7,6},{8,9},{9,8},{10,11... | collective-permute-start | bytes 1572872 | tf_op jit(solution)/shard_map/ppermute | solution.py:32
  195.7 30.1 %collective-permute-start.43 = (bf16[1024,128]{1,0:T(8,128)(2,1)}, bf16[1024,128]{1,0:T(8,128)(2,1)}, u32[]{:S(2)}, u32[]{:S(2)}) collective-permute-start(bf16[1024,128]{1,0:T(8,128)(2,1)} %get-tuple-element.58), channel_id=1, source_target_pairs={{0,1},{1,0},{2,3},{3,2},{4,5},{5,4},{6,7},{7,6},{8,9},{9,8},{10,11... | collective-permute-start | bytes 786440 | tf_op jit(solution)/shard_map/ppermute | solution.py:32
  196.5 32.2 %collective-permute-start.44 = (bf16[1024,128]{1,0:T(8,128)(2,1)}, bf16[1024,128]{1,0:T(8,128)(2,1)}, u32[]{:S(2)}, u32[]{:S(2)}) collective-permute-start(bf16[1024,128]{1,0:T(8,128)(2,1)} %get-tuple-element.59), channel_id=1, source_target_pairs={{0,4},{4,8},{8,12},{12,0},{1,5},{5,9},{9,13},{13,1},{2,6},{6,10},{... | collective-permute-start | bytes 786440 | tf_op jit(solution)/shard_map/ppermute | solution.py:27
  196.6 32.1 %collective-permute-start.45 = (bf16[1024,128]{1,0:T(8,128)(2,1)}, bf16[1024,128]{1,0:T(8,128)(2,1)}, u32[]{:S(2)}, u32[]{:S(2)}) collective-permute-start(bf16[1024,128]{1,0:T(8,128)(2,1)} %copy-done.38), channel_id=1, source_target_pairs={{0,5},{1,4},{4,9},{5,8},{8,13},{9,12},{12,1},{13,0},{2,7},{3,6},{6... | collective-permute-start | bytes 786440 | tf_op jit(solution)/shard_map/ppermute | solution.py:347
  197.1 32.2 %collective-permute-start.46 = (bf16[1024,128]{1,0:T(8,128)(2,1)}, bf16[1024,128]{1,0:T(8,128)(2,1)}, u32[]{:S(2)}, u32[]{:S(2)}) collective-permute-start(bf16[1024,128]{1,0:T(8,128)(2,1)} %copy-done.37), channel_id=1, source_target_pairs={{0,8},{4,12},{8,0},{12,4},{1,9},{5,13},{9,1},{13,5},{2,10},{6,14},... | collective-permute-start | bytes 786440 | tf_op jit(solution)/shard_map/ppermute | solution.py:27
  201.2 31.0 %collective-permute-start.47 = (bf16[1024,128]{1,0:T(8,128)(2,1)}, bf16[1024,128]{1,0:T(8,128)(2,1)}, u32[]{:S(2)}, u32[]{:S(2)}) collective-permute-start(bf16[1024,128]{1,0:T(8,128)(2,1)} %copy-done.36), channel_id=1, source_target_pairs={{0,9},{1,8},{4,13},{5,12},{8,1},{9,0},{12,5},{13,4},{2,11},{3,10},... | collective-permute-start | bytes 786440 | tf_op jit(solution)/shard_map/ppermute | solution.py:347
  216.8 54.9 %all-to-all-start.1 = ((f32[128,8,128]{2,1,0:T(8,128)}), f32[128,8,128]{2,1,0:T(8,128)}, u32[]{:S(2)}, u32[]{:S(2)}) async-start(f32[128,8,128]{2,1,0:T(8,128)} %bitcast.30), calls=%async_computation.1 | async-start | bytes 1048576 | tf_op jit(solution)/shard_map/all_to_all | solution.py:22
  225.8 13.9 %collective-permute-start.48 = (bf16[1024,128]{1,0:T(8,128)(2,1)}, bf16[1024,128]{1,0:T(8,128)(2,1)S(1)}, u32[]{:S(2)}, u32[]{:S(2)}) collective-permute-start(bf16[1024,128]{1,0:T(8,128)(2,1)} %copy-done.35), channel_id=1, source_target_pairs={{0,12},{4,0},{8,4},{12,8},{1,13},{5,1},{9,5},{13,9},{2,14},{6,2},{... | collective-permute-start | bytes 786440 | tf_op jit(solution)/shard_map/ppermute | solution.py:27
  228.7 15.6 %collective-permute-start.49 = (bf16[1024,128]{1,0:T(8,128)(2,1)}, bf16[1024,128]{1,0:T(8,128)(2,1)S(1)}, u32[]{:S(2)}, u32[]{:S(2)}) collective-permute-start(bf16[1024,128]{1,0:T(8,128)(2,1)} %copy-done.34), channel_id=1, source_target_pairs={{0,13},{1,12},{4,1},{5,0},{8,5},{9,4},{12,9},{13,8},{2,15},{3,14},... | collective-permute-start | bytes 786440 | tf_op jit(solution)/shard_map/ppermute | solution.py:347
  228.7 28.7 %collective-permute-start.30 = (bf16[2,2,128,128]{3,2,1,0:T(8,128)(2,1)}, bf16[2,2,128,128]{3,2,1,0:T(8,128)(2,1)}, u32[]{:S(2)}, u32[]{:S(2)}) collective-permute-start(bf16[2,2,128,128]{3,2,1,0:T(8,128)(2,1)} %copy-done.40), channel_id=1, source_target_pairs={{0,12},{4,0},{8,4},{12,8},{1,13},{5,1},{9,5},{13,9},{2,14},{6,2},{... | collective-permute-start | bytes 393224 | tf_op jit(solution)/shard_map/ppermute | solution.py:27
  229.3 29.0 %collective-permute-start.31 = (bf16[2,2,128,128]{3,2,1,0:T(8,128)(2,1)}, bf16[2,2,128,128]{3,2,1,0:T(8,128)(2,1)}, u32[]{:S(2)}, u32[]{:S(2)}) collective-permute-start(bf16[2,2,128,128]{3,2,1,0:T(8,128)(2,1)} %copy-done.39), channel_id=1, source_target_pairs={{0,8},{4,12},{8,0},{12,4},{1,9},{5,13},{9,1},{13,5},{2,10},{6,14},... | collective-permute-start | bytes 393224 | tf_op jit(solution)/shard_map/ppermute | solution.py:27
  232.2 26.2 %collective-permute-start.32 = (bf16[2,2,128,128]{3,2,1,0:T(8,128)(2,1)S(1)}, bf16[2,2,128,128]{3,2,1,0:T(8,128)(2,1)}, u32[]{:S(2)}, u32[]{:S(2)}) collective-permute-start(bf16[2,2,128,128]{3,2,1,0:T(8,128)(2,1)S(1)} %get-tuple-element.51), channel_id=1, source_target_pairs={{0,4},{4,8},{8,12},{12,0},{1,5},{5,9},{9,13},{13,1},{2,6},{6,10},{... | collective-permute-start | bytes 393224 | tf_op jit(solution)/shard_map/ppermute | solution.py:27
  260.3 18.0 %collective-permute-start.33 = (bf16[4,128,128]{2,1,0:T(8,128)(2,1)}, bf16[4,128,128]{2,1,0:T(8,128)(2,1)S(1)}, u32[]{:S(2)}, u32[]{:S(2)}) collective-permute-start(bf16[4,128,128]{2,1,0:T(8,128)(2,1)} %get-tuple-element.53), channel_id=1, source_target_pairs={{0,1},{1,0},{2,3},{3,2},{4,5},{5,4},{6,7},{7,6},{8,9},{9,8},{10,11... | collective-permute-start | bytes 393224 | tf_op jit(solution)/shard_map/ppermute | solution.py:32
  261.0 25.7 %collective-permute-start.34 = (bf16[4,128,128]{2,1,0:T(8,128)(2,1)}, bf16[4,128,128]{2,1,0:T(8,128)(2,1)S(1)}, u32[]{:S(2)}, u32[]{:S(2)}) collective-permute-start(bf16[4,128,128]{2,1,0:T(8,128)(2,1)} %get-tuple-element.54), channel_id=1, source_target_pairs={{0,2},{2,0},{1,3},{3,1},{4,6},{6,4},{5,7},{7,5},{8,10},{10,8},{9,1... | collective-permute-start | bytes 393224 | tf_op jit(solution)/shard_map/ppermute | solution.py:32
  263.7 23.0 %collective-permute-start.35 = (bf16[4,128,128]{2,1,0:T(8,128)(2,1)}, bf16[4,128,128]{2,1,0:T(8,128)(2,1)S(1)}, u32[]{:S(2)}, u32[]{:S(2)}) collective-permute-start(bf16[4,128,128]{2,1,0:T(8,128)(2,1)} %get-tuple-element.55), channel_id=1, source_target_pairs={{0,3},{1,2},{2,1},{3,0},{4,7},{5,6},{6,5},{7,4},{8,11},{9,10},{10,... | collective-permute-start | bytes 393224 | tf_op jit(solution)/shard_map/ppermute | solution.py:32
  269.5 17.3 %collective-permute-start.53 = (bf16[4,128,128]{2,1,0:T(8,128)(2,1)}, bf16[4,128,128]{2,1,0:T(8,128)(2,1)S(1)}, u32[]{:S(2)}, u32[]{:S(2)}) collective-permute-start(bf16[4,128,128]{2,1,0:T(8,128)(2,1)} %get-tuple-element.70), channel_id=1, source_target_pairs={{0,1},{1,0},{2,3},{3,2},{4,5},{5,4},{6,7},{7,6},{8,9},{9,8},{10,11... | collective-permute-start | bytes 393224 | tf_op jit(solution)/shard_map/ppermute | solution.py:32
  269.5 17.3 %collective-permute-start.54 = (bf16[4,128,128]{2,1,0:T(8,128)(2,1)}, bf16[4,128,128]{2,1,0:T(8,128)(2,1)S(1)}, u32[]{:S(2)}, u32[]{:S(2)}) collective-permute-start(bf16[4,128,128]{2,1,0:T(8,128)(2,1)} %get-tuple-element.71), channel_id=1, source_target_pairs={{0,2},{2,0},{1,3},{3,1},{4,6},{6,4},{5,7},{7,5},{8,10},{10,8},{9,1... | collective-permute-start | bytes 393224 | tf_op jit(solution)/shard_map/ppermute | solution.py:32
  271.8 20.9 %all-to-all-start.2 = ((f32[128,8,128]{2,1,0:T(8,128)}), f32[128,8,128]{2,1,0:T(8,128)S(1)}, u32[]{:S(2)}, u32[]{:S(2)}) async-start(f32[128,8,128]{2,1,0:T(8,128)} %bitcast.31), calls=%async_computation.2 | async-start | bytes 1048576 | tf_op jit(solution)/shard_map/all_to_all | solution.py:22
  (72 other events, 513.8 us)
where the time goes:
time: 298 us; the launch traced here: 295 us
  waiting for transfers between devices  93.7 us (31%)
  starting transfers between devices  86.8 us (29%)
  local copies, waits for them, and re-layouts  47.5 us (16%)
  Pallas kernels  44.5 us (15%)
  matrix products  18.1 us (6%)
  other arithmetic  3.78 us (1%)
    ppermute x21, waiting for transfers between devices, shift(): lax.ppermute(array, axis, [(i, (i + step) % size) for i in range(size)])  47.2 us
    ppermute x27, waiting for transfers between devices, flip(): return lax.ppermute(array, axes, [(i, last - i) for i in range(last + 1)])  37.6 us
    ppermute x21, starting transfers between devices, shift(): lax.ppermute(array, axis, [(i, (i + step) % size) for i in range(size)])  35.2 us
    unnamed x122, local copies, waits for them, and re-layouts  29.7 us
    pallas_call x2, Pallas kernels, teacher_partials(): pl.pallas_call(partial_kernel, out_shape=[jax.ShapeDtypeStruct((tokens, w...  22.7 us
    all_to_all x3, starting transfers between devices, exchange(): return lax.all_to_all(blocks, axes, 0, 0, tiled=True)  21.6 us
    ppermute x27, starting transfers between devices, flip(): return lax.ppermute(array, axes, [(i, last - i) for i in range(last + 1)])  21.3 us
    pallas_call x2, Pallas kernels, gradient_term(): pl.pallas_call(gradient_kernel, out_shape=(*[jax.ShapeDtypeStruct(piece,...  10.4 us
  transfers between devices with their start and end apart: 59, of which 16 were waited for; matrix products, arithmetic and copies ran while one was open for 11% of the time, Pallas kernels for 14%

commit v1 on v0

v1 whole, which is shorter than its diff:
```python
import math

import jax
import jax.numpy as jnp
from jax import lax
from jax.experimental import pallas as pl
from jax.experimental.pallas import tpu as pltpu
from jax.sharding import Mesh
from jax.sharding import PartitionSpec as P

HEADS = 16
HEAD_DIM = 64
SPECIAL = 128000

AXES = ("y", "xl", "zh", "zl", "xh", "core")
SIZES = (4, 2, 2, 2, 2, 2)
COL = ("zh", "zl", "xh", "core")
Z = ("zh", "zl")
CHUNKS = 2


def exchange(blocks, axes):
    return lax.all_to_all(blocks, axes, 0, 0, tiled=True)


def shift(array, axes, step):
    size = math.prod(lax.axis_size(axis) for axis in axes)
    return lax.ppermute(array, axes, [(i, (i + step) % size) for i in range(size)])


def flip(array, *axes):
    last = 2 ** len(axes) - 1
    return lax.ppermute(array, axes, [(i, last - i) for i in range(last + 1)])


def partial_kernel(slot_ref, *refs):
    heads, weights, outs = refs[:4], refs[4:-10], refs[-10:-2]
    sorted_ref, total_ref = refs[-2:]
    if len(weights) == 6:
        weights = (*weights[:5], *[weights[5].at[i] for i in range(3)])
    width = outs[0].shape[1]

    @pl.when(pl.program_id(0) == 0)
    def _():
        for step in range(4):
            for near in range(2):
                slot = slot_ref[step * 2 + near]
                lanes = pl.ds(pl.multiple_of((slot % 2) * width, width), width)
                for side in range(2):
                    for half in range(2):
                        sorted_ref[slot // 2, side, half, :, lanes] = weights[side * 4 + step][
                            near, half
                        ]

    def step(far, carry):
        total = None
        for side in range(2):
            for half in range(2):
                term = jnp.dot(
                    heads[half * 2 + side][...],
                    sorted_ref[far, side, half],
                    preferred_element_type=jnp.float32,
                ).astype(jnp.bfloat16)
                term = term.astype(jnp.float32)
                total = term if total is None else total + term
        total_ref[far] = total.astype(jnp.bfloat16)
        return carry

    lax.fori_loop(0, 4, step, 0)
    for far in range(4):
        for side in range(2):
            outs[far * 2 + side][...] = total_ref[far, :, side * width : (side + 1) * width]


def teacher_partials(slots, heads, own, other, chunk):
    tokens, depth = heads[0].shape
    width = own[0].shape[3]
    rows = 512
    weight_spec = pl.BlockSpec(own[0].shape, lambda i, _: (0, 0, 0, 0))
    return pl.pallas_call(
        partial_kernel,
        out_shape=[jax.ShapeDtypeStruct((tokens, width), jnp.bfloat16)] * 8,
        grid_spec=pltpu.PrefetchScalarGridSpec(
            num_scalar_prefetch=1,
            grid=(tokens // rows,),
            in_specs=[pl.BlockSpec((rows, depth), lambda i, _: (i, 0))] * 4
            + [weight_spec] * 4
            + [pl.BlockSpec((None, *own[0].shape), lambda i, _: (chunk, 0, 0, 0, 0))]
            + [
                pl.BlockSpec(x.shape, lambda i, _, n=x.ndim: (0,) * n)
                for x in other[1:]
            ],
            out_specs=[pl.BlockSpec((rows, width), lambda i, _: (i, 0))] * 8,
            scratch_shapes=[
                pltpu.VMEM((4, 2, 2, depth, 2 * width), jnp.bfloat16),
                pltpu.VMEM((4, rows, 2 * width), jnp.bfloat16),
            ],
        ),
        compiler_params=pltpu.CompilerParams(vmem_limit_bytes=58 * 1024 * 1024),
        name="teacher_partials",
    )(slots, *heads, *own, *other)


def pack_kernel(*refs):
    pieces, whole_ref, outs = refs[:4], refs[4], refs[5:]
    width = outs[0].shape[3]
    for chunk, out_ref in enumerate(outs):
        for i in range(4):
            piece = pieces[i][:, chunk * width : (chunk + 1) * width]
            out_ref[i // 2, i % 2] = piece
            whole_ref[chunk, i // 2, i % 2] = piece


def pack(pieces):
    depth, wide = pieces[0].shape
    shape = (2, 2, depth, wide // CHUNKS)
    return pl.pallas_call(
        pack_kernel,
        out_shape=[
            jax.ShapeDtypeStruct((CHUNKS, *shape), pieces[0].dtype),
            *[jax.ShapeDtypeStruct(shape, pieces[0].dtype)] * CHUNKS,
        ],
        name="pack",
    )(*pieces)


def regroup_kernel(*refs):
    for i, out_ref in enumerate(refs[4:]):
        for far in range(4):
            out_ref[far] = refs[far][i // 2, i % 2]


def regroup(pieces):
    shape = (4, *pieces[0].shape[2:])
    return pl.pallas_call(
        regroup_kernel,
        out_shape=[jax.ShapeDtypeStruct(shape, pieces[0].dtype)] * 4,
        name="regroup",
    )(*pieces)


def gradient_kernel(place_ref, *refs):
    kept, parts = refs[:2], refs[2 : 2 + 8 * CHUNKS]
    weight_ref, resid_ref = refs[-8:-6]
    targets, product_ref, target_ref = refs[-6:-2], refs[-2], refs[-1]
    rows = resid_ref.shape[1]
    product_ref[...] = jnp.zeros_like(product_ref)

    def step(far, carry):
        for side in range(2):
            tokens = kept[side][far].reshape(2 * rows, -1)
            wanted = []
            for half in range(2):
                block = place_ref[(far * 2 + half) * 2 + side]
                start = pl.multiple_of((block // 2) * rows, rows)
                sums = []
                for chunk in range(CHUNKS):
                    total = None
                    for source in range(4):
                        part = parts[chunk * 8 + source * 2 + side]
                        term = part[pl.ds(start, rows), :].astype(jnp.float32)
                        total = term if total is None else total + term
                    sums.append(total)
                total = jnp.concatenate(sums, axis=1)
                target = (resid_ref[block].astype(jnp.float32) + total).astype(jnp.bfloat16)
                target_ref[far, half, side] = target
                wanted.append(target)
            predicted = jnp.dot(tokens, weight_ref[...], preferred_element_type=jnp.float32)
            error = (predicted - jnp.concatenate(wanted).astype(jnp.float32)).astype(jnp.bfloat16)
            product_ref[...] += lax.dot_general(
                tokens, error, (((0,), (0,)), ((), ())), preferred_element_type=jnp.float32
            )
        return carry

    lax.fori_loop(0, 4, step, 0)
    for far in range(4):
        targets[far][...] = target_ref[far]


def gradient_term(places, kept, parts, weight, resid):
    rows = resid.shape[1]
    width = weight.shape[1]
    piece = (2, 2, rows, width)
    *targets, product = pl.pallas_call(
        gradient_kernel,
        out_shape=(
            *[jax.ShapeDtypeStruct(piece, jnp.bfloat16)] * 4,
            jax.ShapeDtypeStruct(weight.shape, jnp.float32),
        ),
        grid_spec=pltpu.PrefetchScalarGridSpec(
            num_scalar_prefetch=1,
            grid=(1,),
            in_specs=[
                pl.BlockSpec(x.shape, lambda i, _, n=x.ndim: (0,) * n)
                for x in (*kept, *parts, weight, resid)
            ],
            out_specs=(
                *[pl.BlockSpec(piece, lambda i, _: (0, 0, 0, 0))] * 4,
                pl.BlockSpec(weight.shape, lambda i, _: (0, 0)),
            ),
            scratch_shapes=[pltpu.VMEM((4, *piece), jnp.bfloat16)],
        ),
        compiler_params=pltpu.CompilerParams(vmem_limit_bytes=58 * 1024 * 1024),
        name="gradient_term",
    )(places, *kept, *parts, weight, resid)
    return targets, product


def place_kernel(column_ref, *refs):
    out_ref = refs[-1]
    for i, ref in enumerate(refs[:-1]):
        for far in range(4):
            column = pl.multiple_of(column_ref[i * 4 + far], 128)
            out_ref[:, pl.ds(column, ref.shape[2])] = ref[far]


def place_columns(columns, pieces, out_width):
    rows = pieces[0].shape[1]
    return pl.pallas_call(
        place_kernel,
        out_shape=jax.ShapeDtypeStruct((rows, out_width), pieces[0].dtype),
        grid_spec=pltpu.PrefetchScalarGridSpec(
            num_scalar_prefetch=1,
            grid=(1,),
            in_specs=[pl.BlockSpec(x.shape, lambda i, _: (0, 0, 0)) for x in pieces],
            out_specs=pl.BlockSpec((rows, out_width), lambda i, _: (0, 0)),
        ),
        name="place_columns",
    )(columns, *pieces)


def sum_kernel(scale, *refs):
    out_ref = refs[-1]
    count, _, width = refs[0].shape
    groups = 16
    for chunk, ref in enumerate(refs[:-1]):
        for place in range(groups):
            zh, zl, owner = place // 8, place // 4 % 2, place % 4
            total = ref[place]
            for i in range(1, count // groups):
                total = total + ref[i * groups + place]
            column = ((zh * 8 + owner * 2 + zl) * (len(refs) - 1) + chunk) * width
            out_ref[:, column : column + width] = total * scale


def sum_rows(pieces, out_width, scale):
    rows = pieces[0].shape[1]
    return pl.pallas_call(
        lambda *refs: sum_kernel(scale, *refs),
        out_shape=jax.ShapeDtypeStruct((rows, out_width), jnp.float32),
        name="sum_rows",
    )(*pieces)


def neighbours(array):
    return shift(array, COL, 1), shift(array, COL, -1)


def normed_rows(rows, norm_gain):
    rows_f = rows.astype(jnp.float32)
    mean_sq = jnp.mean(rows_f * rows_f, axis=-1, keepdims=True)
    return (rows_f * lax.rsqrt(mean_sq + 1e-05) * norm_gain.astype(jnp.float32)).astype(
        jnp.bfloat16
    )


def student_hidden(widened_in, norm_gain, qkv_weight, out_weight, doc_ids):
    tok_rows, student_width = widened_in.shape[0] // 3, widened_in.shape[1]
    student_f = widened_in[tok_rows : 2 * tok_rows].astype(jnp.float32)
    normed = normed_rows(widened_in, norm_gain)
    widened = jnp.dot(
        normed, qkv_weight[:, student_width:], preferred_element_type=jnp.float32
    ).astype(jnp.bfloat16)
    queries = jnp.dot(
        normed[tok_rows : 2 * tok_rows],
        qkv_weight[:, :student_width],
        preferred_element_type=jnp.float32,
    ).astype(jnp.bfloat16)
    queries = queries.reshape(tok_rows, HEADS, HEAD_DIM)
    keys_all = widened[:, :student_width].reshape(3 * tok_rows, HEADS, HEAD_DIM)
    values_all = widened[:, student_width:].reshape(3 * tok_rows, HEADS, HEAD_DIM)
    first_pos = lax.axis_index(COL) * tok_rows
    query_pos = first_pos + jnp.arange(tok_rows, dtype=jnp.int32)
    key_pos = first_pos - tok_rows + jnp.arange(3 * tok_rows, dtype=jnp.int32)
    filler = jnp.full((tok_rows,), -1, jnp.int32)
    padded_docs = jnp.concatenate([filler, doc_ids, filler])
    query_docs = lax.dynamic_slice_in_dim(doc_ids, first_pos, tok_rows)
    key_docs = lax.dynamic_slice_in_dim(padded_docs, first_pos, 3 * tok_rows)
    allowed = (query_docs[:, None] == key_docs[None, :]) & (
        jnp.abs(query_pos[:, None] - key_pos[None, :]) <= tok_rows
    )
    scores = jnp.einsum("qhd,khd->hqk", queries, keys_all, preferred_element_type=jnp.float32) * (
        1.0 / math.sqrt(HEAD_DIM)
    )
    scores = jnp.where(allowed[None], scores, -jnp.inf)
    row_max = jnp.max(scores, axis=-1, keepdims=True)
    exp_scores = jnp.exp(scores - row_max)
    weights = (exp_scores / jnp.sum(exp_scores, axis=-1, keepdims=True)).astype(jnp.bfloat16)
    attended = jnp.einsum("hqk,khd->qhd", weights, values_all, preferred_element_type=jnp.float32)
    attended = attended.reshape(tok_rows, student_width).astype(jnp.bfloat16)
    return (student_f + jnp.dot(attended, out_weight, preferred_element_type=jnp.float32)).astype(
        jnp.bfloat16
    )


def body(
    context_heads,
    teacher_proj,
    teacher_resid,
    student_in,
    norm_gain,
    qkv_weight,
    out_weight,
    head_weight,
    token_ids,
    doc_ids,
):
    tok_rows, student_width = student_in.shape
    row_tokens, depth = context_heads.shape
    out_width = teacher_resid.shape[1]
    half_width = teacher_proj.shape[1] // 2
    y, xl, zh, zl, xh, core = (lax.axis_index(axis).astype(jnp.int32) for axis in AXES)
    z, owner = zh * 2 + zl, zh * 2 + xh

    keep = lax.dynamic_slice_in_dim(teacher_proj, zl * half_width, half_width, axis=1)
    give = lax.dynamic_slice_in_dim(teacher_proj, (1 - zl) * half_width, half_width, axis=1)
    across = (keep, flip(give, "zl"), flip(keep, "xl"), flip(give, "xl", "zl"))
    own, other = [], []
    whole, *nears = pack(across)
    whole = flip(whole, "core")
    for chunk, near in enumerate(nears):
        along_y = [near] + [shift(near, ("y",), -step) for step in (1, 3, 2)]
        along_y = [along_y[i] for i in (0, 1, 3, 2)]
        own.append(along_y)
        if chunk:
            stack = jnp.stack(along_y[1:])
            other.append((whole, flip(stack, "core")))
        else:
            other.append([whole] + [flip(piece, "core") for piece in along_y[1:]])

    by_core = context_heads.reshape(row_tokens // (2 * tok_rows), 2, tok_rows, depth)
    here, there = (
        lax.dynamic_index_in_dim(by_core, i, 1, keepdims=False).reshape(row_tokens // 2, depth)
        for i in (core, 1 - core)
    )
    heads = (here, flip(there, "core"), flip(here, "zl"), flip(there, "zl", "core"))

    by_owner = teacher_resid.reshape(tok_rows, 2, 2, 2, 2, half_width).transpose(1, 4, 2, 3, 0, 5)
    resid_cols = exchange(by_owner.reshape(16, tok_rows, half_width), COL)

    before, after = neighbours(student_in)
    widened_in = jnp.concatenate([before, student_in, after])
    hidden = student_hidden(widened_in, norm_gain, qkv_weight, out_weight, doc_ids)
    prediction = jnp.dot(hidden, head_weight, preferred_element_type=jnp.float32)
    kept = jnp.where((token_ids < SPECIAL)[:, None], hidden, jnp.zeros_like(hidden))
    kept = jnp.stack([kept, flip(kept, "xh")])
    from_z = [shift(kept, Z, far) for far in (1, 2, 3)]
    kept = jnp.stack([kept, *from_z])
    kept_all = (kept, flip(kept, "core"))

    steps = jnp.arange(4, dtype=jnp.int32)
    pair = jnp.arange(2, dtype=jnp.int32)
    slots = (
        jnp.bitwise_xor((y + steps) % 4, owner)[:, None] * 2
        + jnp.bitwise_xor(jnp.bitwise_xor(xl, core), pair)[None]
    ).reshape(8)
    places = (
        ((z - steps) % 4)[:, None, None] * 4
        + jnp.bitwise_xor(xh, pair)[None, :, None] * 2
        + jnp.bitwise_xor(core, pair)[None, None, :]
    ).reshape(16)
    block = (owner * 2 + core) * 2 + zl
    sent = []
    for chunk in range(CHUNKS):
        sent.append(teacher_partials(slots, heads, own[chunk], other[chunk], chunk))
    everyone = math.prod(SIZES)
    parts = []
    for chunk in range(CHUNKS):
        for far in range(4):
            for side in range(2):
                axes = ("zh",) * (far // 2) + ("xh",) * (far % 2) + ("core",) * side
                part = sent[chunk][far * 2 + side]
                parts.append(flip(part, *axes) if axes else part)
    weight = lax.dynamic_slice_in_dim(head_weight, block * half_width, half_width, axis=1)
    targets, product = gradient_term(places, kept_all, parts, weight, resid_cols)
    grad_pieces = exchange(product.reshape(everyone, student_width // everyone, half_width), AXES)
    head_grad = sum_rows([grad_pieces], out_width, 1.0 / row_tokens)
    targets = [targets[0]] + [shift(targets[far], Z, -far) for far in (1, 2, 3)]
    grouped = regroup(targets)
    target_pieces, columns = [], []
    for i, piece in enumerate(grouped):
        axes = ("xh",) * (i // 2) + ("core",) * (i % 2)
        target_pieces.append(flip(piece, *axes) if axes else piece)
        from_z = (z + steps) % 4
        source = from_z // 2 * 8 + (xh ^ (i // 2)) * 4 + (core ^ (i % 2)) * 2 + from_z % 2
        columns.append(source * half_width)
    target = place_columns(jnp.concatenate(columns), target_pieces, out_width)
    return (target, prediction, head_grad)


def solution(mesh):
    fine = Mesh(mesh.devices.reshape(SIZES), AXES)
    row, col, whole = (("y", "xl"), COL, AXES)
    return jax.shard_map(
        body,
        mesh=fine,
        in_specs=(
            P(row, col),
            P(col, row),
            P(whole, None),
            P(whole, None),
            P(),
            P(),
            P(),
            P(),
            P(whole),
            P(row),
        ),
        out_specs=(P(whole, None), P(whole, None), P(whole, None)),
        check_vma=False,
    )
```

time: 298 us -> 293 us (0.983)
  local copies, waits for them, and re-layouts: 47.5 us -> 16.4 us
  waiting for transfers between devices: 93.7 us -> 120 us
  other arithmetic: 3.78 us -> 8 us
  starting transfers between devices: 86.8 us -> 82.8 us
    unnamed x122 -> x62, local copies, waits for them, and re-layouts: 29.7 us -> 1.79 us
    ppermute x27 -> x30, starting transfers between devices: 21.3 us -> 43 us  [flip(): return lax.ppermute(array, axes, [(i, last - i) for i in range(last + 1)])]
    ppermute x27 -> x30, waiting for transfers between devices: 37.6 us -> 57.4 us  [flip(): return lax.ppermute(array, axes, [(i, last - i) for i in range(last + 1)])]
    ppermute x29 -> x14, starting transfers between devices: 43.9 us -> 27.1 us  [shift(): lax.ppermute(array, axes, [(i, (i + step) % size) for i in range(size)])]
    all_to_all x3 -> x2, starting transfers between devices: 21.6 us -> 12.6 us  [exchange(): return lax.all_to_all(blocks, axes, 0, 0, tiled=True)]
    ppermute x29 -> x14, waiting for transfers between devices: 56 us -> 62.5 us  [shift(): lax.ppermute(array, axes, [(i, (i + step) % size) for i in range(size)])]
    another operation x1 -> x3, other arithmetic: 0.05 us -> 4.37 us  [the longest x1 2.72 us: body(): stack = jnp.stack(along_y[1:])]
    reshape x2, local copies, waits for them, and re-layouts: 5.18 us -> 2.13 us  [body(): teacher_resid.reshape(tok_rows, 2, 2, 2, 2, half_width)]
  transfers between devices with their start and end apart: 59 -> 46, of which waited for: 16 -> 17; matrix products, arithmetic and copies ran while one was open for 11% -> 14% of each run, Pallas kernels for 14% -> 11%
where the time goes in v1:
time: 293 us; the launch traced here: 291 us
  waiting for transfers between devices  120 us (41%)
  starting transfers between devices  82.8 us (28%)
  Pallas kernels  43.1 us (15%)
  matrix products  20.1 us (7%)
  local copies, waits for them, and re-layouts  16.4 us (6%)
  other arithmetic  8 us (3%)
    ppermute x14, waiting for transfers between devices, shift(): lax.ppermute(array, axes, [(i, (i + step) % size) for i in range(size)])  62.5 us
    ppermute x30, waiting for transfers between devices, flip(): return lax.ppermute(array, axes, [(i, last - i) for i in range(last + 1)])  57.4 us
    ppermute x30, starting transfers between devices, flip(): return lax.ppermute(array, axes, [(i, last - i) for i in range(last + 1)])  43 us
    ppermute x14, starting transfers between devices, shift(): lax.ppermute(array, axes, [(i, (i + step) % size) for i in range(size)])  27.1 us
    pallas_call x2, Pallas kernels, teacher_partials(): pl.pallas_call(partial_kernel, out_shape=[jax.ShapeDtypeStruct((tokens, w...  23.1 us
    all_to_all x2, starting transfers between devices, exchange(): return lax.all_to_all(blocks, axes, 0, 0, tiled=True)  12.6 us
    pallas_call x1, Pallas kernels, gradient_term(): pl.pallas_call(gradient_kernel, out_shape=(*[jax.ShapeDtypeStruct(piece,...  10.2 us
    dot_general x1, matrix products, body(): jnp.dot(hidden, head_weight, preferred_element_type=jnp.float32)  6.11 us
  transfers between devices with their start and end apart: 46, of which 17 were waited for; matrix products, arithmetic and copies ran while one was open for 14% of the time, Pallas kernels for 11%

profile of v1, /device:TPU:0, one launch (start us, length us, event | category | flops | bytes accessed | tf_op | source)
XLA Modules:
  0.0 291.3 jit_solution(10993230685037956780)
XLA Ops:
  1.9 2.1 collective-permute-start.10
  5.1 5.4 %collective-permute-start.1 = (bf16[128,1024]{1,0:T(8,128)(2,1)}, bf16[128,1024]{1,0:T(8,128)(2,1)S(1)}, u32[]{:S(2)}, u32[]{:S(2)}) collective-permute-start(bf16[128,1024]{1,0:T(8,128)(2,1)} %param.13), channel_id=1, source_target_pairs={{0,15},{1,0},{2,1},{3,2},{4,3},{5,4},{6,5},{7,6},{8,7},{9,8},{10,9... | collective-permute-start | bytes 786440 | tf_op jit(solution)/shard_map/ppermute | solution.py:28
  14.0 4.0 %collective-permute-done.10.refs_1_ = bf16[512,256]{1,0:T(8,128)(2,1)} collective-permute-done((bf16[512,256]{1,0:T(8,128)(2,1)S(1)}, bf16[512,256]{1,0:T(8,128)(2,1)}, u32[]{:S(2)}, u32[]{:S(2)}) %collective-permute-start.10) | collective-permute-done | bytes 262176 | tf_op jit(solution)/shard_map/ppermute | solution.py:33
  18.0 5.0 %collective-permute-done.11.refs_2_ = bf16[512,256]{1,0:T(8,128)(2,1)} collective-permute-done((bf16[512,256]{1,0:T(8,128)(2,1)S(1)}, bf16[512,256]{1,0:T(8,128)(2,1)}, u32[]{:S(2)}, u32[]{:S(2)}) %collective-permute-start.11) | collective-permute-done | bytes 262176 | tf_op jit(solution)/shard_map/ppermute | solution.py:33
  23.0 2.8 pack.1
  25.8 3.0 %collective-permute-start.27 = (bf16[2,2,512,128]{3,2,1,0:T(8,128)(2,1)}, bf16[2,2,512,128]{3,2,1,0:T(8,128)(2,1)}, u32[]{:S(2)}, u32[]{:S(2)}) collective-permute-start(bf16[2,2,512,128]{3,2,1,0:T(8,128)(2,1)} %get-tuple-element.41.refs_4_), channel_id=1, source_target_pairs={{0,96},{32,0},{64,32},{96,64},{1,97},{33,1},{65,33},{97,65},{2,98}... | collective-permute-start | bytes 1572872 | tf_op jit(solution)/shard_map/ppermute | solution.py:28
  30.9 4.0 %fusion.3 = bf16[384,2048]{1,0:T(8,128)(2,1)S(1)} fusion(bf16[384,1024]{1,0:T(8,128)(2,1)S(1)} %fusion.11, bf16[1024,3072]{1,0:T(8,128)(2,1)} %param.15), kind=kOutput, calls=%fused_computation.6 | convolution fusion | flops 1611399168 | bytes 6553600 | tf_op jit(solution)/shard_map/dot_general | solution.py:271
  34.9 2.7 fusion.17
  38.6 2.3 copy.21
  43.2 4.0 %fusion.38 = (f32[16,128]{1,0:T(8,128)S(1)}, f32[16,128,384]{2,1,0:T(8,128)}) fusion(pred[128,384]{1,0:T(8,128)(4,1)S(1)} %fusion.24, bf16[128,16,64]{0,2,1:T(8,128)(2,1)S(1)} %bitcast.50, bf16[384,16,64]{0,2,1:T(8,128)(2,1)} %bitcast.45), kind=kOutput, calls=%fused_computation.82 | convolution fusion | flops 103809408 | bytes 4251648 | tf_op jit(solution)/shard_map/sub | solution.py:297
  47.2 2.8 fusion.16
  50.5 3.1 %collective-permute-start.2 = (bf16[128,1024]{1,0:T(8,128)(2,1)S(1)}, bf16[128,1024]{1,0:T(8,128)(2,1)S(1)}, u32[]{:S(2)}, u32[]{:S(2)}) collective-permute-start(bf16[128,1024]{1,0:T(8,128)(2,1)S(1)} %get-tuple-element.69), channel_id=1, source_target_pairs={{0,2},{2,0},{1,3},{3,1},{4,6},{6,4},{5,7},{7,5},{8,10},{10,8},{9,1... | collective-permute-start | bytes 786440 | tf_op jit(solution)/shard_map/ppermute | solution.py:33
  53.6 2.3 collective-permute-start.13
  55.8 2.6 collective-permute-done.2
  58.4 2.2 collective-permute-start.14
  61.7 3.8 %collective-permute-start.5 = (bf16[2,128,1024]{2,1,0:T(8,128)(2,1)S(1)}, bf16[2,128,1024]{2,1,0:T(8,128)(2,1)S(1)}, u32[]{:S(2)}, u32[]{:S(2)}) collective-permute-start(bf16[2,128,1024]{2,1,0:T(8,128)(2,1)S(1)} %get-tuple-element.66), channel_id=1, source_target_pairs={{0,12},{4,0},{8,4},{12,8},{1,13},{5,1},{9,5},{13,9},{2,14},{6,2},{... | collective-permute-start | bytes 1572872 | tf_op jit(solution)/shard_map/ppermute | solution.py:28
  67.3 9.0 %collective-permute-done.13.refs_5_ = bf16[2,2,512,128]{3,2,1,0:T(8,128)(2,1)} collective-permute-done((bf16[2,2,512,128]{3,2,1,0:T(8,128)(2,1)S(1)}, bf16[2,2,512,128]{3,2,1,0:T(8,128)(2,1)}, u32[]{:S(2)}, u32[]{:S(2)}) %collective-permute-start.13) | collective-permute-done | bytes 524320 | tf_op jit(solution)/shard_map/ppermute | solution.py:28
  77.7 3.6 %collective-permute-start.4 = (bf16[2,128,1024]{2,1,0:T(8,128)(2,1)S(1)}, bf16[2,128,1024]{2,1,0:T(8,128)(2,1)S(1)}, u32[]{:S(2)}, u32[]{:S(2)}) collective-permute-start(bf16[2,128,1024]{2,1,0:T(8,128)(2,1)S(1)} %get-tuple-element.66), channel_id=1, source_target_pairs={{0,8},{4,12},{8,0},{12,4},{1,9},{5,13},{9,1},{13,5},{2,10},{6,14},... | collective-permute-start | bytes 1572872 | tf_op jit(solution)/shard_map/ppermute | solution.py:28
  83.6 2.7 pad_maximum_fusion.1
  86.4 30.2 %collective-permute-done.4 = bf16[2,128,1024]{2,1,0:T(8,128)(2,1)S(1)} collective-permute-done((bf16[2,128,1024]{2,1,0:T(8,128)(2,1)S(1)}, bf16[2,128,1024]{2,1,0:T(8,128)(2,1)S(1)}, u32[]{:S(2)}, u32[]{:S(2)}) %collective-permute-start.4) | collective-permute-done | bytes 524320 | tf_op jit(solution)/shard_map/ppermute | solution.py:28
  118.8 10.4 %collective-permute-done.9.refs_3_ = bf16[1024,512]{1,0:T(8,128)(2,1)} collective-permute-done((bf16[1024,512]{1,0:T(8,128)(2,1)S(1)}, bf16[1024,512]{1,0:T(8,128)(2,1)}, u32[]{:S(2)}, u32[]{:S(2)}) %collective-permute-start.9) | collective-permute-done | bytes 1048608 | tf_op jit(solution)/shard_map/ppermute | solution.py:33
  132.2 11.5 %teacher_partials.2 = (bf16[1024,128]{1,0:T(8,128)(2,1)}, bf16[1024,128]{1,0:T(8,128)(2,1)}, bf16[1024,128]{1,0:T(8,128)(2,1)}, bf16[1024,128]{1,0:T(8,128)(2,1)...) custom-call(s32[8]{0:T(128)} %add.286.slot_ref, ...), custom_call_target="tpu_custom_call" | custom-call | tf_op jit(solution)/shard_map/teacher_partials/pallas_call | solution.py:80
  143.9 3.0 %collective-permute-start.21 = (bf16[1024,128]{1,0:T(8,128)(2,1)}, bf16[1024,128]{1,0:T(8,128)(2,1)S(1)}, u32[]{:S(2)}, u32[]{:S(2)}) collective-permute-start(bf16[1024,128]{1,0:T(8,128)(2,1)} %get-tuple-element.35), channel_id=1, source_target_pairs={{0,2},{2,0},{1,3},{3,1},{4,6},{6,4},{5,7},{7,5},{8,10},{10,8},{9,1... | collective-permute-start | bytes 786440 | tf_op jit(solution)/shard_map/ppermute | solution.py:33
  149.1 3.8 %all-to-all-start = ((bf16[16,128,256]{2,1,0:T(8,128)(2,1)}), bf16[16,128,256]{2,1,0:T(8,128)(2,1)S(1)}, u32[]{:S(2)}, u32[]{:S(2)}) async-start(bf16[16,128,256]{2,1,0:T(8,128)(2,1)} %bitcast.18), calls=%async_computation | async-start | bytes 2097152 | tf_op jit(solution)/shard_map/all_to_all | solution.py:23
  152.9 3.2 %collective-permute-start.22 = (bf16[1024,128]{1,0:T(8,128)(2,1)}, bf16[1024,128]{1,0:T(8,128)(2,1)S(1)}, u32[]{:S(2)}, u32[]{:S(2)}) collective-permute-start(bf16[1024,128]{1,0:T(8,128)(2,1)} %get-tuple-element.36), channel_id=1, source_target_pairs={{0,3},{1,2},{2,1},{3,0},{4,7},{5,6},{6,5},{7,4},{8,11},{9,10},{10,... | collective-permute-start | bytes 786440 | tf_op jit(solution)/shard_map/ppermute | solution.py:33
  156.1 3.0 %collective-permute-start.23 = (bf16[1024,128]{1,0:T(8,128)(2,1)}, bf16[1024,128]{1,0:T(8,128)(2,1)S(1)}, u32[]{:S(2)}, u32[]{:S(2)}) collective-permute-start(bf16[1024,128]{1,0:T(8,128)(2,1)} %get-tuple-element.37), channel_id=1, source_target_pairs={{0,8},{8,0},{1,9},{9,1},{2,10},{10,2},{3,11},{11,3},{4,12},{12,4},... | collective-permute-start | bytes 786440 | tf_op jit(solution)/shard_map/ppermute | solution.py:33
  159.4 3.0 %collective-permute-start.25 = (bf16[1024,128]{1,0:T(8,128)(2,1)S(1)}, bf16[1024,128]{1,0:T(8,128)(2,1)S(1)}, u32[]{:S(2)}, u32[]{:S(2)}) collective-permute-start(bf16[1024,128]{1,0:T(8,128)(2,1)S(1)} %copy-done.26), channel_id=1, source_target_pairs={{0,10},{2,8},{8,2},{10,0},{1,11},{3,9},{9,3},{11,1},{4,14},{6,12},... | collective-permute-start | bytes 786440 | tf_op jit(solution)/shard_map/ppermute | solution.py:33
  162.4 11.6 %teacher_partials.3 = (bf16[1024,128]{1,0:T(8,128)(2,1)}, bf16[1024,128]{1,0:T(8,128)(2,1)}, bf16[1024,128]{1,0:T(8,128)(2,1)}, bf16[1024,128]{1,0:T(8,128)(2,1)...) custom-call(s32[8]{0:T(128)} %add.286.slot_ref, ...), custom_call_target="tpu_custom_call" | custom-call | tf_op jit(solution)/shard_map/teacher_partials/pallas_call | solution.py:80
  174.0 3.6 %collective-permute-start.26 = (bf16[1024,128]{1,0:T(8,128)(2,1)}, bf16[1024,128]{1,0:T(8,128)(2,1)S(1)}, u32[]{:S(2)}, u32[]{:S(2)}) collective-permute-start(bf16[1024,128]{1,0:T(8,128)(2,1)} %get-tuple-element.40), channel_id=1, source_target_pairs={{0,11},{1,10},{2,9},{3,8},{8,3},{9,2},{10,1},{11,0},{4,15},{5,14},... | collective-permute-start | bytes 786440 | tf_op jit(solution)/shard_map/ppermute | solution.py:33
  177.7 13.0 %collective-permute-done.24.refs_7_ = bf16[1024,128]{1,0:T(8,128)(2,1)S(1)} collective-permute-done((bf16[1024,128]{1,0:T(8,128)(2,1)S(1)}, bf16[1024,128]{1,0:T(8,128)(2,1)S(1)}, u32[]{:S(2)}, u32[]{:S(2)}) %collective-permute-start.24) | collective-permute-done | bytes 262176 | tf_op jit(solution)/shard_map/ppermute | solution.py:33
  190.6 3.5 %collective-permute-start.32 = (bf16[1024,128]{1,0:T(8,128)(2,1)}, bf16[1024,128]{1,0:T(8,128)(2,1)S(1)}, u32[]{:S(2)}, u32[]{:S(2)}) collective-permute-start(bf16[1024,128]{1,0:T(8,128)(2,1)} %get-tuple-element.44), channel_id=1, source_target_pairs={{0,2},{2,0},{1,3},{3,1},{4,6},{6,4},{5,7},{7,5},{8,10},{10,8},{9,1... | collective-permute-start | bytes 786440 | tf_op jit(solution)/shard_map/ppermute | solution.py:33
  194.8 2.5 collective-permute-start.35
  197.3 4.2 %collective-permute-done.32.refs_12_ = bf16[1024,128]{1,0:T(8,128)(2,1)S(1)} collective-permute-done((bf16[1024,128]{1,0:T(8,128)(2,1)}, bf16[1024,128]{1,0:T(8,128)(2,1)S(1)}, u32[]{:S(2)}, u32[]{:S(2)}) %collective-permute-start.32) | collective-permute-done | bytes 262176 | tf_op jit(solution)/shard_map/ppermute | solution.py:33
  201.5 3.5 %collective-permute-start.36 = (bf16[1024,128]{1,0:T(8,128)(2,1)}, bf16[1024,128]{1,0:T(8,128)(2,1)}, u32[]{:S(2)}, u32[]{:S(2)}) collective-permute-start(bf16[1024,128]{1,0:T(8,128)(2,1)} %get-tuple-element.48), channel_id=1, source_target_pairs={{0,10},{2,8},{8,2},{10,0},{1,11},{3,9},{9,3},{11,1},{4,14},{6,12},... | collective-permute-start | bytes 786440 | tf_op jit(solution)/shard_map/ppermute | solution.py:33
  206.8 2.8 collective-permute-start.37
  210.2 1.9 constant_dynamic-slice_fusion.refs_18_
  212.1 8.4 %collective-permute-done.35.refs_15_ = bf16[1024,128]{1,0:T(8,128)(2,1)} collective-permute-done((bf16[1024,128]{1,0:T(8,128)(2,1)}, bf16[1024,128]{1,0:T(8,128)(2,1)}, u32[]{:S(2)}, u32[]{:S(2)}) %collective-permute-start.35) | collective-permute-done | bytes 262176 | tf_op jit(solution)/shard_map/ppermute | solution.py:33
  220.6 10.2 %gradient_term.1 = (bf16[2,2,128,256]{3,2,1,0:T(8,128)(2,1)}, bf16[2,2,128,256]{3,2,1,0:T(8,128)(2,1)}, bf16[2,2,128,256]{3,2,1,0:T(8,128)(2,1)}, bf16[2,2,128,256]{3,2,1,0:T(8,128)(2,1)}, f32[1024,256]{1,0:T(8,128)}) custom-call(s32[16]{0:T(128)} %add.266.place_ref, bf16[4,2,128,1024]{3,2,1,0:T(8,128)(2,1)} %pad_maximum_fusion.refs_0_, ...), custom_call_target="tpu_custom_call" | custom-call | tf_op jit(solution)/shard_map/gradient_term/pallas_call | solution.py:184
  230.9 8.8 %all-to-all-start.1 = ((f32[128,8,256]{2,1,0:T(8,128)}), f32[128,8,256]{2,1,0:T(8,128)S(1)}, u32[]{:S(2)}, u32[]{:S(2)}) async-start(f32[128,8,256]{2,1,0:T(8,128)} %bitcast.43), calls=%async_computation.1 | async-start | bytes 2097152 | tf_op jit(solution)/shard_map/all_to_all | solution.py:23
  239.7 2.9 collective-permute-start.38
  244.7 18.7 %collective-permute-done.38.refs_1_ = bf16[2,2,128,256]{3,2,1,0:T(8,128)(2,1)S(1)} collective-permute-done((bf16[2,2,128,256]{3,2,1,0:T(8,128)(2,1)S(1)}, bf16[2,2,128,256]{3,2,1,0:T(8,128)(2,1)S(1)}, u32[]{:S(2)}, u32[]{:S(2)}) %collective-permute-start.38) | collective-permute-done | bytes 262176 | tf_op jit(solution)/shard_map/ppermute | solution.py:28
  263.4 3.5 %collective-permute-done.40.refs_3_ = bf16[2,2,128,256]{3,2,1,0:T(8,128)(2,1)S(1)} collective-permute-done((bf16[2,2,128,256]{3,2,1,0:T(8,128)(2,1)S(1)}, bf16[2,2,128,256]{3,2,1,0:T(8,128)(2,1)S(1)}, u32[]{:S(2)}, u32[]{:S(2)}) %collective-permute-start.40) | collective-permute-done | bytes 262176 | tf_op jit(solution)/shard_map/ppermute | solution.py:28
  267.6 2.2 regroup.1
  269.8 2.7 collective-permute-start.42
  273.2 6.1 %fusion.39 = f32[128,4096]{1,0:T(8,128)} fusion(bf16[128,1024]{1,0:T(8,128)(2,1)S(1)} %get-tuple-element.70, bf16[1024,4096]{1,0:T(8,128)(2,1)} %param.17), kind=kOutput, calls=%fused_computation.83 | convolution fusion | flops 1073741824 | bytes 10747904 | tf_op jit(solution)/shard_map/dot_general | solution.py:354
  280.8 4.6 %collective-permute-done.43.refs_3_ = bf16[4,128,256]{2,1,0:T(8,128)(2,1)} collective-permute-done((bf16[4,128,256]{2,1,0:T(8,128)(2,1)}, bf16[4,128,256]{2,1,0:T(8,128)(2,1)}, u32[]{:S(2)}, u32[]{:S(2)}) %collective-permute-start.43) | collective-permute-done | bytes 262176 | tf_op jit(solution)/shard_map/ppermute | solution.py:33
  285.5 2.9 %place_columns.1 = bf16[128,4096]{1,0:T(8,128)(2,1)} custom-call(s32[16]{0:T(128)} %pad_add_fusion.column_ref, bf16[4,128,256]{2,1,0:T(8,128)(2,1)} %get-tuple-element.54.refs_0_, bf16[4,128,256]{2,1,0:T(8,128)(2,1)} %collective-permute-done.41.refs_1_, bf16[4,128,256]{2,1,0:T(8,128)(2,1)} %collective-permute-done.42.refs_2_, ...), custom_call_target="tpu_custom_call" | custom-call | tf_op jit(solution)/shard_map/place_columns/pallas_call | solution.py:219
  289.4 1.9 sum_rows.1
  (153 shorter events, 35.5 us)
Async XLA Ops:
  0.6 49.3 %copy-start = (bf16[1024,1024]{1,0:T(8,128)(2,1)S(1)}, bf16[1024,1024]{1,0:T(8,128)(2,1)}, u32[]{:S(2)}) copy-start(bf16[1024,1024]{1,0:T(8,128)(2,1)} %param.16) | copy-start | bytes 6291460
  1.9 16.1 %collective-permute-start.10 = (bf16[512,256]{1,0:T(8,128)(2,1)S(1)}, bf16[512,256]{1,0:T(8,128)(2,1)}, u32[]{:S(2)}, u32[]{:S(2)}) collective-permute-start(bf16[512,256]{1,0:T(8,128)(2,1)S(1)} %get-tuple-element.63), channel_id=1, source_target_pairs={{0,4},{4,0},{1,5},{5,1},{2,6},{6,2},{3,7},{7,3},{8,12},{12,8},{9,1... | collective-permute-start | bytes 786440 | tf_op jit(solution)/shard_map/ppermute | solution.py:33
  4.0 19.0 %collective-permute-start.12 = (bf16[512,256]{1,0:T(8,128)(2,1)S(1)}, bf16[512,256]{1,0:T(8,128)(2,1)}, u32[]{:S(2)}, u32[]{:S(2)}) collective-permute-start(bf16[512,256]{1,0:T(8,128)(2,1)S(1)} %get-tuple-element.63), channel_id=1, source_target_pairs={{0,20},{4,16},{16,4},{20,0},{1,21},{5,17},{17,5},{21,1},{2,22},{6,... | collective-permute-start | bytes 786440 | tf_op jit(solution)/shard_map/ppermute | solution.py:33
  5.1 25.3 %collective-permute-start = (bf16[128,1024]{1,0:T(8,128)(2,1)}, bf16[128,1024]{1,0:T(8,128)(2,1)S(1)}, u32[]{:S(2)}, u32[]{:S(2)}) collective-permute-start(bf16[128,1024]{1,0:T(8,128)(2,1)} %param.13), channel_id=1, source_target_pairs={{0,1},{1,2},{2,3},{3,4},{4,5},{5,6},{6,7},{7,8},{8,9},{9,10},{10,1... | collective-permute-start | bytes 786440 | tf_op jit(solution)/shard_map/ppermute | solution.py:28
  5.1 25.3 %collective-permute-start.1 = (bf16[128,1024]{1,0:T(8,128)(2,1)}, bf16[128,1024]{1,0:T(8,128)(2,1)S(1)}, u32[]{:S(2)}, u32[]{:S(2)}) collective-permute-start(bf16[128,1024]{1,0:T(8,128)(2,1)} %param.13), channel_id=1, source_target_pairs={{0,15},{1,0},{2,1},{3,2},{4,3},{5,4},{6,5},{7,6},{8,7},{9,8},{10,9... | collective-permute-start | bytes 786440 | tf_op jit(solution)/shard_map/ppermute | solution.py:28
  10.4 12.6 %collective-permute-start.11 = (bf16[512,256]{1,0:T(8,128)(2,1)S(1)}, bf16[512,256]{1,0:T(8,128)(2,1)}, u32[]{:S(2)}, u32[]{:S(2)}) collective-permute-start(bf16[512,256]{1,0:T(8,128)(2,1)S(1)} %get-tuple-element.64.refs_0_), channel_id=1, source_target_pairs={{0,16},{16,0},{1,17},{17,1},{2,18},{18,2},{3,19},{19,3},{4,20},{20... | collective-permute-start | bytes 786440 | tf_op jit(solution)/shard_map/ppermute | solution.py:33
  25.8 35.0 %collective-permute-start.27 = (bf16[2,2,512,128]{3,2,1,0:T(8,128)(2,1)}, bf16[2,2,512,128]{3,2,1,0:T(8,128)(2,1)}, u32[]{:S(2)}, u32[]{:S(2)}) collective-permute-start(bf16[2,2,512,128]{3,2,1,0:T(8,128)(2,1)} %get-tuple-element.41.refs_4_), channel_id=1, source_target_pairs={{0,96},{32,0},{64,32},{96,64},{1,97},{33,1},{65,33},{97,65},{2,98}... | collective-permute-start | bytes 1572872 | tf_op jit(solution)/shard_map/ppermute | solution.py:28
  28.8 32.9 %collective-permute-start.28 = (bf16[2,2,512,128]{3,2,1,0:T(8,128)(2,1)}, bf16[2,2,512,128]{3,2,1,0:T(8,128)(2,1)}, u32[]{:S(2)}, u32[]{:S(2)}) collective-permute-start(bf16[2,2,512,128]{3,2,1,0:T(8,128)(2,1)} %get-tuple-element.41.refs_4_), channel_id=1, source_target_pairs={{0,64},{32,96},{64,0},{96,32},{1,65},{33,97},{65,1},{97,33},{2,66}... | collective-permute-start | bytes 1572872 | tf_op jit(solution)/shard_map/ppermute | solution.py:28
  29.4 36.1 %collective-permute-start.29 = (bf16[2,2,512,128]{3,2,1,0:T(8,128)(2,1)}, bf16[2,2,512,128]{3,2,1,0:T(8,128)(2,1)}, u32[]{:S(2)}, u32[]{:S(2)}) collective-permute-start(bf16[2,2,512,128]{3,2,1,0:T(8,128)(2,1)} %get-tuple-element.41.refs_4_), channel_id=1, source_target_pairs={{0,32},{32,64},{64,96},{96,0},{1,33},{33,65},{65,97},{97,1},{2,34}... | collective-permute-start | bytes 1572872 | tf_op jit(solution)/shard_map/ppermute | solution.py:28
  50.5 8.0 %collective-permute-start.2 = (bf16[128,1024]{1,0:T(8,128)(2,1)S(1)}, bf16[128,1024]{1,0:T(8,128)(2,1)S(1)}, u32[]{:S(2)}, u32[]{:S(2)}) collective-permute-start(bf16[128,1024]{1,0:T(8,128)(2,1)S(1)} %get-tuple-element.69), channel_id=1, source_target_pairs={{0,2},{2,0},{1,3},{3,1},{4,6},{6,4},{5,7},{7,5},{8,10},{10,8},{9,1... | collective-permute-start | bytes 786440 | tf_op jit(solution)/shard_map/ppermute | solution.py:33
  53.6 22.8 %collective-permute-start.13 = (bf16[2,2,512,128]{3,2,1,0:T(8,128)(2,1)S(1)}, bf16[2,2,512,128]{3,2,1,0:T(8,128)(2,1)}, u32[]{:S(2)}, u32[]{:S(2)}) collective-permute-start(bf16[2,2,512,128]{3,2,1,0:T(8,128)(2,1)S(1)} %copy-done.11), channel_id=1, source_target_pairs={{0,96},{32,0},{64,32},{96,64},{1,97},{33,1},{65,33},{97,65},{2,98}... | collective-permute-start | bytes 1572872 | tf_op jit(solution)/shard_map/ppermute | solution.py:28
  58.4 19.3 %collective-permute-start.14 = (bf16[2,2,512,128]{3,2,1,0:T(8,128)(2,1)S(1)}, bf16[2,2,512,128]{3,2,1,0:T(8,128)(2,1)}, u32[]{:S(2)}, u32[]{:S(2)}) collective-permute-start(bf16[2,2,512,128]{3,2,1,0:T(8,128)(2,1)S(1)} %copy-done.11), channel_id=1, source_target_pairs={{0,64},{32,96},{64,0},{96,32},{1,65},{33,97},{65,1},{97,33},{2,66}... | collective-permute-start | bytes 1572872 | tf_op jit(solution)/shard_map/ppermute | solution.py:28
  60.7 21.7 %collective-permute-start.15 = (bf16[2,2,512,128]{3,2,1,0:T(8,128)(2,1)S(1)}, bf16[2,2,512,128]{3,2,1,0:T(8,128)(2,1)}, u32[]{:S(2)}, u32[]{:S(2)}) collective-permute-start(bf16[2,2,512,128]{3,2,1,0:T(8,128)(2,1)S(1)} %copy-done.11), channel_id=1, source_target_pairs={{0,32},{32,64},{64,96},{96,0},{1,33},{33,65},{65,97},{97,1},{2,34}... | collective-permute-start | bytes 1572872 | tf_op jit(solution)/shard_map/ppermute | solution.py:28
  61.7 20.7 %collective-permute-start.5 = (bf16[2,128,1024]{2,1,0:T(8,128)(2,1)S(1)}, bf16[2,128,1024]{2,1,0:T(8,128)(2,1)S(1)}, u32[]{:S(2)}, u32[]{:S(2)}) collective-permute-start(bf16[2,128,1024]{2,1,0:T(8,128)(2,1)S(1)} %get-tuple-element.66), channel_id=1, source_target_pairs={{0,12},{4,0},{8,4},{12,8},{1,13},{5,1},{9,5},{13,9},{2,14},{6,2},{... | collective-permute-start | bytes 1572872 | tf_op jit(solution)/shard_map/ppermute | solution.py:28
  65.5 18.1 %collective-permute-start.3 = (bf16[2,128,1024]{2,1,0:T(8,128)(2,1)S(1)}, bf16[2,128,1024]{2,1,0:T(8,128)(2,1)S(1)}, u32[]{:S(2)}, u32[]{:S(2)}) collective-permute-start(bf16[2,128,1024]{2,1,0:T(8,128)(2,1)S(1)} %get-tuple-element.66), channel_id=1, source_target_pairs={{0,4},{4,8},{8,12},{12,0},{1,5},{5,9},{9,13},{13,1},{2,6},{6,10},{... | collective-permute-start | bytes 1572872 | tf_op jit(solution)/shard_map/ppermute | solution.py:28
  67.3 50.8 %copy-start.2 = (bf16[8,1,128,512]{3,2,1,0:T(8,128)(2,1)}, bf16[8,1,128,512]{3,2,1,0:T(8,128)(2,1)S(1)}, u32[]{:S(2)}) copy-start(bf16[8,1,128,512]{3,2,1,0:T(8,128)(2,1)S(1)} %get-tuple-element.60) | copy-start | bytes 3145732
  76.3 41.8 %collective-permute-start.8 = (bf16[1024,512]{1,0:T(8,128)(2,1)S(1)}, bf16[1024,512]{1,0:T(8,128)(2,1)S(1)}, u32[]{:S(2)}, u32[]{:S(2)}) collective-permute-start(bf16[1024,512]{1,0:T(8,128)(2,1)S(1)} %bitcast.37), channel_id=1, source_target_pairs={{0,4},{4,0},{1,5},{5,1},{2,6},{6,2},{3,7},{7,3},{8,12},{12,8},{9,1... | collective-permute-start | bytes 3145736 | tf_op jit(solution)/shard_map/ppermute | solution.py:33
  77.7 38.8 %collective-permute-start.4 = (bf16[2,128,1024]{2,1,0:T(8,128)(2,1)S(1)}, bf16[2,128,1024]{2,1,0:T(8,128)(2,1)S(1)}, u32[]{:S(2)}, u32[]{:S(2)}) collective-permute-start(bf16[2,128,1024]{2,1,0:T(8,128)(2,1)S(1)} %get-tuple-element.66), channel_id=1, source_target_pairs={{0,8},{4,12},{8,0},{12,4},{1,9},{5,13},{9,1},{13,5},{2,10},{6,14},... | collective-permute-start | bytes 1572872 | tf_op jit(solution)/shard_map/ppermute | solution.py:28
  82.4 36.3 %collective-permute-start.7 = (bf16[1024,512]{1,0:T(8,128)(2,1)S(1)}, bf16[1024,512]{1,0:T(8,128)(2,1)S(1)}, u32[]{:S(2)}, u32[]{:S(2)}) collective-permute-start(bf16[1024,512]{1,0:T(8,128)(2,1)S(1)} %bitcast.41), channel_id=1, source_target_pairs={{0,1},{1,0},{2,3},{3,2},{4,5},{5,4},{6,7},{7,6},{8,9},{9,8},{10,11... | collective-permute-start | bytes 3145736 | tf_op jit(solution)/shard_map/ppermute | solution.py:33
  82.4 46.8 %collective-permute-start.9 = (bf16[1024,512]{1,0:T(8,128)(2,1)S(1)}, bf16[1024,512]{1,0:T(8,128)(2,1)}, u32[]{:S(2)}, u32[]{:S(2)}) collective-permute-start(bf16[1024,512]{1,0:T(8,128)(2,1)S(1)} %bitcast.42), channel_id=1, source_target_pairs={{0,5},{1,4},{4,1},{5,0},{2,7},{3,6},{6,3},{7,2},{8,13},{9,12},{12,... | collective-permute-start | bytes 3145736 | tf_op jit(solution)/shard_map/ppermute | solution.py:33
  83.6 45.6 %collective-permute-start.16 = (bf16[2,2,2,512,128]{4,3,2,1,0:T(8,128)(2,1)S(1)}, bf16[2,2,2,512,128]{4,3,2,1,0:T(8,128)(2,1)}, u32[]{:S(2)}, u32[]{:S(2)}) collective-permute-start(bf16[2,2,2,512,128]{4,3,2,1,0:T(8,128)(2,1)S(1)} %copy-done.25), channel_id=1, source_target_pairs={{0,1},{1,0},{2,3},{3,2},{4,5},{5,4},{6,7},{7,6},{8,9},{9,8},{10,11... | collective-permute-start | bytes 3145736 | tf_op jit(solution)/shard_map/ppermute | solution.py:33
  116.6 42.9 %collective-permute-start.30 = (bf16[3,2,2,512,128]{4,3,2,1,0:T(8,128)(2,1)}, bf16[3,2,2,512,128]{4,3,2,1,0:T(8,128)(2,1)}, u32[]{:S(2)}, u32[]{:S(2)}) collective-permute-start(bf16[3,2,2,512,128]{4,3,2,1,0:T(8,128)(2,1)} %pad_maximum_fusion.1), channel_id=1, source_target_pairs={{0,1},{1,0},{2,3},{3,2},{4,5},{5,4},{6,7},{7,6},{8,9},{9,8},{10,11... | collective-permute-start | bytes 4718600 | tf_op jit(solution)/shard_map/ppermute | solution.py:33
  118.1 102.4 %collective-permute-start.6 = (bf16[4,2,128,1024]{3,2,1,0:T(8,128)(2,1)}, bf16[4,2,128,1024]{3,2,1,0:T(8,128)(2,1)}, u32[]{:S(2)}, u32[]{:S(2)}) collective-permute-start(bf16[4,2,128,1024]{3,2,1,0:T(8,128)(2,1)} %pad_maximum_fusion.refs_0_), channel_id=1, source_target_pairs={{0,1},{1,0},{2,3},{3,2},{4,5},{5,4},{6,7},{7,6},{8,9},{9,8},{10,11... | collective-permute-start | bytes 6291464 | tf_op jit(solution)/shard_map/ppermute | solution.py:33
  118.7 11.7 %collective-permute-start.17 = (bf16[2,2,512,128]{3,2,1,0:T(8,128)(2,1)}, bf16[2,2,512,128]{3,2,1,0:T(8,128)(2,1)}, u32[]{:S(2)}, u32[]{:S(2)}) collective-permute-start(bf16[2,2,512,128]{3,2,1,0:T(8,128)(2,1)} %collective-permute-done.13.refs_5_), channel_id=1, source_target_pairs={{0,1},{1,0},{2,3},{3,2},{4,5},{5,4},{6,7},{7,6},{8,9},{9,8},{10,11... | collective-permute-start | bytes 1572872 | tf_op jit(solution)/shard_map/ppermute | solution.py:33
  129.2 2.3 collective-permute-start.18
  129.2 3.0 %collective-permute-start.19 = (bf16[2,2,512,128]{3,2,1,0:T(8,128)(2,1)}, bf16[2,2,512,128]{3,2,1,0:T(8,128)(2,1)}, u32[]{:S(2)}, u32[]{:S(2)}) collective-permute-start(bf16[2,2,512,128]{3,2,1,0:T(8,128)(2,1)} %collective-permute-done.15.refs_7_), channel_id=1, source_target_pairs={{0,1},{1,0},{2,3},{3,2},{4,5},{5,4},{6,7},{7,6},{8,9},{9,8},{10,11... | collective-permute-start | bytes 1572872 | tf_op jit(solution)/shard_map/ppermute | solution.py:33
  143.7 12.3 %collective-permute-start.20 = (bf16[1024,128]{1,0:T(8,128)(2,1)}, bf16[1024,128]{1,0:T(8,128)(2,1)S(1)}, u32[]{:S(2)}, u32[]{:S(2)}) collective-permute-start(bf16[1024,128]{1,0:T(8,128)(2,1)} %get-tuple-element.34), channel_id=1, source_target_pairs={{0,1},{1,0},{2,3},{3,2},{4,5},{5,4},{6,7},{7,6},{8,9},{9,8},{10,11... | collective-permute-start | bytes 786440 | tf_op jit(solution)/shard_map/ppermute | solution.py:33
  143.9 15.1 %collective-permute-start.21 = (bf16[1024,128]{1,0:T(8,128)(2,1)}, bf16[1024,128]{1,0:T(8,128)(2,1)S(1)}, u32[]{:S(2)}, u32[]{:S(2)}) collective-permute-start(bf16[1024,128]{1,0:T(8,128)(2,1)} %get-tuple-element.35), channel_id=1, source_target_pairs={{0,2},{2,0},{1,3},{3,1},{4,6},{6,4},{5,7},{7,5},{8,10},{10,8},{9,1... | collective-permute-start | bytes 786440 | tf_op jit(solution)/shard_map/ppermute | solution.py:33
  149.1 63.0 %all-to-all-start = ((bf16[16,128,256]{2,1,0:T(8,128)(2,1)}), bf16[16,128,256]{2,1,0:T(8,128)(2,1)S(1)}, u32[]{:S(2)}, u32[]{:S(2)}) async-start(bf16[16,128,256]{2,1,0:T(8,128)(2,1)} %bitcast.18), calls=%async_computation | async-start | bytes 2097152 | tf_op jit(solution)/shard_map/all_to_all | solution.py:23
  152.9 21.1 %collective-permute-start.22 = (bf16[1024,128]{1,0:T(8,128)(2,1)}, bf16[1024,128]{1,0:T(8,128)(2,1)S(1)}, u32[]{:S(2)}, u32[]{:S(2)}) collective-permute-start(bf16[1024,128]{1,0:T(8,128)(2,1)} %get-tuple-element.36), channel_id=1, source_target_pairs={{0,3},{1,2},{2,1},{3,0},{4,7},{5,6},{6,5},{7,4},{8,11},{9,10},{10,... | collective-permute-start | bytes 786440 | tf_op jit(solution)/shard_map/ppermute | solution.py:33
  156.1 21.6 %collective-permute-start.23 = (bf16[1024,128]{1,0:T(8,128)(2,1)}, bf16[1024,128]{1,0:T(8,128)(2,1)S(1)}, u32[]{:S(2)}, u32[]{:S(2)}) collective-permute-start(bf16[1024,128]{1,0:T(8,128)(2,1)} %get-tuple-element.37), channel_id=1, source_target_pairs={{0,8},{8,0},{1,9},{9,1},{2,10},{10,2},{3,11},{11,3},{4,12},{12,4},... | collective-permute-start | bytes 786440 | tf_op jit(solution)/shard_map/ppermute | solution.py:33
  159.0 31.6 %collective-permute-start.24 = (bf16[1024,128]{1,0:T(8,128)(2,1)S(1)}, bf16[1024,128]{1,0:T(8,128)(2,1)S(1)}, u32[]{:S(2)}, u32[]{:S(2)}) collective-permute-start(bf16[1024,128]{1,0:T(8,128)(2,1)S(1)} %copy-done.27), channel_id=1, source_target_pairs={{0,9},{1,8},{8,1},{9,0},{2,11},{3,10},{10,3},{11,2},{4,13},{5,12},... | collective-permute-start | bytes 786440 | tf_op jit(solution)/shard_map/ppermute | solution.py:33
  159.4 34.7 %collective-permute-start.25 = (bf16[1024,128]{1,0:T(8,128)(2,1)S(1)}, bf16[1024,128]{1,0:T(8,128)(2,1)S(1)}, u32[]{:S(2)}, u32[]{:S(2)}) collective-permute-start(bf16[1024,128]{1,0:T(8,128)(2,1)S(1)} %copy-done.26), channel_id=1, source_target_pairs={{0,10},{2,8},{8,2},{10,0},{1,11},{3,9},{9,3},{11,1},{4,14},{6,12},... | collective-permute-start | bytes 786440 | tf_op jit(solution)/shard_map/ppermute | solution.py:33
  174.0 20.2 %collective-permute-start.26 = (bf16[1024,128]{1,0:T(8,128)(2,1)}, bf16[1024,128]{1,0:T(8,128)(2,1)S(1)}, u32[]{:S(2)}, u32[]{:S(2)}) collective-permute-start(bf16[1024,128]{1,0:T(8,128)(2,1)} %get-tuple-element.40), channel_id=1, source_target_pairs={{0,11},{1,10},{2,9},{3,8},{8,3},{9,2},{10,1},{11,0},{4,15},{5,14},... | collective-permute-start | bytes 786440 | tf_op jit(solution)/shard_map/ppermute | solution.py:33
  177.7 17.2 %collective-permute-start.31 = (bf16[1024,128]{1,0:T(8,128)(2,1)}, bf16[1024,128]{1,0:T(8,128)(2,1)S(1)}, u32[]{:S(2)}, u32[]{:S(2)}) collective-permute-start(bf16[1024,128]{1,0:T(8,128)(2,1)} %get-tuple-element.43), channel_id=1, source_target_pairs={{0,1},{1,0},{2,3},{3,2},{4,5},{5,4},{6,7},{7,6},{8,9},{9,8},{10,11... | collective-permute-start | bytes 786440 | tf_op jit(solution)/shard_map/ppermute | solution.py:33
  190.6 10.9 %collective-permute-start.32 = (bf16[1024,128]{1,0:T(8,128)(2,1)}, bf16[1024,128]{1,0:T(8,128)(2,1)S(1)}, u32[]{:S(2)}, u32[]{:S(2)}) collective-permute-start(bf16[1024,128]{1,0:T(8,128)(2,1)} %get-tuple-element.44), channel_id=1, source_target_pairs={{0,2},{2,0},{1,3},{3,1},{4,6},{6,4},{5,7},{7,5},{8,10},{10,8},{9,1... | collective-permute-start | bytes 786440 | tf_op jit(solution)/shard_map/ppermute | solution.py:33
  194.1 12.6 %collective-permute-start.33 = (bf16[1024,128]{1,0:T(8,128)(2,1)}, bf16[1024,128]{1,0:T(8,128)(2,1)S(1)}, u32[]{:S(2)}, u32[]{:S(2)}) collective-permute-start(bf16[1024,128]{1,0:T(8,128)(2,1)} %get-tuple-element.45), channel_id=1, source_target_pairs={{0,3},{1,2},{2,1},{3,0},{4,7},{5,6},{6,5},{7,4},{8,11},{9,10},{10,... | collective-permute-start | bytes 786440 | tf_op jit(solution)/shard_map/ppermute | solution.py:33
  194.2 17.8 %collective-permute-start.34 = (bf16[1024,128]{1,0:T(8,128)(2,1)}, bf16[1024,128]{1,0:T(8,128)(2,1)}, u32[]{:S(2)}, u32[]{:S(2)}) collective-permute-start(bf16[1024,128]{1,0:T(8,128)(2,1)} %get-tuple-element.46), channel_id=1, source_target_pairs={{0,8},{8,0},{1,9},{9,1},{2,10},{10,2},{3,11},{11,3},{4,12},{12,4},... | collective-permute-start | bytes 786440 | tf_op jit(solution)/shard_map/ppermute | solution.py:33
  194.8 25.7 %collective-permute-start.35 = (bf16[1024,128]{1,0:T(8,128)(2,1)}, bf16[1024,128]{1,0:T(8,128)(2,1)}, u32[]{:S(2)}, u32[]{:S(2)}) collective-permute-start(bf16[1024,128]{1,0:T(8,128)(2,1)} %get-tuple-element.47), channel_id=1, source_target_pairs={{0,9},{1,8},{8,1},{9,0},{2,11},{3,10},{10,3},{11,2},{4,13},{5,12},... | collective-permute-start | bytes 786440 | tf_op jit(solution)/shard_map/ppermute | solution.py:33
  201.5 19.0 %collective-permute-start.36 = (bf16[1024,128]{1,0:T(8,128)(2,1)}, bf16[1024,128]{1,0:T(8,128)(2,1)}, u32[]{:S(2)}, u32[]{:S(2)}) collective-permute-start(bf16[1024,128]{1,0:T(8,128)(2,1)} %get-tuple-element.48), channel_id=1, source_target_pairs={{0,10},{2,8},{8,2},{10,0},{1,11},{3,9},{9,3},{11,1},{4,14},{6,12},... | collective-permute-start | bytes 786440 | tf_op jit(solution)/shard_map/ppermute | solution.py:33
  206.8 13.8 %collective-permute-start.37 = (bf16[1024,128]{1,0:T(8,128)(2,1)}, bf16[1024,128]{1,0:T(8,128)(2,1)}, u32[]{:S(2)}, u32[]{:S(2)}) collective-permute-start(bf16[1024,128]{1,0:T(8,128)(2,1)} %get-tuple-element.49), channel_id=1, source_target_pairs={{0,11},{1,10},{2,9},{3,8},{8,3},{9,2},{10,1},{11,0},{4,15},{5,14},... | collective-permute-start | bytes 786440 | tf_op jit(solution)/shard_map/ppermute | solution.py:33
  230.9 57.5 %all-to-all-start.1 = ((f32[128,8,256]{2,1,0:T(8,128)}), f32[128,8,256]{2,1,0:T(8,128)S(1)}, u32[]{:S(2)}, u32[]{:S(2)}) async-start(f32[128,8,256]{2,1,0:T(8,128)} %bitcast.43), calls=%async_computation.1 | async-start | bytes 2097152 | tf_op jit(solution)/shard_map/all_to_all | solution.py:23
  239.7 23.7 %collective-permute-start.38 = (bf16[2,2,128,256]{3,2,1,0:T(8,128)(2,1)S(1)}, bf16[2,2,128,256]{3,2,1,0:T(8,128)(2,1)S(1)}, u32[]{:S(2)}, u32[]{:S(2)}) collective-permute-start(bf16[2,2,128,256]{3,2,1,0:T(8,128)(2,1)S(1)} %copy-done.30), channel_id=1, source_target_pairs={{0,12},{4,0},{8,4},{12,8},{1,13},{5,1},{9,5},{13,9},{2,14},{6,2},{... | collective-permute-start | bytes 786440 | tf_op jit(solution)/shard_map/ppermute | solution.py:28
  242.6 20.8 %collective-permute-start.39 = (bf16[2,2,128,256]{3,2,1,0:T(8,128)(2,1)S(1)}, bf16[2,2,128,256]{3,2,1,0:T(8,128)(2,1)S(1)}, u32[]{:S(2)}, u32[]{:S(2)}) collective-permute-start(bf16[2,2,128,256]{3,2,1,0:T(8,128)(2,1)S(1)} %copy-done.29), channel_id=1, source_target_pairs={{0,8},{4,12},{8,0},{12,4},{1,9},{5,13},{9,1},{13,5},{2,10},{6,14},... | collective-permute-start | bytes 786440 | tf_op jit(solution)/shard_map/ppermute | solution.py:28
  242.9 24.0 %collective-permute-start.40 = (bf16[2,2,128,256]{3,2,1,0:T(8,128)(2,1)S(1)}, bf16[2,2,128,256]{3,2,1,0:T(8,128)(2,1)S(1)}, u32[]{:S(2)}, u32[]{:S(2)}) collective-permute-start(bf16[2,2,128,256]{3,2,1,0:T(8,128)(2,1)S(1)} %copy-done.28), channel_id=1, source_target_pairs={{0,4},{4,8},{8,12},{12,0},{1,5},{5,9},{9,13},{13,1},{2,6},{6,10},{... | collective-permute-start | bytes 786440 | tf_op jit(solution)/shard_map/ppermute | solution.py:28
  269.8 9.5 %collective-permute-start.41 = (bf16[4,128,256]{2,1,0:T(8,128)(2,1)}, bf16[4,128,256]{2,1,0:T(8,128)(2,1)}, u32[]{:S(2)}, u32[]{:S(2)}) collective-permute-start(bf16[4,128,256]{2,1,0:T(8,128)(2,1)} %get-tuple-element.55), channel_id=1, source_target_pairs={{0,1},{1,0},{2,3},{3,2},{4,5},{5,4},{6,7},{7,6},{8,9},{9,8},{10,11... | collective-permute-start | bytes 786440 | tf_op jit(solution)/shard_map/ppermute | solution.py:33
  269.8 11.0 %collective-permute-start.42 = (bf16[4,128,256]{2,1,0:T(8,128)(2,1)}, bf16[4,128,256]{2,1,0:T(8,128)(2,1)}, u32[]{:S(2)}, u32[]{:S(2)}) collective-permute-start(bf16[4,128,256]{2,1,0:T(8,128)(2,1)} %get-tuple-element.56), channel_id=1, source_target_pairs={{0,2},{2,0},{1,3},{3,1},{4,6},{6,4},{5,7},{7,5},{8,10},{10,8},{9,1... | collective-permute-start | bytes 786440 | tf_op jit(solution)/shard_map/ppermute | solution.py:33
  272.6 12.9 %collective-permute-start.43 = (bf16[4,128,256]{2,1,0:T(8,128)(2,1)}, bf16[4,128,256]{2,1,0:T(8,128)(2,1)}, u32[]{:S(2)}, u32[]{:S(2)}) collective-permute-start(bf16[4,128,256]{2,1,0:T(8,128)(2,1)} %get-tuple-element.57), channel_id=1, source_target_pairs={{0,3},{1,2},{2,1},{3,0},{4,7},{5,6},{6,5},{7,4},{8,11},{9,10},{10,... | collective-permute-start | bytes 786440 | tf_op jit(solution)/shard_map/ppermute | solution.py:33
  (29 other events, 475.3 us)

commit v2 on v1

--- a/solution.py
+++ b/solution.py
@@ -8,7 +8,6 @@
 from jax.sharding import Mesh
 from jax.sharding import PartitionSpec as P
 
-HEADS = 16
 HEAD_DIM = 64
 SPECIAL = 128000
 
@@ -34,11 +33,9 @@
 
 
 def partial_kernel(slot_ref, *refs):
-    heads, weights, outs = refs[:4], refs[4:-10], refs[-10:-2]
-    sorted_ref, total_ref = refs[-2:]
-    if len(weights) == 6:
-        weights = (*weights[:5], *[weights[5].at[i] for i in range(3)])
-    width = outs[0].shape[1]
+    heads, weights, outs = refs[:4], refs[4:12], refs[12:16]
+    sorted_ref, total_ref = refs[16:]
+    width = outs[0].shape[1] // 2
 
     @pl.when(pl.program_id(0) == 0)
     def _():
@@ -68,8 +65,7 @@
 
     lax.fori_loop(0, 4, step, 0)
     for far in range(4):
-        for side in range(2):
-            outs[far * 2 + side][...] = total_ref[far, :, side * width : (side + 1) * width]
+        outs[far][...] = total_ref[far]
 
 
 def teacher_partials(slots, heads, own, other, chunk):
@@ -79,7 +75,7 @@
     weight_spec = pl.BlockSpec(own[0].shape, lambda i, _: (0, 0, 0, 0))
     return pl.pallas_call(
         partial_kernel,
-        out_shape=[jax.ShapeDtypeStruct((tokens, width), jnp.bfloat16)] * 8,
+        out_shape=[jax.ShapeDtypeStruct((tokens, 2 * width), jnp.bfloat16)] * 4,
         grid_spec=pltpu.PrefetchScalarGridSpec(
             num_scalar_prefetch=1,
             grid=(tokens // rows,),
@@ -90,7 +86,7 @@
                 pl.BlockSpec(x.shape, lambda i, _, n=x.ndim: (0,) * n)
                 for x in other[1:]
             ],
-            out_specs=[pl.BlockSpec((rows, width), lambda i, _: (i, 0))] * 8,
+            out_specs=[pl.BlockSpec((rows, 2 * width), lambda i, _: (i, 0))] * 4,
             scratch_shapes=[
                 pltpu.VMEM((4, 2, 2, depth, 2 * width), jnp.bfloat16),
                 pltpu.VMEM((4, rows, 2 * width), jnp.bfloat16),
@@ -125,93 +121,108 @@
 
 
 def regroup_kernel(*refs):
-    for i, out_ref in enumerate(refs[4:]):
+    for half, out_ref in enumerate(refs[4:]):
         for far in range(4):
-            out_ref[far] = refs[far][i // 2, i % 2]
+            out_ref[far] = refs[far][half]
 
 
 def regroup(pieces):
-    shape = (4, *pieces[0].shape[2:])
+    shape = (4, *pieces[0].shape[1:])
     return pl.pallas_call(
         regroup_kernel,
-        out_shape=[jax.ShapeDtypeStruct(shape, pieces[0].dtype)] * 4,
+        out_shape=[jax.ShapeDtypeStruct(shape, pieces[0].dtype)] * 2,
         name="regroup",
     )(*pieces)
 
 
-def gradient_kernel(place_ref, *refs):
-    kept, parts = refs[:2], refs[2 : 2 + 8 * CHUNKS]
-    weight_ref, resid_ref = refs[-8:-6]
-    targets, product_ref, target_ref = refs[-6:-2], refs[-2], refs[-1]
-    rows = resid_ref.shape[1]
+def gradient_kernel(place_ref, kept_ref, *refs):
+    parts = refs[: 4 * CHUNKS]
+    weight_ref, resid_ref = refs[4 * CHUNKS : 4 * CHUNKS + 2]
+    targets, (own_ref, give_ref), (target_ref, product_ref) = refs[-8:-4], refs[-4:-2], refs[-2:]
+    rows, wide = resid_ref.shape[1:]
+    width = wide // 2
+    piece = width // CHUNKS
+    core = place_ref[8]
     product_ref[...] = jnp.zeros_like(product_ref)
 
     def step(far, carry):
-        for side in range(2):
-            tokens = kept[side][far].reshape(2 * rows, -1)
-            wanted = []
-            for half in range(2):
-                block = place_ref[(far * 2 + half) * 2 + side]
-                start = pl.multiple_of((block // 2) * rows, rows)
-                sums = []
+        tokens = kept_ref[far].reshape(2 * rows, -1)
+        wanted = []
+        for half in range(2):
+            block = place_ref[far * 2 + half]
+            start = pl.multiple_of(block * rows, rows)
+            sums = []
+            for side in range(2):
                 for chunk in range(CHUNKS):
                     total = None
                     for source in range(4):
-                        part = parts[chunk * 8 + source * 2 + side]
-                        term = part[pl.ds(start, rows), :].astype(jnp.float32)
+                        part = parts[chunk * 4 + source]
+                        lanes = slice(side * piece, (side + 1) * piece)
+                        term = part[pl.ds(start, rows), lanes].astype(jnp.float32)
                         total = term if total is None else total + term
                     sums.append(total)
-                total = jnp.concatenate(sums, axis=1)
-                target = (resid_ref[block].astype(jnp.float32) + total).astype(jnp.bfloat16)
-                target_ref[far, half, side] = target
-                wanted.append(target)
-            predicted = jnp.dot(tokens, weight_ref[...], preferred_element_type=jnp.float32)
-            error = (predicted - jnp.concatenate(wanted).astype(jnp.float32)).astype(jnp.bfloat16)
-            product_ref[...] += lax.dot_general(
-                tokens, error, (((0,), (0,)), ((), ())), preferred_element_type=jnp.float32
-            )
+            resid = [
+                resid_ref[block, :, pl.ds(pl.multiple_of(column * width, width), width)]
+                for column in (core, 1 - core)
+            ]
+            resid = jnp.concatenate(resid, axis=1).astype(jnp.float32)
+            target = (resid + jnp.concatenate(sums, axis=1)).astype(jnp.bfloat16)
+            target_ref[far, half] = target
+            wanted.append(target)
+        predicted = jnp.dot(tokens, weight_ref[...], preferred_element_type=jnp.float32)
+        error = (predicted - jnp.concatenate(wanted).astype(jnp.float32)).astype(jnp.bfloat16)
+        product_ref[...] += lax.dot_general(
+            tokens, error, (((0,), (0,)), ((), ())), preferred_element_type=jnp.float32
+        )
         return carry
 
     lax.fori_loop(0, 4, step, 0)
     for far in range(4):
         targets[far][...] = target_ref[far]
+    own_ref[...] = product_ref[:, :width]
+    give_ref[...] = product_ref[:, width:]
 
 
 def gradient_term(places, kept, parts, weight, resid):
-    rows = resid.shape[1]
-    width = weight.shape[1]
-    piece = (2, 2, rows, width)
-    *targets, product = pl.pallas_call(
+    rows, wide = resid.shape[1:]
+    piece = (2, rows, wide)
+    half = (weight.shape[0], wide // 2)
+    *targets, own, give = pl.pallas_call(
         gradient_kernel,
         out_shape=(
             *[jax.ShapeDtypeStruct(piece, jnp.bfloat16)] * 4,
-            jax.ShapeDtypeStruct(weight.shape, jnp.float32),
+            *[jax.ShapeDtypeStruct(half, jnp.float32)] * 2,
         ),
         grid_spec=pltpu.PrefetchScalarGridSpec(
             num_scalar_prefetch=1,
             grid=(1,),
             in_specs=[
                 pl.BlockSpec(x.shape, lambda i, _, n=x.ndim: (0,) * n)
-                for x in (*kept, *parts, weight, resid)
+                for x in (kept, *parts, weight, resid)
             ],
             out_specs=(
-                *[pl.BlockSpec(piece, lambda i, _: (0, 0, 0, 0))] * 4,
-                pl.BlockSpec(weight.shape, lambda i, _: (0, 0)),
+                *[pl.BlockSpec(piece, lambda i, _: (0, 0, 0))] * 4,
+                *[pl.BlockSpec(half, lambda i, _: (0, 0))] * 2,
             ),
-            scratch_shapes=[pltpu.VMEM((4, *piece), jnp.bfloat16)],
+            scratch_shapes=[
+                pltpu.VMEM((4, *piece), jnp.bfloat16),
+                pltpu.VMEM(weight.shape, jnp.float32),
+            ],
         ),
         compiler_params=pltpu.CompilerParams(vmem_limit_bytes=58 * 1024 * 1024),
         name="gradient_term",
-    )(places, *kept, *parts, weight, resid)
-    return targets, product
+    )(places, kept, *parts, weight, resid)
+    return targets, own, give
 
 
 def place_kernel(column_ref, *refs):
     out_ref = refs[-1]
+    width = refs[0].shape[2] // 2
     for i, ref in enumerate(refs[:-1]):
         for far in range(4):
-            column = pl.multiple_of(column_ref[i * 4 + far], 128)
-            out_ref[:, pl.ds(column, ref.shape[2])] = ref[far]
+            for side in range(2):
+                column = pl.multiple_of(column_ref[(i * 4 + far) * 2 + side], width)
+                out_ref[:, pl.ds(column, width)] = ref[far, :, side * width : (side + 1) * width]
 
 
 def place_columns(columns, pieces, out_width):
@@ -264,6 +275,42 @@
     )
 
 
+def attend_kernel(query_ref, keyval_ref, allowed_ref, out_ref):
+    tok_rows, width = query_ref.shape
+    pair = 2 * HEAD_DIM
+    allowed = allowed_ref[...] > 0.0
+    lane = lax.broadcasted_iota(jnp.int32, (tok_rows, pair), 1)
+    for first in range(0, width, pair):
+        queries = query_ref[:, first : first + pair]
+        keys = keyval_ref[:, first : first + pair]
+        values = keyval_ref[:, width + first : width + first + pair]
+        mixed = []
+        for head in range(2):
+            inside = (lane < HEAD_DIM) if head == 0 else (lane >= HEAD_DIM)
+            mine = jnp.where(inside, queries.astype(jnp.float32), 0.0).astype(jnp.bfloat16)
+            scores = lax.dot_general(
+                mine, keys, (((1,), (1,)), ((), ())), preferred_element_type=jnp.float32
+            ) * (1.0 / math.sqrt(HEAD_DIM))
+            scores = jnp.where(allowed, scores, -jnp.inf)
+            exp_scores = jnp.exp(scores - jnp.max(scores, axis=-1, keepdims=True))
+            weights = exp_scores / jnp.sum(exp_scores, axis=-1, keepdims=True)
+            mixed.append(
+                jnp.dot(
+                    weights.astype(jnp.bfloat16), values, preferred_element_type=jnp.float32
+                )
+            )
+        out = jnp.where(lane < HEAD_DIM, mixed[0], mixed[1])
+        out_ref[:, first : first + pair] = out.astype(jnp.bfloat16)
+
+
+def attend(queries, keyvals, allowed):
+    return pl.pallas_call(
+        attend_kernel,
+        out_shape=jax.ShapeDtypeStruct(queries.shape, jnp.bfloat16),
+        name="attend_heads",
+    )(queries, keyvals, allowed)
+
+
 def student_hidden(widened_in, norm_gain, qkv_weight, out_weight, doc_ids):
     tok_rows, student_width = widened_in.shape[0] // 3, widened_in.shape[1]
     student_f = widened_in[tok_rows : 2 * tok_rows].astype(jnp.float32)
@@ -276,9 +323,6 @@
         qkv_weight[:, :student_width],
         preferred_element_type=jnp.float32,
     ).astype(jnp.bfloat16)
-    queries = queries.reshape(tok_rows, HEADS, HEAD_DIM)
-    keys_all = widened[:, :student_width].reshape(3 * tok_rows, HEADS, HEAD_DIM)
-    values_all = widened[:, student_width:].reshape(3 * tok_rows, HEADS, HEAD_DIM)
     first_pos = lax.axis_index(COL) * tok_rows
     query_pos = first_pos + jnp.arange(tok_rows, dtype=jnp.int32)
     key_pos = first_pos - tok_rows + jnp.arange(3 * tok_rows, dtype=jnp.int32)
@@ -289,15 +333,7 @@
     allowed = (query_docs[:, None] == key_docs[None, :]) & (
         jnp.abs(query_pos[:, None] - key_pos[None, :]) <= tok_rows
     )
-    scores = jnp.einsum("qhd,khd->hqk", queries, keys_all, preferred_element_type=jnp.float32) * (
-        1.0 / math.sqrt(HEAD_DIM)
-    )
-    scores = jnp.where(allowed[None], scores, -jnp.inf)
-    row_max = jnp.max(scores, axis=-1, keepdims=True)
-    exp_scores = jnp.exp(scores - row_max)
-    weights = (exp_scores / jnp.sum(exp_scores, axis=-1, keepdims=True)).astype(jnp.bfloat16)
-    attended = jnp.einsum("hqk,khd->qhd", weights, values_all, preferred_element_type=jnp.float32)
-    attended = attended.reshape(tok_rows, student_width).astype(jnp.bfloat16)
+    attended = attend(queries, widened, allowed.astype(jnp.float32))
     return (student_f + jnp.dot(attended, out_weight, preferred_element_type=jnp.float32)).astype(
         jnp.bfloat16
     )
@@ -328,15 +364,11 @@
     own, other = [], []
     whole, *nears = pack(across)
     whole = flip(whole, "core")
-    for chunk, near in enumerate(nears):
+    for near in nears:
         along_y = [near] + [shift(near, ("y",), -step) for step in (1, 3, 2)]
         along_y = [along_y[i] for i in (0, 1, 3, 2)]
         own.append(along_y)
-        if chunk:
-            stack = jnp.stack(along_y[1:])
-            other.append((whole, flip(stack, "core")))
-        else:
-            other.append([whole] + [flip(piece, "core") for piece in along_y[1:]])
+        other.append([whole] + [flip(piece, "core") for piece in along_y[1:]])
 
     by_core = context_heads.reshape(row_tokens // (2 * tok_rows), 2, tok_rows, depth)
     here, there = (
@@ -345,8 +377,10 @@
     )
     heads = (here, flip(there, "core"), flip(here, "zl"), flip(there, "zl", "core"))
 
-    by_owner = teacher_resid.reshape(tok_rows, 2, 2, 2, 2, half_width).transpose(1, 4, 2, 3, 0, 5)
-    resid_cols = exchange(by_owner.reshape(16, tok_rows, half_width), COL)
+    by_owner = teacher_resid.reshape(tok_rows, 2, 2, 2, 2, half_width).transpose(1, 4, 2, 0, 3, 5)
+    resid_cols = exchange(
+        by_owner.reshape(8, tok_rows, 2 * half_width), ("zh", "zl", "xh")
+    )
 
     before, after = neighbours(student_in)
     widened_in = jnp.concatenate([before, student_in, after])
@@ -356,7 +390,6 @@
     kept = jnp.stack([kept, flip(kept, "xh")])
     from_z = [shift(kept, Z, far) for far in (1, 2, 3)]
     kept = jnp.stack([kept, *from_z])
-    kept_all = (kept, flip(kept, "core"))
 
     steps = jnp.arange(4, dtype=jnp.int32)
     pair = jnp.arange(2, dtype=jnp.int32)
@@ -365,11 +398,18 @@
         + jnp.bitwise_xor(jnp.bitwise_xor(xl, core), pair)[None]
     ).reshape(8)
     places = (
-        ((z - steps) % 4)[:, None, None] * 4
-        + jnp.bitwise_xor(xh, pair)[None, :, None] * 2
-        + jnp.bitwise_xor(core, pair)[None, None, :]
-    ).reshape(16)
-    block = (owner * 2 + core) * 2 + zl
+        ((z - steps) % 4)[:, None] * 2 + jnp.bitwise_xor(xh, pair)[None, :]
+    ).reshape(8)
+    places = jnp.concatenate([places, core.reshape(1)])
+    weight = jnp.concatenate(
+        [
+            lax.dynamic_slice_in_dim(
+                head_weight, (owner * 4 + half * 2 + zl) * half_width, half_width, axis=1
+            )
+            for half in (core, 1 - core)
+        ],
+        axis=1,
+    )
     sent = []
     for chunk in range(CHUNKS):
         sent.append(teacher_partials(slots, heads, own[chunk], other[chunk], chunk))
@@ -377,24 +417,25 @@
     parts = []
     for chunk in range(CHUNKS):
         for far in range(4):
-            for side in range(2):
-                axes = ("zh",) * (far // 2) + ("xh",) * (far % 2) + ("core",) * side
-                part = sent[chunk][far * 2 + side]
-                parts.append(flip(part, *axes) if axes else part)
-    weight = lax.dynamic_slice_in_dim(head_weight, block * half_width, half_width, axis=1)
-    targets, product = gradient_term(places, kept_all, parts, weight, resid_cols)
+            axes = ("zh",) * (far // 2) + ("xh",) * (far % 2)
+            part = sent[chunk][far]
+            parts.append(flip(part, *axes) if axes else part)
+    targets, product, give = gradient_term(places, kept, parts, weight, resid_cols)
+    product = product + flip(give, "core")
     grad_pieces = exchange(product.reshape(everyone, student_width // everyone, half_width), AXES)
     head_grad = sum_rows([grad_pieces], out_width, 1.0 / row_tokens)
     targets = [targets[0]] + [shift(targets[far], Z, -far) for far in (1, 2, 3)]
-    grouped = regroup(targets)
-    target_pieces, columns = [], []
-    for i, piece in enumerate(grouped):
-        axes = ("xh",) * (i // 2) + ("core",) * (i % 2)
-        target_pieces.append(flip(piece, *axes) if axes else piece)
-        from_z = (z + steps) % 4
-        source = from_z // 2 * 8 + (xh ^ (i // 2)) * 4 + (core ^ (i % 2)) * 2 + from_z % 2
-        columns.append(source * half_width)
-    target = place_columns(jnp.concatenate(columns), target_pieces, out_width)
+    near, far_half = regroup(targets)
+    pieces = (near, flip(far_half, "xh"))
+    from_z = (z + steps) % 4
+    columns = [
+        (
+            (from_z // 2 * 8 + (xh ^ half) * 4 + from_z % 2)[:, None]
+            + jnp.bitwise_xor(core, pair)[None] * 2
+        ).reshape(8)
+        for half in range(2)
+    ]
+    target = place_columns(jnp.concatenate(columns) * half_width, pieces, out_width)
     return (target, prediction, head_grad)
 
 

time: 293 us -> 268 us (0.915)
  starting transfers between devices: 82.8 us -> 66.1 us
  waiting for transfers between devices: 120 us -> 107 us
  Pallas kernels: 43.1 us -> 49.8 us
  other arithmetic: 8 us -> 13.4 us
  matrix products: 20.1 us -> 15.4 us
    ppermute x14, waiting for transfers between devices: 62.5 us -> 46.9 us  [shift(): lax.ppermute(array, axes, [(i, (i + step) % size) for i in range(size)])]
    ppermute x30 -> x22, starting transfers between devices: 43 us -> 30.7 us  [flip(): return lax.ppermute(array, axes, [(i, last - i) for i in range(last + 1)])]
    pallas_call x2 -> x3, Pallas kernels: 23.1 us -> 30.2 us  [the longest x2 22.5 us: teacher_partials(): pl.pallas_call(partial_kernel, out_shape=[jax.ShapeDtypeStruct((tokens, 2...]
    slice x3 -> x0, local copies, waits for them, and re-layouts: 4.46 us -> none  [the longest x2 3.3 us: student_hidden(): keys_all = widened[:, :student_width].reshape(3 * tok_rows, HEADS, HEAD_DIM)]
    sub x1 -> x0, matrix products: 3.95 us -> none  [student_hidden(): exp_scores = jnp.exp(scores - row_max)]
    another operation x2, other arithmetic: 1.65 us -> 5.01 us  [body(): kept = jnp.stack([kept, *from_z])]
    ppermute x30 -> x22, waiting for transfers between devices: 57.4 us -> 60.3 us  [flip(): return lax.ppermute(array, axes, [(i, last - i) for i in range(last + 1)])]
  transfers between devices with their start and end apart: 46 -> 38, of which waited for: 17 -> 12; matrix products, arithmetic and copies ran while one was open for 14% -> 14% of each run, Pallas kernels for 11% -> 14%
where the time goes in v2:
time: 268 us; the launch traced here: 267 us
  waiting for transfers between devices  107 us (40%)
  starting transfers between devices  66.1 us (25%)
  Pallas kernels  49.8 us (19%)
  matrix products  15.4 us (6%)
  local copies, waits for them, and re-layouts  14.4 us (5%)
  other arithmetic  13.4 us (5%)
    ppermute x22, waiting for transfers between devices, flip(): return lax.ppermute(array, axes, [(i, last - i) for i in range(last + 1)])  60.3 us
    ppermute x14, waiting for transfers between devices, shift(): lax.ppermute(array, axes, [(i, (i + step) % size) for i in range(size)])  46.9 us
    ppermute x22, starting transfers between devices, flip(): return lax.ppermute(array, axes, [(i, last - i) for i in range(last + 1)])  30.7 us
    ppermute x14, starting transfers between devices, shift(): lax.ppermute(array, axes, [(i, (i + step) % size) for i in range(size)])  24.8 us
    pallas_call x2, Pallas kernels, teacher_partials(): pl.pallas_call(partial_kernel, out_shape=[jax.ShapeDtypeStruct((tokens, 2...  22.5 us
    all_to_all x2, starting transfers between devices, exchange(): return lax.all_to_all(blocks, axes, 0, 0, tiled=True)  10.6 us
    pallas_call x1, Pallas kernels, gradient_term(): pl.pallas_call(gradient_kernel, out_shape=(*[jax.ShapeDtypeStruct(piece,...  9.71 us
    pallas_call x1, Pallas kernels, attend(): pl.pallas_call(attend_kernel, out_shape=jax.ShapeDtypeStruct(queries.shap...  7.73 us
  transfers between devices with their start and end apart: 38, of which 12 were waited for; matrix products, arithmetic and copies ran while one was open for 14% of the time, Pallas kernels for 14%

profile of v2, /device:TPU:0, one launch (start us, length us, event | category | flops | bytes accessed | tf_op | source)
XLA Modules:
  0.0 267.2 jit_solution(11571005404601092786)
XLA Ops:
  1.9 3.0 %collective-permute-start.11 = (bf16[512,256]{1,0:T(8,128)(2,1)S(1)}, bf16[512,256]{1,0:T(8,128)(2,1)}, u32[]{:S(2)}, u32[]{:S(2)}) collective-permute-start(bf16[512,256]{1,0:T(8,128)(2,1)S(1)} %get-tuple-element.45), channel_id=1, source_target_pairs={{0,20},{4,16},{16,4},{20,0},{1,21},{5,17},{17,5},{21,1},{2,22},{6,... | collective-permute-start | bytes 786440 | tf_op jit(solution)/shard_map/ppermute | solution.py:32
  5.1 5.4 %collective-permute-start.1 = (bf16[128,1024]{1,0:T(8,128)(2,1)}, bf16[128,1024]{1,0:T(8,128)(2,1)S(1)}, u32[]{:S(2)}, u32[]{:S(2)}) collective-permute-start(bf16[128,1024]{1,0:T(8,128)(2,1)} %param.13), channel_id=1, source_target_pairs={{0,15},{1,0},{2,1},{3,2},{4,3},{5,4},{6,5},{7,6},{8,7},{9,8},{10,9... | collective-permute-start | bytes 786440 | tf_op jit(solution)/shard_map/ppermute | solution.py:27
  14.7 8.2 %collective-permute-done.10.refs_2_ = bf16[512,256]{1,0:T(8,128)(2,1)} collective-permute-done((bf16[512,256]{1,0:T(8,128)(2,1)S(1)}, bf16[512,256]{1,0:T(8,128)(2,1)}, u32[]{:S(2)}, u32[]{:S(2)}) %collective-permute-start.10) | collective-permute-done | bytes 262176 | tf_op jit(solution)/shard_map/ppermute | solution.py:32
  22.9 2.8 %pack.1 = (bf16[2,2,2,512,128]{4,3,2,1,0:T(8,128)(2,1)}, bf16[2,2,512,128]{3,2,1,0:T(8,128)(2,1)}, bf16[2,2,512,128]{3,2,1,0:T(8,128)(2,1)}) custom-call(bf16[512,256]{1,0:T(8,128)(2,1)} %copy-done.9, bf16[512,256]{1,0:T(8,128)(2,1)} %collective-permute-done.9.refs_1_, bf16[512,256]{1,0:T(8,128)(2,1)} %collective-permute-done.10.refs_2_, ...), custom_call_target="tpu_custom_call" | custom-call | tf_op jit(solution)/shard_map/pack/pallas_call | solution.py:113
  25.7 3.0 %collective-permute-start.22 = (bf16[2,2,512,128]{3,2,1,0:T(8,128)(2,1)}, bf16[2,2,512,128]{3,2,1,0:T(8,128)(2,1)S(1)}, u32[]{:S(2)}, u32[]{:S(2)}) collective-permute-start(bf16[2,2,512,128]{3,2,1,0:T(8,128)(2,1)} %get-tuple-element.28.refs_4_), channel_id=1, source_target_pairs={{0,96},{32,0},{64,32},{96,64},{1,97},{33,1},{65,33},{97,65},{2,98}... | collective-permute-start | bytes 1572872 | tf_op jit(solution)/shard_map/ppermute | solution.py:27
  30.8 5.1 %fusion.2.keyval_ref = bf16[384,2048]{1,0:T(8,128)(2,1)} fusion(bf16[384,1024]{1,0:T(8,128)(2,1)S(1)} %fusion.9, bf16[1024,3072]{1,0:T(8,128)(2,1)} %param.15), kind=kOutput, calls=%fused_computation.2 | convolution fusion | flops 1611399168 | bytes 6553600 | tf_op jit(solution)/shard_map/dot_general | solution.py:318
  36.0 2.7 %fusion.10.query_ref = bf16[128,1024]{1,0:T(8,128)(2,1)} fusion(bf16[1024,3072]{1,0:T(8,128)(2,1)} %param.15, bf16[384,1024]{1,0:T(8,128)(2,1)S(1)} %fusion.9), kind=kOutput, calls=%fused_computation.12 | convolution fusion | flops 268566528 | bytes 2621440 | tf_op jit(solution)/shard_map/dot_general | solution.py:321
  38.7 2.3 collective-permute-start.12
  41.0 7.7 %attend_heads.1 = bf16[128,1024]{1,0:T(8,128)(2,1)} custom-call(bf16[128,1024]{1,0:T(8,128)(2,1)} %fusion.10.query_ref, bf16[384,2048]{1,0:T(8,128)(2,1)} %fusion.2.keyval_ref, f32[128,384]{1,0:T(8,128)} %fusion.16.allowed_ref), custom_call_target="tpu_custom_call" | custom-call | tf_op jit(solution)/shard_map/attend_heads/pallas_call | solution.py:307
  50.1 3.1 %collective-permute-start.2 = (bf16[128,1024]{1,0:T(8,128)(2,1)S(1)}, bf16[128,1024]{1,0:T(8,128)(2,1)S(1)}, u32[]{:S(2)}, u32[]{:S(2)}) collective-permute-start(bf16[128,1024]{1,0:T(8,128)(2,1)S(1)} %get-tuple-element.51), channel_id=1, source_target_pairs={{0,2},{2,0},{1,3},{3,1},{4,6},{6,4},{5,7},{7,5},{8,10},{10,8},{9,1... | collective-permute-start | bytes 786440 | tf_op jit(solution)/shard_map/ppermute | solution.py:32
  53.2 2.7 %constant_dynamic-slice_fusion.4 = (bf16[8,1,128,512]{3,2,1,0:T(8,128)(2,1)}, bf16[8,1,128,512]{3,2,1,0:T(8,128)(2,1)S(1)}) fusion(bf16[8,2,128,512]{3,2,1,0:T(8,128)(2,1)} %bitcast.29, s32[]{:T(128)S(6)} %select_n.94, s32[]{:T(128)S(6)} %select_n.93), kind=kLoop, calls=%fused_computation.46 | loop fusion | bytes 4194312 | tf_op jit(solution)/shard_map/jit(dynamic_index_in_dim)/dynamic_slice | solution.py:375
  55.9 2.2 collective-permute-done.2
  59.2 1.8 collective-permute-start.8
  61.1 1.7 collective-permute-start.13
  63.0 14.7 %collective-permute-done.13.refs_6_ = bf16[2,2,512,128]{3,2,1,0:T(8,128)(2,1)S(1)} collective-permute-done((bf16[2,2,512,128]{3,2,1,0:T(8,128)(2,1)}, bf16[2,2,512,128]{3,2,1,0:T(8,128)(2,1)S(1)}, u32[]{:S(2)}, u32[]{:S(2)}) %collective-permute-start.13) | collective-permute-done | bytes 524320 | tf_op jit(solution)/shard_map/ppermute | solution.py:27
  77.6 10.2 %collective-permute-done.14.refs_7_ = bf16[2,2,512,128]{3,2,1,0:T(8,128)(2,1)S(1)} collective-permute-done((bf16[2,2,512,128]{3,2,1,0:T(8,128)(2,1)}, bf16[2,2,512,128]{3,2,1,0:T(8,128)(2,1)S(1)}, u32[]{:S(2)}, u32[]{:S(2)}) %collective-permute-start.14) | collective-permute-done | bytes 524320 | tf_op jit(solution)/shard_map/ppermute | solution.py:27
  89.2 11.0 %collective-permute-done.8.refs_3_ = bf16[1024,512]{1,0:T(8,128)(2,1)} collective-permute-done((bf16[1024,512]{1,0:T(8,128)(2,1)}, bf16[1024,512]{1,0:T(8,128)(2,1)}, u32[]{:S(2)}, u32[]{:S(2)}) %collective-permute-start.8) | collective-permute-done | bytes 1048608 | tf_op jit(solution)/shard_map/ppermute | solution.py:32
  100.2 2.0 collective-permute-start.16
  102.9 2.1 fusion.26
  105.8 3.6 %collective-permute-start.4 = (bf16[2,128,1024]{2,1,0:T(8,128)(2,1)}, bf16[2,128,1024]{2,1,0:T(8,128)(2,1)}, u32[]{:S(2)}, u32[]{:S(2)}) collective-permute-start(bf16[2,128,1024]{2,1,0:T(8,128)(2,1)} %get-tuple-element.48), channel_id=1, source_target_pairs={{0,8},{4,12},{8,0},{12,4},{1,9},{5,13},{9,1},{13,5},{2,10},{6,14},... | collective-permute-start | bytes 1572872 | tf_op jit(solution)/shard_map/ppermute | solution.py:27
  109.4 11.3 %teacher_partials.3 = (bf16[1024,256]{1,0:T(8,128)(2,1)}, bf16[1024,256]{1,0:T(8,128)(2,1)}, bf16[1024,256]{1,0:T(8,128)(2,1)}, bf16[1024,256]{1,0:T(8,128)(2,1)}) custom-call(s32[8]{0:T(128)} %add.306.slot_ref, bf16[1024,512]{1,0:T(8,128)(2,1)} %bitcast.26, bf16[1024,512]{1,0:T(8,128)(2,1)} %copy-done.4, bf16[1024,512]{1,0:T(8,128)(2,1)} %copy-done.3, ...), custom_call_target="tpu_custom_call" | custom-call | tf_op jit(solution)/shard_map/teacher_partials/pallas_call | solution.py:76
  120.7 2.4 collective-permute-start.5
  123.1 3.1 %collective-permute-start.28 = (bf16[1024,256]{1,0:T(8,128)(2,1)}, bf16[1024,256]{1,0:T(8,128)(2,1)S(1)}, u32[]{:S(2)}, u32[]{:S(2)}) collective-permute-start(bf16[1024,256]{1,0:T(8,128)(2,1)} %get-tuple-element.30), channel_id=1, source_target_pairs={{0,2},{2,0},{1,3},{3,1},{4,6},{6,4},{5,7},{7,5},{8,10},{10,8},{9,1... | collective-permute-start | bytes 1572872 | tf_op jit(solution)/shard_map/ppermute | solution.py:32
  126.2 1.8 reshape.166
  128.9 1.5 reshape.167
  130.4 3.6 %all-to-all-start = ((bf16[8,128,512]{2,1,0:T(8,128)(2,1)}), bf16[8,128,512]{2,1,0:T(8,128)(2,1)S(1)}, u32[]{:S(2)}, u32[]{:S(2)}) async-start(bf16[8,128,512]{2,1,0:T(8,128)(2,1)} %reshape.167), calls=%async_computation | async-start | bytes 2097152 | tf_op jit(solution)/shard_map/all_to_all | solution.py:22
  134.1 3.4 %collective-permute-start.29 = (bf16[1024,256]{1,0:T(8,128)(2,1)}, bf16[1024,256]{1,0:T(8,128)(2,1)S(1)}, u32[]{:S(2)}, u32[]{:S(2)}) collective-permute-start(bf16[1024,256]{1,0:T(8,128)(2,1)} %get-tuple-element.31), channel_id=1, source_target_pairs={{0,8},{8,0},{1,9},{9,1},{2,10},{10,2},{3,11},{11,3},{4,12},{12,4},... | collective-permute-start | bytes 1572872 | tf_op jit(solution)/shard_map/ppermute | solution.py:32
  137.6 11.2 %teacher_partials.2 = (bf16[1024,256]{1,0:T(8,128)(2,1)}, bf16[1024,256]{1,0:T(8,128)(2,1)}, bf16[1024,256]{1,0:T(8,128)(2,1)}, bf16[1024,256]{1,0:T(8,128)(2,1)}) custom-call(s32[8]{0:T(128)} %add.306.slot_ref, bf16[1024,512]{1,0:T(8,128)(2,1)} %bitcast.27, bf16[1024,512]{1,0:T(8,128)(2,1)} %copy-done.4, bf16[1024,512]{1,0:T(8,128)(2,1)} %copy-done.3, ...), custom_call_target="tpu_custom_call" | custom-call | tf_op jit(solution)/shard_map/teacher_partials/pallas_call | solution.py:76
  148.8 3.0 %collective-permute-start.30 = (bf16[1024,256]{1,0:T(8,128)(2,1)}, bf16[1024,256]{1,0:T(8,128)(2,1)}, u32[]{:S(2)}, u32[]{:S(2)}) collective-permute-start(bf16[1024,256]{1,0:T(8,128)(2,1)} %get-tuple-element.32), channel_id=1, source_target_pairs={{0,10},{2,8},{8,2},{10,0},{1,11},{3,9},{9,3},{11,1},{4,14},{6,12},... | collective-permute-start | bytes 1572872 | tf_op jit(solution)/shard_map/ppermute | solution.py:32
  152.0 3.4 %collective-permute-start.20 = (bf16[1024,256]{1,0:T(8,128)(2,1)}, bf16[1024,256]{1,0:T(8,128)(2,1)}, u32[]{:S(2)}, u32[]{:S(2)}) collective-permute-start(bf16[1024,256]{1,0:T(8,128)(2,1)} %get-tuple-element.26), channel_id=1, source_target_pairs={{0,8},{8,0},{1,9},{9,1},{2,10},{10,2},{3,11},{11,3},{4,12},{12,4},... | collective-permute-start | bytes 1572872 | tf_op jit(solution)/shard_map/ppermute | solution.py:32
  155.4 2.9 %collective-permute-start.21 = (bf16[1024,256]{1,0:T(8,128)(2,1)}, bf16[1024,256]{1,0:T(8,128)(2,1)}, u32[]{:S(2)}, u32[]{:S(2)}) collective-permute-start(bf16[1024,256]{1,0:T(8,128)(2,1)} %get-tuple-element.27), channel_id=1, source_target_pairs={{0,10},{2,8},{8,2},{10,0},{1,11},{3,9},{9,3},{11,1},{4,14},{6,12},... | collective-permute-start | bytes 1572872 | tf_op jit(solution)/shard_map/ppermute | solution.py:32
  161.3 2.9 %pad_maximum_fusion.kept_ref = bf16[4,2,128,1024]{3,2,1,0:T(8,128)(2,1)} fusion(bf16[1,2,128,1024]{3,2,1,0:T(8,128)(2,1)} %bitcast.6, bf16[1,2,128,1024]{3,2,1,0:T(8,128)(2,1)} %bitcast.5, bf16[1,2,128,1024]{3,2,1,0:T(8,128)(2,1)} %bitcast.4, bf16[1,2,128,1024]{3,2,1,0:T(8,128)(2,1)S(1)} %copy-done.8), kind=kLoop, calls=%fused_computation.3 | loop fusion | flops 3145728 | bytes 4194304 | tf_op jit(solution)/shard_map/stack | solution.py:392
  164.3 8.6 %collective-permute-done.29.refs_6_ = bf16[1024,256]{1,0:T(8,128)(2,1)S(1)} collective-permute-done((bf16[1024,256]{1,0:T(8,128)(2,1)}, bf16[1024,256]{1,0:T(8,128)(2,1)S(1)}, u32[]{:S(2)}, u32[]{:S(2)}) %collective-permute-start.29) | collective-permute-done | bytes 524320 | tf_op jit(solution)/shard_map/ppermute | solution.py:32
  172.8 3.5 %collective-permute-done.19.refs_1_ = bf16[1024,256]{1,0:T(8,128)(2,1)} collective-permute-done((bf16[1024,256]{1,0:T(8,128)(2,1)}, bf16[1024,256]{1,0:T(8,128)(2,1)}, u32[]{:S(2)}, u32[]{:S(2)}) %collective-permute-start.19) | collective-permute-done | bytes 524320 | tf_op jit(solution)/shard_map/ppermute | solution.py:32
  176.3 17.0 %collective-permute-done.20.refs_2_ = bf16[1024,256]{1,0:T(8,128)(2,1)} collective-permute-done((bf16[1024,256]{1,0:T(8,128)(2,1)}, bf16[1024,256]{1,0:T(8,128)(2,1)}, u32[]{:S(2)}, u32[]{:S(2)}) %collective-permute-start.20) | collective-permute-done | bytes 524320 | tf_op jit(solution)/shard_map/ppermute | solution.py:32
  193.3 9.7 %gradient_term.1 = (bf16[2,128,512]{2,1,0:T(8,128)(2,1)}, bf16[2,128,512]{2,1,0:T(8,128)(2,1)}, bf16[2,128,512]{2,1,0:T(8,128)(2,1)}, bf16[2,128,512]{2,1,0:T(8,...) custom-call(s32[9]{0:T(128)} %pad_add_fusion.place_ref, bf16[4,2,128,1024]{3,2,1,0:T(8,128)(2,1)} %pad_maximum_fusion.kept_ref, ...), custom_call_target="tpu_custom_call" | custom-call | tf_op jit(solution)/shard_map/gradient_term/pallas_call | solution.py:190
  203.1 2.9 %collective-permute-done.35 = f32[1024,256]{1,0:T(8,128)S(1)} collective-permute-done((f32[1024,256]{1,0:T(8,128)}, f32[1024,256]{1,0:T(8,128)S(1)}, u32[]{:S(2)}, u32[]{:S(2)}) %collective-permute-start.35) | collective-permute-done | bytes 1048608 | tf_op jit(solution)/shard_map/ppermute | solution.py:32
  205.9 2.5 add_bitcast_fusion
  208.4 7.1 %all-to-all-start.1 = ((f32[128,8,256]{2,1,0:T(8,128)}), f32[128,8,256]{2,1,0:T(8,128)S(1)}, u32[]{:S(2)}, u32[]{:S(2)}) async-start(f32[128,8,256]{2,1,0:T(8,128)} %add_bitcast_fusion), calls=%async_computation.1 | async-start | bytes 2097152 | tf_op jit(solution)/shard_map/all_to_all | solution.py:22
  215.5 2.9 %collective-permute-start.31 = (bf16[2,128,512]{2,1,0:T(8,128)(2,1)S(1)}, bf16[2,128,512]{2,1,0:T(8,128)(2,1)S(1)}, u32[]{:S(2)}, u32[]{:S(2)}) collective-permute-start(bf16[2,128,512]{2,1,0:T(8,128)(2,1)S(1)} %copy-done.22), channel_id=1, source_target_pairs={{0,12},{4,0},{8,4},{12,8},{1,13},{5,1},{9,5},{13,9},{2,14},{6,2},{... | collective-permute-start | bytes 786440 | tf_op jit(solution)/shard_map/ppermute | solution.py:27
  220.7 18.5 %collective-permute-done.31.refs_1_ = bf16[2,128,512]{2,1,0:T(8,128)(2,1)S(1)} collective-permute-done((bf16[2,128,512]{2,1,0:T(8,128)(2,1)S(1)}, bf16[2,128,512]{2,1,0:T(8,128)(2,1)S(1)}, u32[]{:S(2)}, u32[]{:S(2)}) %collective-permute-start.31) | collective-permute-done | bytes 262176 | tf_op jit(solution)/shard_map/ppermute | solution.py:27
  239.2 3.5 %collective-permute-done.33.refs_3_ = bf16[2,128,512]{2,1,0:T(8,128)(2,1)S(1)} collective-permute-done((bf16[2,128,512]{2,1,0:T(8,128)(2,1)S(1)}, bf16[2,128,512]{2,1,0:T(8,128)(2,1)S(1)}, u32[]{:S(2)}, u32[]{:S(2)}) %collective-permute-start.33) | collective-permute-done | bytes 262176 | tf_op jit(solution)/shard_map/ppermute | solution.py:27
  243.4 2.2 regroup.1
  245.6 2.7 collective-permute-start.34
  248.2 6.1 %fusion.27 = f32[128,4096]{1,0:T(8,128)} fusion(bf16[128,1024]{1,0:T(8,128)(2,1)S(1)} %get-tuple-element.52, bf16[1024,4096]{1,0:T(8,128)(2,1)} %param.17), kind=kOutput, calls=%fused_computation.72 | convolution fusion | flops 1073741824 | bytes 10747904 | tf_op jit(solution)/shard_map/dot_general | solution.py:388
  254.3 6.9 %collective-permute-done.34.refs_1_ = bf16[4,128,512]{2,1,0:T(8,128)(2,1)} collective-permute-done((bf16[4,128,512]{2,1,0:T(8,128)(2,1)}, bf16[4,128,512]{2,1,0:T(8,128)(2,1)}, u32[]{:S(2)}, u32[]{:S(2)}) %collective-permute-start.34) | collective-permute-done | bytes 524320 | tf_op jit(solution)/shard_map/ppermute | solution.py:32
  261.3 2.9 %place_columns.1 = bf16[128,4096]{1,0:T(8,128)(2,1)} custom-call(s32[16]{0:T(128)} %add_multiply_fusion.column_ref, bf16[4,128,512]{2,1,0:T(8,128)(2,1)} %get-tuple-element.37.refs_0_, bf16[4,128,512]{2,1,0:T(8,128)(2,1)} %collective-permute-done.34.refs_1_), custom_call_target="tpu_custom_call" | custom-call | tf_op jit(solution)/shard_map/place_columns/pallas_call | solution.py:230
  265.2 1.9 sum_rows.1
  (120 shorter events, 21.5 us)
Async XLA Ops:
  0.6 48.1 %copy-start = (bf16[1024,1024]{1,0:T(8,128)(2,1)S(1)}, bf16[1024,1024]{1,0:T(8,128)(2,1)}, u32[]{:S(2)}) copy-start(bf16[1024,1024]{1,0:T(8,128)(2,1)} %param.16) | copy-start | bytes 6291460
  0.6 29.7 %copy-start.7 = (bf16[128,1024]{1,0:T(8,128)(2,1)S(1)}, bf16[128,1024]{1,0:T(8,128)(2,1)}, u32[]{:S(2)}) copy-start(bf16[128,1024]{1,0:T(8,128)(2,1)} %param.13) | copy-start | bytes 786436
  1.9 21.0 %copy-start.9 = (bf16[512,256]{1,0:T(8,128)(2,1)}, bf16[512,256]{1,0:T(8,128)(2,1)S(1)}, u32[]{:S(2)}) copy-start(bf16[512,256]{1,0:T(8,128)(2,1)S(1)} %get-tuple-element.46.refs_0_) | copy-start | bytes 786436
  1.9 21.0 %collective-permute-start.11 = (bf16[512,256]{1,0:T(8,128)(2,1)S(1)}, bf16[512,256]{1,0:T(8,128)(2,1)}, u32[]{:S(2)}, u32[]{:S(2)}) collective-permute-start(bf16[512,256]{1,0:T(8,128)(2,1)S(1)} %get-tuple-element.45), channel_id=1, source_target_pairs={{0,20},{4,16},{16,4},{20,0},{1,21},{5,17},{17,5},{21,1},{2,22},{6,... | collective-permute-start | bytes 786440 | tf_op jit(solution)/shard_map/ppermute | solution.py:32
  5.0 17.9 %collective-permute-start.9 = (bf16[512,256]{1,0:T(8,128)(2,1)S(1)}, bf16[512,256]{1,0:T(8,128)(2,1)}, u32[]{:S(2)}, u32[]{:S(2)}) collective-permute-start(bf16[512,256]{1,0:T(8,128)(2,1)S(1)} %get-tuple-element.45), channel_id=1, source_target_pairs={{0,4},{4,0},{1,5},{5,1},{2,6},{6,2},{3,7},{7,3},{8,12},{12,8},{9,1... | collective-permute-start | bytes 786440 | tf_op jit(solution)/shard_map/ppermute | solution.py:32
  5.1 25.3 %collective-permute-start = (bf16[128,1024]{1,0:T(8,128)(2,1)}, bf16[128,1024]{1,0:T(8,128)(2,1)S(1)}, u32[]{:S(2)}, u32[]{:S(2)}) collective-permute-start(bf16[128,1024]{1,0:T(8,128)(2,1)} %param.13), channel_id=1, source_target_pairs={{0,1},{1,2},{2,3},{3,4},{4,5},{5,6},{6,7},{7,8},{8,9},{9,10},{10,1... | collective-permute-start | bytes 786440 | tf_op jit(solution)/shard_map/ppermute | solution.py:27
  5.1 25.3 %collective-permute-start.1 = (bf16[128,1024]{1,0:T(8,128)(2,1)}, bf16[128,1024]{1,0:T(8,128)(2,1)S(1)}, u32[]{:S(2)}, u32[]{:S(2)}) collective-permute-start(bf16[128,1024]{1,0:T(8,128)(2,1)} %param.13), channel_id=1, source_target_pairs={{0,15},{1,0},{2,1},{3,2},{4,3},{5,4},{6,5},{7,6},{8,7},{9,8},{10,9... | collective-permute-start | bytes 786440 | tf_op jit(solution)/shard_map/ppermute | solution.py:27
  10.4 12.5 %collective-permute-start.10 = (bf16[512,256]{1,0:T(8,128)(2,1)S(1)}, bf16[512,256]{1,0:T(8,128)(2,1)}, u32[]{:S(2)}, u32[]{:S(2)}) collective-permute-start(bf16[512,256]{1,0:T(8,128)(2,1)S(1)} %get-tuple-element.46.refs_0_), channel_id=1, source_target_pairs={{0,16},{16,0},{1,17},{17,1},{2,18},{18,2},{3,19},{19,3},{4,20},{20... | collective-permute-start | bytes 786440 | tf_op jit(solution)/shard_map/ppermute | solution.py:32
  25.7 32.7 %collective-permute-start.22 = (bf16[2,2,512,128]{3,2,1,0:T(8,128)(2,1)}, bf16[2,2,512,128]{3,2,1,0:T(8,128)(2,1)S(1)}, u32[]{:S(2)}, u32[]{:S(2)}) collective-permute-start(bf16[2,2,512,128]{3,2,1,0:T(8,128)(2,1)} %get-tuple-element.28.refs_4_), channel_id=1, source_target_pairs={{0,96},{32,0},{64,32},{96,64},{1,97},{33,1},{65,33},{97,65},{2,98}... | collective-permute-start | bytes 1572872 | tf_op jit(solution)/shard_map/ppermute | solution.py:27
  28.7 30.5 %collective-permute-start.23 = (bf16[2,2,512,128]{3,2,1,0:T(8,128)(2,1)}, bf16[2,2,512,128]{3,2,1,0:T(8,128)(2,1)}, u32[]{:S(2)}, u32[]{:S(2)}) collective-permute-start(bf16[2,2,512,128]{3,2,1,0:T(8,128)(2,1)} %get-tuple-element.28.refs_4_), channel_id=1, source_target_pairs={{0,64},{32,96},{64,0},{96,32},{1,65},{33,97},{65,1},{97,33},{2,66}... | collective-permute-start | bytes 1572872 | tf_op jit(solution)/shard_map/ppermute | solution.py:27
  29.3 31.7 %collective-permute-start.24 = (bf16[2,2,512,128]{3,2,1,0:T(8,128)(2,1)}, bf16[2,2,512,128]{3,2,1,0:T(8,128)(2,1)}, u32[]{:S(2)}, u32[]{:S(2)}) collective-permute-start(bf16[2,2,512,128]{3,2,1,0:T(8,128)(2,1)} %get-tuple-element.28.refs_4_), channel_id=1, source_target_pairs={{0,32},{32,64},{64,96},{96,0},{1,33},{33,65},{65,97},{97,1},{2,34}... | collective-permute-start | bytes 1572872 | tf_op jit(solution)/shard_map/ppermute | solution.py:27
  38.7 24.0 %collective-permute-start.12 = (bf16[2,2,512,128]{3,2,1,0:T(8,128)(2,1)}, bf16[2,2,512,128]{3,2,1,0:T(8,128)(2,1)}, u32[]{:S(2)}, u32[]{:S(2)}) collective-permute-start(bf16[2,2,512,128]{3,2,1,0:T(8,128)(2,1)} %get-tuple-element.22.refs_4_), channel_id=1, source_target_pairs={{0,96},{32,0},{64,32},{96,64},{1,97},{33,1},{65,33},{97,65},{2,98}... | collective-permute-start | bytes 1572872 | tf_op jit(solution)/shard_map/ppermute | solution.py:27
  50.1 8.0 %collective-permute-start.2 = (bf16[128,1024]{1,0:T(8,128)(2,1)S(1)}, bf16[128,1024]{1,0:T(8,128)(2,1)S(1)}, u32[]{:S(2)}, u32[]{:S(2)}) collective-permute-start(bf16[128,1024]{1,0:T(8,128)(2,1)S(1)} %get-tuple-element.51), channel_id=1, source_target_pairs={{0,2},{2,0},{1,3},{3,1},{4,6},{6,4},{5,7},{7,5},{8,10},{10,8},{9,1... | collective-permute-start | bytes 786440 | tf_op jit(solution)/shard_map/ppermute | solution.py:32
  55.9 53.5 %copy-start.2 = (bf16[8,1,128,512]{3,2,1,0:T(8,128)(2,1)}, bf16[8,1,128,512]{3,2,1,0:T(8,128)(2,1)S(1)}, u32[]{:S(2)}) copy-start(bf16[8,1,128,512]{3,2,1,0:T(8,128)(2,1)S(1)} %get-tuple-element.44) | copy-start | bytes 3145732
  58.1 29.8 %collective-permute-start.7 = (bf16[1024,512]{1,0:T(8,128)(2,1)S(1)}, bf16[1024,512]{1,0:T(8,128)(2,1)S(1)}, u32[]{:S(2)}, u32[]{:S(2)}) collective-permute-start(bf16[1024,512]{1,0:T(8,128)(2,1)S(1)} %bitcast.25), channel_id=1, source_target_pairs={{0,4},{4,0},{1,5},{5,1},{2,6},{6,2},{3,7},{7,3},{8,12},{12,8},{9,1... | collective-permute-start | bytes 3145736 | tf_op jit(solution)/shard_map/ppermute | solution.py:32
  59.2 29.4 %collective-permute-start.6 = (bf16[1024,512]{1,0:T(8,128)(2,1)}, bf16[1024,512]{1,0:T(8,128)(2,1)S(1)}, u32[]{:S(2)}, u32[]{:S(2)}) collective-permute-start(bf16[1024,512]{1,0:T(8,128)(2,1)} %bitcast.9), channel_id=1, source_target_pairs={{0,1},{1,0},{2,3},{3,2},{4,5},{5,4},{6,7},{7,6},{8,9},{9,8},{10,11... | collective-permute-start | bytes 3145736 | tf_op jit(solution)/shard_map/ppermute | solution.py:32
  59.2 41.0 %collective-permute-start.8 = (bf16[1024,512]{1,0:T(8,128)(2,1)}, bf16[1024,512]{1,0:T(8,128)(2,1)}, u32[]{:S(2)}, u32[]{:S(2)}) collective-permute-start(bf16[1024,512]{1,0:T(8,128)(2,1)} %bitcast.9), channel_id=1, source_target_pairs={{0,5},{1,4},{4,1},{5,0},{2,7},{3,6},{6,3},{7,2},{8,13},{9,12},{12,... | collective-permute-start | bytes 3145736 | tf_op jit(solution)/shard_map/ppermute | solution.py:32
  61.1 16.6 %collective-permute-start.13 = (bf16[2,2,512,128]{3,2,1,0:T(8,128)(2,1)}, bf16[2,2,512,128]{3,2,1,0:T(8,128)(2,1)S(1)}, u32[]{:S(2)}, u32[]{:S(2)}) collective-permute-start(bf16[2,2,512,128]{3,2,1,0:T(8,128)(2,1)} %get-tuple-element.22.refs_4_), channel_id=1, source_target_pairs={{0,64},{32,96},{64,0},{96,32},{1,65},{33,97},{65,1},{97,33},{2,66}... | collective-permute-start | bytes 1572872 | tf_op jit(solution)/shard_map/ppermute | solution.py:27
  62.8 25.1 %collective-permute-start.14 = (bf16[2,2,512,128]{3,2,1,0:T(8,128)(2,1)}, bf16[2,2,512,128]{3,2,1,0:T(8,128)(2,1)S(1)}, u32[]{:S(2)}, u32[]{:S(2)}) collective-permute-start(bf16[2,2,512,128]{3,2,1,0:T(8,128)(2,1)} %get-tuple-element.22.refs_4_), channel_id=1, source_target_pairs={{0,32},{32,64},{64,96},{96,0},{1,33},{33,65},{65,97},{97,1},{2,34}... | collective-permute-start | bytes 1572872 | tf_op jit(solution)/shard_map/ppermute | solution.py:27
  77.6 24.6 %collective-permute-start.25 = (bf16[2,2,512,128]{3,2,1,0:T(8,128)(2,1)}, bf16[2,2,512,128]{3,2,1,0:T(8,128)(2,1)}, u32[]{:S(2)}, u32[]{:S(2)}) collective-permute-start(bf16[2,2,512,128]{3,2,1,0:T(8,128)(2,1)} %copy-done.12), channel_id=1, source_target_pairs={{0,1},{1,0},{2,3},{3,2},{4,5},{5,4},{6,7},{7,6},{8,9},{9,8},{10,11... | collective-permute-start | bytes 1572872 | tf_op jit(solution)/shard_map/ppermute | solution.py:32
  87.8 18.0 %collective-permute-start.15 = (bf16[2,2,2,512,128]{4,3,2,1,0:T(8,128)(2,1)}, bf16[2,2,2,512,128]{4,3,2,1,0:T(8,128)(2,1)}, u32[]{:S(2)}, u32[]{:S(2)}) collective-permute-start(bf16[2,2,2,512,128]{4,3,2,1,0:T(8,128)(2,1)} %get-tuple-element.23), channel_id=1, source_target_pairs={{0,1},{1,0},{2,3},{3,2},{4,5},{5,4},{6,7},{7,6},{8,9},{9,8},{10,11... | collective-permute-start | bytes 3145736 | tf_op jit(solution)/shard_map/ppermute | solution.py:32
  88.6 20.8 %copy-start.3 = (bf16[1024,512]{1,0:T(8,128)(2,1)}, bf16[1024,512]{1,0:T(8,128)(2,1)S(1)}, u32[]{:S(2)}) copy-start(bf16[1024,512]{1,0:T(8,128)(2,1)S(1)} %collective-permute-done.7.refs_2_) | copy-start | bytes 3145732
  88.6 13.7 %collective-permute-start.26 = (bf16[2,2,512,128]{3,2,1,0:T(8,128)(2,1)}, bf16[2,2,512,128]{3,2,1,0:T(8,128)(2,1)}, u32[]{:S(2)}, u32[]{:S(2)}) collective-permute-start(bf16[2,2,512,128]{3,2,1,0:T(8,128)(2,1)} %collective-permute-done.23.refs_6_), channel_id=1, source_target_pairs={{0,1},{1,0},{2,3},{3,2},{4,5},{5,4},{6,7},{7,6},{8,9},{9,8},{10,11... | collective-permute-start | bytes 1572872 | tf_op jit(solution)/shard_map/ppermute | solution.py:32
  88.7 20.8 %copy-start.4 = (bf16[1024,512]{1,0:T(8,128)(2,1)}, bf16[1024,512]{1,0:T(8,128)(2,1)S(1)}, u32[]{:S(2)}) copy-start(bf16[1024,512]{1,0:T(8,128)(2,1)S(1)} %collective-permute-done.6.refs_1_) | copy-start | bytes 3145732
  88.7 16.3 %collective-permute-start.27 = (bf16[2,2,512,128]{3,2,1,0:T(8,128)(2,1)}, bf16[2,2,512,128]{3,2,1,0:T(8,128)(2,1)}, u32[]{:S(2)}, u32[]{:S(2)}) collective-permute-start(bf16[2,2,512,128]{3,2,1,0:T(8,128)(2,1)} %collective-permute-done.24.refs_7_), channel_id=1, source_target_pairs={{0,1},{1,0},{2,3},{3,2},{4,5},{5,4},{6,7},{7,6},{8,9},{9,8},{10,11... | collective-permute-start | bytes 1572872 | tf_op jit(solution)/shard_map/ppermute | solution.py:32
  100.2 20.5 %collective-permute-start.16 = (bf16[2,2,512,128]{3,2,1,0:T(8,128)(2,1)}, bf16[2,2,512,128]{3,2,1,0:T(8,128)(2,1)}, u32[]{:S(2)}, u32[]{:S(2)}) collective-permute-start(bf16[2,2,512,128]{3,2,1,0:T(8,128)(2,1)} %collective-permute-done.12.refs_5_), channel_id=1, source_target_pairs={{0,1},{1,0},{2,3},{3,2},{4,5},{5,4},{6,7},{7,6},{8,9},{9,8},{10,11... | collective-permute-start | bytes 1572872 | tf_op jit(solution)/shard_map/ppermute | solution.py:32
  102.2 20.9 %collective-permute-start.17 = (bf16[2,2,512,128]{3,2,1,0:T(8,128)(2,1)}, bf16[2,2,512,128]{3,2,1,0:T(8,128)(2,1)}, u32[]{:S(2)}, u32[]{:S(2)}) collective-permute-start(bf16[2,2,512,128]{3,2,1,0:T(8,128)(2,1)} %copy-done.11), channel_id=1, source_target_pairs={{0,1},{1,0},{2,3},{3,2},{4,5},{5,4},{6,7},{7,6},{8,9},{9,8},{10,11... | collective-permute-start | bytes 1572872 | tf_op jit(solution)/shard_map/ppermute | solution.py:32
  102.3 31.8 %collective-permute-start.18 = (bf16[2,2,512,128]{3,2,1,0:T(8,128)(2,1)}, bf16[2,2,512,128]{3,2,1,0:T(8,128)(2,1)}, u32[]{:S(2)}, u32[]{:S(2)}) collective-permute-start(bf16[2,2,512,128]{3,2,1,0:T(8,128)(2,1)} %copy-done.13), channel_id=1, source_target_pairs={{0,1},{1,0},{2,3},{3,2},{4,5},{5,4},{6,7},{7,6},{8,9},{9,8},{10,11... | collective-permute-start | bytes 1572872 | tf_op jit(solution)/shard_map/ppermute | solution.py:32
  104.9 43.9 %collective-permute-start.3 = (bf16[2,128,1024]{2,1,0:T(8,128)(2,1)}, bf16[2,128,1024]{2,1,0:T(8,128)(2,1)}, u32[]{:S(2)}, u32[]{:S(2)}) collective-permute-start(bf16[2,128,1024]{2,1,0:T(8,128)(2,1)} %get-tuple-element.48), channel_id=1, source_target_pairs={{0,4},{4,8},{8,12},{12,0},{1,5},{5,9},{9,13},{13,1},{2,6},{6,10},{... | collective-permute-start | bytes 1572872 | tf_op jit(solution)/shard_map/ppermute | solution.py:27
  105.8 46.0 %collective-permute-start.4 = (bf16[2,128,1024]{2,1,0:T(8,128)(2,1)}, bf16[2,128,1024]{2,1,0:T(8,128)(2,1)}, u32[]{:S(2)}, u32[]{:S(2)}) collective-permute-start(bf16[2,128,1024]{2,1,0:T(8,128)(2,1)} %get-tuple-element.48), channel_id=1, source_target_pairs={{0,8},{4,12},{8,0},{12,4},{1,9},{5,13},{9,1},{13,5},{2,10},{6,14},... | collective-permute-start | bytes 1572872 | tf_op jit(solution)/shard_map/ppermute | solution.py:27
  120.7 31.2 %collective-permute-start.5 = (bf16[2,128,1024]{2,1,0:T(8,128)(2,1)}, bf16[2,128,1024]{2,1,0:T(8,128)(2,1)}, u32[]{:S(2)}, u32[]{:S(2)}) collective-permute-start(bf16[2,128,1024]{2,1,0:T(8,128)(2,1)} %get-tuple-element.48), channel_id=1, source_target_pairs={{0,12},{4,0},{8,4},{12,8},{1,13},{5,1},{9,5},{13,9},{2,14},{6,2},{... | collective-permute-start | bytes 1572872 | tf_op jit(solution)/shard_map/ppermute | solution.py:27
  123.1 32.3 %collective-permute-start.28 = (bf16[1024,256]{1,0:T(8,128)(2,1)}, bf16[1024,256]{1,0:T(8,128)(2,1)S(1)}, u32[]{:S(2)}, u32[]{:S(2)}) collective-permute-start(bf16[1024,256]{1,0:T(8,128)(2,1)} %get-tuple-element.30), channel_id=1, source_target_pairs={{0,2},{2,0},{1,3},{3,1},{4,6},{6,4},{5,7},{7,5},{8,10},{10,8},{9,1... | collective-permute-start | bytes 1572872 | tf_op jit(solution)/shard_map/ppermute | solution.py:32
  130.4 33.9 %all-to-all-start = ((bf16[8,128,512]{2,1,0:T(8,128)(2,1)}), bf16[8,128,512]{2,1,0:T(8,128)(2,1)S(1)}, u32[]{:S(2)}, u32[]{:S(2)}) async-start(bf16[8,128,512]{2,1,0:T(8,128)(2,1)} %reshape.167), calls=%async_computation | async-start | bytes 2097152 | tf_op jit(solution)/shard_map/all_to_all | solution.py:22
  134.1 38.7 %collective-permute-start.29 = (bf16[1024,256]{1,0:T(8,128)(2,1)}, bf16[1024,256]{1,0:T(8,128)(2,1)S(1)}, u32[]{:S(2)}, u32[]{:S(2)}) collective-permute-start(bf16[1024,256]{1,0:T(8,128)(2,1)} %get-tuple-element.31), channel_id=1, source_target_pairs={{0,8},{8,0},{1,9},{9,1},{2,10},{10,2},{3,11},{11,3},{4,12},{12,4},... | collective-permute-start | bytes 1572872 | tf_op jit(solution)/shard_map/ppermute | solution.py:32
  148.8 24.0 %collective-permute-start.30 = (bf16[1024,256]{1,0:T(8,128)(2,1)}, bf16[1024,256]{1,0:T(8,128)(2,1)}, u32[]{:S(2)}, u32[]{:S(2)}) collective-permute-start(bf16[1024,256]{1,0:T(8,128)(2,1)} %get-tuple-element.32), channel_id=1, source_target_pairs={{0,10},{2,8},{8,2},{10,0},{1,11},{3,9},{9,3},{11,1},{4,14},{6,12},... | collective-permute-start | bytes 1572872 | tf_op jit(solution)/shard_map/ppermute | solution.py:32
  151.8 24.5 %collective-permute-start.19 = (bf16[1024,256]{1,0:T(8,128)(2,1)}, bf16[1024,256]{1,0:T(8,128)(2,1)}, u32[]{:S(2)}, u32[]{:S(2)}) collective-permute-start(bf16[1024,256]{1,0:T(8,128)(2,1)} %get-tuple-element.25), channel_id=1, source_target_pairs={{0,2},{2,0},{1,3},{3,1},{4,6},{6,4},{5,7},{7,5},{8,10},{10,8},{9,1... | collective-permute-start | bytes 1572872 | tf_op jit(solution)/shard_map/ppermute | solution.py:32
  152.0 41.4 %collective-permute-start.20 = (bf16[1024,256]{1,0:T(8,128)(2,1)}, bf16[1024,256]{1,0:T(8,128)(2,1)}, u32[]{:S(2)}, u32[]{:S(2)}) collective-permute-start(bf16[1024,256]{1,0:T(8,128)(2,1)} %get-tuple-element.26), channel_id=1, source_target_pairs={{0,8},{8,0},{1,9},{9,1},{2,10},{10,2},{3,11},{11,3},{4,12},{12,4},... | collective-permute-start | bytes 1572872 | tf_op jit(solution)/shard_map/ppermute | solution.py:32
  155.4 37.9 %collective-permute-start.21 = (bf16[1024,256]{1,0:T(8,128)(2,1)}, bf16[1024,256]{1,0:T(8,128)(2,1)}, u32[]{:S(2)}, u32[]{:S(2)}) collective-permute-start(bf16[1024,256]{1,0:T(8,128)(2,1)} %get-tuple-element.27), channel_id=1, source_target_pairs={{0,10},{2,8},{8,2},{10,0},{1,11},{3,9},{9,3},{11,1},{4,14},{6,12},... | collective-permute-start | bytes 1572872 | tf_op jit(solution)/shard_map/ppermute | solution.py:32
  164.3 29.1 %copy-start.5 = (bf16[8,128,512]{2,1,0:T(8,128)(2,1)}, bf16[8,128,512]{2,1,0:T(8,128)(2,1)S(1)}, u32[]{:S(2)}) copy-start(bf16[8,128,512]{2,1,0:T(8,128)(2,1)S(1)} %all-to-all-done.refs_9_) | copy-start | bytes 3145732
  172.8 20.5 %copy-start.15 = (bf16[1024,256]{1,0:T(8,128)(2,1)}, bf16[1024,256]{1,0:T(8,128)(2,1)S(1)}, u32[]{:S(2)}) copy-start(bf16[1024,256]{1,0:T(8,128)(2,1)S(1)} %collective-permute-done.29.refs_6_) | copy-start | bytes 1572868
  203.1 2.9 %collective-permute-start.35 = (f32[1024,256]{1,0:T(8,128)}, f32[1024,256]{1,0:T(8,128)S(1)}, u32[]{:S(2)}, u32[]{:S(2)}) collective-permute-start(f32[1024,256]{1,0:T(8,128)} %get-tuple-element.40), channel_id=1, source_target_pairs={{0,1},{1,0},{2,3},{3,2},{4,5},{5,4},{6,7},{7,6},{8,9},{9,8},{10,11... | collective-permute-start | bytes 3145736 | tf_op jit(solution)/shard_map/ppermute | solution.py:32
  205.9 12.8 %copy-start.20 = (bf16[2,128,512]{2,1,0:T(8,128)(2,1)S(1)}, bf16[2,128,512]{2,1,0:T(8,128)(2,1)}, u32[]{:S(2)}) copy-start(bf16[2,128,512]{2,1,0:T(8,128)(2,1)} %get-tuple-element.36) | copy-start | bytes 786436
  208.4 55.8 %all-to-all-start.1 = ((f32[128,8,256]{2,1,0:T(8,128)}), f32[128,8,256]{2,1,0:T(8,128)S(1)}, u32[]{:S(2)}, u32[]{:S(2)}) async-start(f32[128,8,256]{2,1,0:T(8,128)} %add_bitcast_fusion), calls=%async_computation.1 | async-start | bytes 2097152 | tf_op jit(solution)/shard_map/all_to_all | solution.py:22
  215.5 23.7 %collective-permute-start.31 = (bf16[2,128,512]{2,1,0:T(8,128)(2,1)S(1)}, bf16[2,128,512]{2,1,0:T(8,128)(2,1)S(1)}, u32[]{:S(2)}, u32[]{:S(2)}) collective-permute-start(bf16[2,128,512]{2,1,0:T(8,128)(2,1)S(1)} %copy-done.22), channel_id=1, source_target_pairs={{0,12},{4,0},{8,4},{12,8},{1,13},{5,1},{9,5},{13,9},{2,14},{6,2},{... | collective-permute-start | bytes 786440 | tf_op jit(solution)/shard_map/ppermute | solution.py:27
  218.4 20.8 %collective-permute-start.32 = (bf16[2,128,512]{2,1,0:T(8,128)(2,1)S(1)}, bf16[2,128,512]{2,1,0:T(8,128)(2,1)S(1)}, u32[]{:S(2)}, u32[]{:S(2)}) collective-permute-start(bf16[2,128,512]{2,1,0:T(8,128)(2,1)S(1)} %copy-done.21), channel_id=1, source_target_pairs={{0,8},{4,12},{8,0},{12,4},{1,9},{5,13},{9,1},{13,5},{2,10},{6,14},... | collective-permute-start | bytes 786440 | tf_op jit(solution)/shard_map/ppermute | solution.py:27
  218.7 23.9 %collective-permute-start.33 = (bf16[2,128,512]{2,1,0:T(8,128)(2,1)S(1)}, bf16[2,128,512]{2,1,0:T(8,128)(2,1)S(1)}, u32[]{:S(2)}, u32[]{:S(2)}) collective-permute-start(bf16[2,128,512]{2,1,0:T(8,128)(2,1)S(1)} %copy-done.20), channel_id=1, source_target_pairs={{0,4},{4,8},{8,12},{12,0},{1,5},{5,9},{9,13},{13,1},{2,6},{6,10},{... | collective-permute-start | bytes 786440 | tf_op jit(solution)/shard_map/ppermute | solution.py:27
  245.6 15.7 %collective-permute-start.34 = (bf16[4,128,512]{2,1,0:T(8,128)(2,1)}, bf16[4,128,512]{2,1,0:T(8,128)(2,1)}, u32[]{:S(2)}, u32[]{:S(2)}) collective-permute-start(bf16[4,128,512]{2,1,0:T(8,128)(2,1)} %get-tuple-element.38), channel_id=1, source_target_pairs={{0,2},{2,0},{1,3},{3,1},{4,6},{6,4},{5,7},{7,5},{8,10},{10,8},{9,1... | collective-permute-start | bytes 1572872 | tf_op jit(solution)/shard_map/ppermute | solution.py:32
  248.2 18.9 %copy-start.1 = (bf16[1024,1024]{1,0:T(8,128)(2,1)S(1)}, bf16[1024,1024]{1,0:T(8,128)(2,1)}, u32[]{:S(2)}) copy-start(bf16[1024,1024]{1,0:T(8,128)(2,1)} %param.16) | copy-start | bytes 6291460
  (13 other events, 57.5 us)

commit v3 on v2

--- a/solution.py
+++ b/solution.py
@@ -135,84 +135,97 @@
     )(*pieces)
 
 
-def gradient_kernel(place_ref, kept_ref, *refs):
-    parts = refs[: 4 * CHUNKS]
-    weight_ref, resid_ref = refs[4 * CHUNKS : 4 * CHUNKS + 2]
-    targets, (own_ref, give_ref), (target_ref, product_ref) = refs[-8:-4], refs[-4:-2], refs[-2:]
+def target_kernel(place_ref, *refs):
+    parts, resid_ref, targets = refs[: 4 * CHUNKS], refs[4 * CHUNKS], refs[-4:]
     rows, wide = resid_ref.shape[1:]
     width = wide // 2
     piece = width // CHUNKS
     core = place_ref[8]
-    product_ref[...] = jnp.zeros_like(product_ref)
-
-    def step(far, carry):
-        tokens = kept_ref[far].reshape(2 * rows, -1)
-        wanted = []
+    for far in range(4):
         for half in range(2):
             block = place_ref[far * 2 + half]
             start = pl.multiple_of(block * rows, rows)
-            sums = []
             for side in range(2):
+                column = pl.multiple_of((core if side == 0 else 1 - core) * width, width)
+                resid = resid_ref[block, :, pl.ds(column, width)].astype(jnp.float32)
+                sums = []
                 for chunk in range(CHUNKS):
                     total = None
                     for source in range(4):
-                        part = parts[chunk * 4 + source]
                         lanes = slice(side * piece, (side + 1) * piece)
-                        term = part[pl.ds(start, rows), lanes].astype(jnp.float32)
+                        term = parts[chunk * 4 + source][pl.ds(start, rows), lanes]
+                        term = term.astype(jnp.float32)
                         total = term if total is None else total + term
                     sums.append(total)
-            resid = [
-                resid_ref[block, :, pl.ds(pl.multiple_of(column * width, width), width)]
-                for column in (core, 1 - core)
-            ]
-            resid = jnp.concatenate(resid, axis=1).astype(jnp.float32)
-            target = (resid + jnp.concatenate(sums, axis=1)).astype(jnp.bfloat16)
-            target_ref[far, half] = target
-            wanted.append(target)
-        predicted = jnp.dot(tokens, weight_ref[...], preferred_element_type=jnp.float32)
-        error = (predicted - jnp.concatenate(wanted).astype(jnp.float32)).astype(jnp.bfloat16)
-        product_ref[...] += lax.dot_general(
-            tokens, error, (((0,), (0,)), ((), ())), preferred_element_type=jnp.float32
-        )
-        return carry
-
-    lax.fori_loop(0, 4, step, 0)
-    for far in range(4):
-        targets[far][...] = target_ref[far]
-    own_ref[...] = product_ref[:, :width]
-    give_ref[...] = product_ref[:, width:]
-
-
-def gradient_term(places, kept, parts, weight, resid):
-    rows, wide = resid.shape[1:]
-    piece = (2, rows, wide)
-    half = (weight.shape[0], wide // 2)
-    *targets, own, give = pl.pallas_call(
-        gradient_kernel,
-        out_shape=(
-            *[jax.ShapeDtypeStruct(piece, jnp.bfloat16)] * 4,
-            *[jax.ShapeDtypeStruct(half, jnp.float32)] * 2,
-        ),
+                target = (resid + jnp.concatenate(sums, axis=1)).astype(jnp.bfloat16)
+                targets[far][half, :, side * width : (side + 1) * width] = target
+
+
+def whole_spec(x):
+    return pl.BlockSpec(x.shape, lambda i, _: (0,) * len(x.shape))
+
+
+def make_targets(places, parts, resid):
+    piece = jax.ShapeDtypeStruct((2, *resid.shape[1:]), jnp.bfloat16)
+    return pl.pallas_call(
+        target_kernel,
+        out_shape=[piece] * 4,
         grid_spec=pltpu.PrefetchScalarGridSpec(
             num_scalar_prefetch=1,
             grid=(1,),
-            in_specs=[
-                pl.BlockSpec(x.shape, lambda i, _, n=x.ndim: (0,) * n)
-                for x in (kept, *parts, weight, resid)
-            ],
-            out_specs=(
-                *[pl.BlockSpec(piece, lambda i, _: (0, 0, 0))] * 4,
-                *[pl.BlockSpec(half, lambda i, _: (0, 0))] * 2,
-            ),
-            scratch_shapes=[
-                pltpu.VMEM((4, *piece), jnp.bfloat16),
-                pltpu.VMEM(weight.shape, jnp.float32),
-            ],
+            in_specs=[whole_spec(x) for x in (*parts, resid)],
+            out_specs=[whole_spec(piece)] * 4,
         ),
         compiler_params=pltpu.CompilerParams(vmem_limit_bytes=58 * 1024 * 1024),
+        name="make_targets",
+    )(places, *parts, resid)
+
+
+def gradient_kernel(kept_ref, weight_ref, *refs):
+    targets, (own_ref, give_ref), product_ref = refs[:4], refs[4:6], refs[6]
+    rows, wide = targets[0].shape[1:]
+    for far in range(4):
+        tokens = kept_ref[far].reshape(2 * rows, -1)
+        wanted = targets[far][...].reshape(2 * rows, wide).astype(jnp.float32)
+        predicted = jnp.dot(tokens, weight_ref[...], preferred_element_type=jnp.float32)
+        error = (predicted - wanted).astype(jnp.bfloat16)
+        term = lax.dot_general(
+            tokens, error, (((0,), (0,)), ((), ())), preferred_element_type=jnp.float32
+        )
+        if far == 0:
+            product_ref[...] = term
+        elif far < 3:
+            product_ref[...] += term
+        else:
+            term = product_ref[...] + term
+            own_ref[...] = term[:, : wide // 2]
+            give_ref[...] = term[:, wide // 2 :]
+
+
+def gradient_term(kept, weight, targets):
+    half = jax.ShapeDtypeStruct((weight.shape[0], weight.shape[1] // 2), jnp.float32)
+    return pl.pallas_call(
+        gradient_kernel,
+        out_shape=[half] * 2,
+        scratch_shapes=[pltpu.VMEM(weight.shape, jnp.float32)],
+        compiler_params=pltpu.CompilerParams(vmem_limit_bytes=58 * 1024 * 1024),
         name="gradient_term",
-    )(places, kept, *parts, weight, resid)
-    return targets, own, give
+    )(kept, weight, *targets)
+
+
+def regroup_kernel(*refs):
+    for half, out_ref in enumerate(refs[4:]):
+        for far in range(4):
+            out_ref[far] = refs[far][half]
+
+
+def regroup(pieces):
+    shape = (4, *pieces[0].shape[1:])
+    return pl.pallas_call(
+        regroup_kernel,
+        out_shape=[jax.ShapeDtypeStruct(shape, pieces[0].dtype)] * 2,
+        name="regroup",
+    )(*pieces)
 
 
 def place_kernel(column_ref, *refs):
@@ -420,7 +433,8 @@
             axes = ("zh",) * (far // 2) + ("xh",) * (far % 2)
             part = sent[chunk][far]
             parts.append(flip(part, *axes) if axes else part)
-    targets, product, give = gradient_term(places, kept, parts, weight, resid_cols)
+    targets = make_targets(places, parts, resid_cols)
+    product, give = gradient_term(kept, weight, targets)
     product = product + flip(give, "core")
     grad_pieces = exchange(product.reshape(everyone, student_width // everyone, half_width), AXES)
     head_grad = sum_rows([grad_pieces], out_width, 1.0 / row_tokens)

time: 268 us -> 279 us (1.041)
  waiting for transfers between devices: 107 us -> 117 us
    ppermute x22, waiting for transfers between devices: 60.3 us -> 72.1 us  [flip(): return lax.ppermute(array, axes, [(i, last - i) for i in range(last + 1)])]
    pallas_call x1 -> x2, Pallas kernels: 9.71 us -> 11 us  [the longest x1 6.35 us: gradient_term(): pl.pallas_call(gradient_kernel, out_shape=[half] * 2, scratch_shapes=[plt...]
  transfers between devices with their start and end apart: 38 -> 38, of which waited for: 12 -> 13; matrix products, arithmetic and copies ran while one was open for 14% -> 13% of each run, Pallas kernels for 14% -> 14%
where the time goes in v3:
time: 279 us; the launch traced here: 278 us
  waiting for transfers between devices  117 us (42%)
  starting transfers between devices  66.8 us (24%)
  Pallas kernels  51.2 us (18%)
  matrix products  15.4 us (6%)
  local copies, waits for them, and re-layouts  13.5 us (5%)
  other arithmetic  13.3 us (5%)
    ppermute x22, waiting for transfers between devices, flip(): return lax.ppermute(array, axes, [(i, last - i) for i in range(last + 1)])  72.1 us
    ppermute x14, waiting for transfers between devices, shift(): lax.ppermute(array, axes, [(i, (i + step) % size) for i in range(size)])  44.6 us
    ppermute x22, starting transfers between devices, flip(): return lax.ppermute(array, axes, [(i, last - i) for i in range(last + 1)])  29.2 us
    ppermute x14, starting transfers between devices, shift(): lax.ppermute(array, axes, [(i, (i + step) % size) for i in range(size)])  25.6 us
    pallas_call x2, Pallas kernels, teacher_partials(): pl.pallas_call(partial_kernel, out_shape=[jax.ShapeDtypeStruct((tokens, 2...  22.5 us
    all_to_all x2, starting transfers between devices, exchange(): return lax.all_to_all(blocks, axes, 0, 0, tiled=True)  12 us
    pallas_call x1, Pallas kernels, attend(): pl.pallas_call(attend_kernel, out_shape=jax.ShapeDtypeStruct(queries.shap...  7.72 us
    pallas_call x1, Pallas kernels, gradient_term(): pl.pallas_call(gradient_kernel, out_shape=[half] * 2, scratch_shapes=[plt...  6.35 us
  transfers between devices with their start and end apart: 38, of which 13 were waited for; matrix products, arithmetic and copies ran while one was open for 13% of the time, Pallas kernels for 14%

profile of v3, /device:TPU:0, one launch (start us, length us, event | category | flops | bytes accessed | tf_op | source)
XLA Modules:
  0.0 277.8 jit_solution(17355666535199595731)
XLA Ops:
  1.9 2.1 collective-permute-start.3
  5.1 5.1 %collective-permute-start.30 = (bf16[128,1024]{1,0:T(8,128)(2,1)}, bf16[128,1024]{1,0:T(8,128)(2,1)S(1)}, u32[]{:S(2)}, u32[]{:S(2)}) collective-permute-start(bf16[128,1024]{1,0:T(8,128)(2,1)} %param.13), channel_id=1, source_target_pairs={{0,15},{1,0},{2,1},{3,2},{4,3},{5,4},{6,5},{7,6},{8,7},{9,8},{10,9... | collective-permute-start | bytes 786440 | tf_op jit(solution)/shard_map/ppermute | solution.py:27
  14.1 4.0 %collective-permute-done.3.refs_1_ = bf16[512,256]{1,0:T(8,128)(2,1)} collective-permute-done((bf16[512,256]{1,0:T(8,128)(2,1)S(1)}, bf16[512,256]{1,0:T(8,128)(2,1)}, u32[]{:S(2)}, u32[]{:S(2)}) %collective-permute-start.3) | collective-permute-done | bytes 262176 | tf_op jit(solution)/shard_map/ppermute | solution.py:32
  18.0 5.0 %collective-permute-done.4.refs_2_ = bf16[512,256]{1,0:T(8,128)(2,1)} collective-permute-done((bf16[512,256]{1,0:T(8,128)(2,1)S(1)}, bf16[512,256]{1,0:T(8,128)(2,1)}, u32[]{:S(2)}, u32[]{:S(2)}) %collective-permute-start.4) | collective-permute-done | bytes 262176 | tf_op jit(solution)/shard_map/ppermute | solution.py:32
  23.0 2.9 %pack.1 = (bf16[2,2,2,512,128]{4,3,2,1,0:T(8,128)(2,1)}, bf16[2,2,512,128]{3,2,1,0:T(8,128)(2,1)}, bf16[2,2,512,128]{3,2,1,0:T(8,128)(2,1)}) custom-call(bf16[512,256]{1,0:T(8,128)(2,1)} %copy-done.9, bf16[512,256]{1,0:T(8,128)(2,1)} %collective-permute-done.3.refs_1_, bf16[512,256]{1,0:T(8,128)(2,1)} %collective-permute-done.4.refs_2_, ...), custom_call_target="tpu_custom_call" | custom-call | tf_op jit(solution)/shard_map/pack/pallas_call | solution.py:113
  25.9 3.0 %collective-permute-start.6 = (bf16[2,2,512,128]{3,2,1,0:T(8,128)(2,1)}, bf16[2,2,512,128]{3,2,1,0:T(8,128)(2,1)S(1)}, u32[]{:S(2)}, u32[]{:S(2)}) collective-permute-start(bf16[2,2,512,128]{3,2,1,0:T(8,128)(2,1)} %get-tuple-element.22.refs_4_), channel_id=1, source_target_pairs={{0,96},{32,0},{64,32},{96,64},{1,97},{33,1},{65,33},{97,65},{2,98}... | collective-permute-start | bytes 1572872 | tf_op jit(solution)/shard_map/ppermute | solution.py:27
  31.0 2.7 fusion.10.query_ref
  33.7 5.1 %fusion.2.keyval_ref = bf16[384,2048]{1,0:T(8,128)(2,1)} fusion(bf16[384,1024]{1,0:T(8,128)(2,1)S(1)} %fusion.9, bf16[1024,3072]{1,0:T(8,128)(2,1)} %param.15), kind=kOutput, calls=%fused_computation.2 | convolution fusion | flops 1611399168 | bytes 6553600 | tf_op jit(solution)/shard_map/dot_general | solution.py:331
  38.9 2.3 collective-permute-start.16
  41.1 7.7 %attend_heads.1 = bf16[128,1024]{1,0:T(8,128)(2,1)} custom-call(bf16[128,1024]{1,0:T(8,128)(2,1)} %fusion.10.query_ref, bf16[384,2048]{1,0:T(8,128)(2,1)} %fusion.2.keyval_ref, f32[128,384]{1,0:T(8,128)} %fusion.16.allowed_ref), custom_call_target="tpu_custom_call" | custom-call | tf_op jit(solution)/shard_map/attend_heads/pallas_call | solution.py:320
  50.3 3.1 %collective-permute-start.31 = (bf16[128,1024]{1,0:T(8,128)(2,1)S(1)}, bf16[128,1024]{1,0:T(8,128)(2,1)S(1)}, u32[]{:S(2)}, u32[]{:S(2)}) collective-permute-start(bf16[128,1024]{1,0:T(8,128)(2,1)S(1)} %get-tuple-element.51), channel_id=1, source_target_pairs={{0,2},{2,0},{1,3},{3,1},{4,6},{6,4},{5,7},{7,5},{8,10},{10,8},{9,1... | collective-permute-start | bytes 786440 | tf_op jit(solution)/shard_map/ppermute | solution.py:32
  53.4 4.8 %collective-permute-done.31 = bf16[128,1024]{1,0:T(8,128)(2,1)S(1)} collective-permute-done((bf16[128,1024]{1,0:T(8,128)(2,1)S(1)}, bf16[128,1024]{1,0:T(8,128)(2,1)S(1)}, u32[]{:S(2)}, u32[]{:S(2)}) %collective-permute-start.31) | collective-permute-done | bytes 262176 | tf_op jit(solution)/shard_map/ppermute | solution.py:32
  58.2 1.7 collective-permute-start.17
  59.9 2.7 constant_dynamic-slice_fusion.4
  63.5 1.6 collective-permute-start.1
  65.1 8.1 %collective-permute-done.16.refs_5_ = bf16[2,2,512,128]{3,2,1,0:T(8,128)(2,1)} collective-permute-done((bf16[2,2,512,128]{3,2,1,0:T(8,128)(2,1)}, bf16[2,2,512,128]{3,2,1,0:T(8,128)(2,1)}, u32[]{:S(2)}, u32[]{:S(2)}) %collective-permute-start.16) | collective-permute-done | bytes 524320 | tf_op jit(solution)/shard_map/ppermute | solution.py:27
  73.3 2.1 collective-permute-start.18
  75.4 14.5 %collective-permute-done.18.refs_7_ = bf16[2,2,512,128]{3,2,1,0:T(8,128)(2,1)} collective-permute-done((bf16[2,2,512,128]{3,2,1,0:T(8,128)(2,1)}, bf16[2,2,512,128]{3,2,1,0:T(8,128)(2,1)}, u32[]{:S(2)}, u32[]{:S(2)}) %collective-permute-start.18) | collective-permute-done | bytes 524320 | tf_op jit(solution)/shard_map/ppermute | solution.py:27
  90.7 19.4 %collective-permute-done.2.refs_3_ = bf16[1024,512]{1,0:T(8,128)(2,1)} collective-permute-done((bf16[1024,512]{1,0:T(8,128)(2,1)}, bf16[1024,512]{1,0:T(8,128)(2,1)}, u32[]{:S(2)}, u32[]{:S(2)}) %collective-permute-start.2) | collective-permute-done | bytes 1048608 | tf_op jit(solution)/shard_map/ppermute | solution.py:32
  111.3 2.1 fusion.26
  113.4 4.3 %collective-permute-start.34 = (bf16[2,128,1024]{2,1,0:T(8,128)(2,1)}, bf16[2,128,1024]{2,1,0:T(8,128)(2,1)}, u32[]{:S(2)}, u32[]{:S(2)}) collective-permute-start(bf16[2,128,1024]{2,1,0:T(8,128)(2,1)} %get-tuple-element.46), channel_id=1, source_target_pairs={{0,12},{4,0},{8,4},{12,8},{1,13},{5,1},{9,5},{13,9},{2,14},{6,2},{... | collective-permute-start | bytes 1572872 | tf_op jit(solution)/shard_map/ppermute | solution.py:27
  118.3 11.2 %teacher_partials.2 = (bf16[1024,256]{1,0:T(8,128)(2,1)}, bf16[1024,256]{1,0:T(8,128)(2,1)}, bf16[1024,256]{1,0:T(8,128)(2,1)}, bf16[1024,256]{1,0:T(8,128)(2,1)}) custom-call(s32[8]{0:T(128)} %add.294.slot_ref, bf16[1024,512]{1,0:T(8,128)(2,1)} %bitcast.26, bf16[1024,512]{1,0:T(8,128)(2,1)} %copy-done.3, bf16[1024,512]{1,0:T(8,128)(2,1)} %copy-done.4, ...), custom_call_target="tpu_custom_call" | custom-call | tf_op jit(solution)/shard_map/teacher_partials/pallas_call | solution.py:76
  130.7 3.2 %collective-permute-start.13 = (bf16[1024,256]{1,0:T(8,128)(2,1)}, bf16[1024,256]{1,0:T(8,128)(2,1)S(1)}, u32[]{:S(2)}, u32[]{:S(2)}) collective-permute-start(bf16[1024,256]{1,0:T(8,128)(2,1)} %get-tuple-element.25), channel_id=1, source_target_pairs={{0,2},{2,0},{1,3},{3,1},{4,6},{6,4},{5,7},{7,5},{8,10},{10,8},{9,1... | collective-permute-start | bytes 1572872 | tf_op jit(solution)/shard_map/ppermute | solution.py:32
  134.0 1.8 reshape.166
  138.1 3.8 %all-to-all-start = ((bf16[8,128,512]{2,1,0:T(8,128)(2,1)}), bf16[8,128,512]{2,1,0:T(8,128)(2,1)S(1)}, u32[]{:S(2)}, u32[]{:S(2)}) async-start(bf16[8,128,512]{2,1,0:T(8,128)(2,1)} %reshape.167), calls=%async_computation | async-start | bytes 2097152 | tf_op jit(solution)/shard_map/all_to_all | solution.py:22
  142.1 3.5 %collective-permute-start.14 = (bf16[1024,256]{1,0:T(8,128)(2,1)}, bf16[1024,256]{1,0:T(8,128)(2,1)}, u32[]{:S(2)}, u32[]{:S(2)}) collective-permute-start(bf16[1024,256]{1,0:T(8,128)(2,1)} %get-tuple-element.26), channel_id=1, source_target_pairs={{0,8},{8,0},{1,9},{9,1},{2,10},{10,2},{3,11},{11,3},{4,12},{12,4},... | collective-permute-start | bytes 1572872 | tf_op jit(solution)/shard_map/ppermute | solution.py:32
  145.6 11.3 %teacher_partials.3 = (bf16[1024,256]{1,0:T(8,128)(2,1)}, bf16[1024,256]{1,0:T(8,128)(2,1)}, bf16[1024,256]{1,0:T(8,128)(2,1)}, bf16[1024,256]{1,0:T(8,128)(2,1)}) custom-call(s32[8]{0:T(128)} %add.294.slot_ref, bf16[1024,512]{1,0:T(8,128)(2,1)} %bitcast.27, bf16[1024,512]{1,0:T(8,128)(2,1)} %copy-done.3, bf16[1024,512]{1,0:T(8,128)(2,1)} %copy-done.4, ...), custom_call_target="tpu_custom_call" | custom-call | tf_op jit(solution)/shard_map/teacher_partials/pallas_call | solution.py:76
  156.9 3.0 %collective-permute-start.15 = (bf16[1024,256]{1,0:T(8,128)(2,1)}, bf16[1024,256]{1,0:T(8,128)(2,1)}, u32[]{:S(2)}, u32[]{:S(2)}) collective-permute-start(bf16[1024,256]{1,0:T(8,128)(2,1)} %get-tuple-element.27), channel_id=1, source_target_pairs={{0,10},{2,8},{8,2},{10,0},{1,11},{3,9},{9,3},{11,1},{4,14},{6,12},... | collective-permute-start | bytes 1572872 | tf_op jit(solution)/shard_map/ppermute | solution.py:32
  160.0 3.4 %collective-permute-start.23 = (bf16[1024,256]{1,0:T(8,128)(2,1)}, bf16[1024,256]{1,0:T(8,128)(2,1)}, u32[]{:S(2)}, u32[]{:S(2)}) collective-permute-start(bf16[1024,256]{1,0:T(8,128)(2,1)} %get-tuple-element.31), channel_id=1, source_target_pairs={{0,8},{8,0},{1,9},{9,1},{2,10},{10,2},{3,11},{11,3},{4,12},{12,4},... | collective-permute-start | bytes 1572872 | tf_op jit(solution)/shard_map/ppermute | solution.py:32
  163.5 3.0 %collective-permute-start.24 = (bf16[1024,256]{1,0:T(8,128)(2,1)}, bf16[1024,256]{1,0:T(8,128)(2,1)}, u32[]{:S(2)}, u32[]{:S(2)}) collective-permute-start(bf16[1024,256]{1,0:T(8,128)(2,1)} %get-tuple-element.32), channel_id=1, source_target_pairs={{0,10},{2,8},{8,2},{10,0},{1,11},{3,9},{9,3},{11,1},{4,14},{6,12},... | collective-permute-start | bytes 1572872 | tf_op jit(solution)/shard_map/ppermute | solution.py:32
  169.5 2.8 %pad_maximum_fusion.kept_ref = bf16[4,2,128,1024]{3,2,1,0:T(8,128)(2,1)} fusion(bf16[1,2,128,1024]{3,2,1,0:T(8,128)(2,1)} %bitcast.10, bf16[1,2,128,1024]{3,2,1,0:T(8,128)(2,1)} %bitcast.9, bf16[1,2,128,1024]{3,2,1,0:T(8,128)(2,1)S(1)} %bitcast.31, bf16[1,2,128,1024]{3,2,1,0:T(8,128)(2,1)S(1)} %copy-done.8), kind=kLoop, calls=%fused_computation.3 | loop fusion | flops 3145728 | bytes 4194304 | tf_op jit(solution)/shard_map/stack | solution.py:405
  172.3 8.7 %collective-permute-done.14.refs_2_ = bf16[1024,256]{1,0:T(8,128)(2,1)} collective-permute-done((bf16[1024,256]{1,0:T(8,128)(2,1)}, bf16[1024,256]{1,0:T(8,128)(2,1)}, u32[]{:S(2)}, u32[]{:S(2)}) %collective-permute-start.14) | collective-permute-done | bytes 524320 | tf_op jit(solution)/shard_map/ppermute | solution.py:32
  181.0 3.4 %collective-permute-done.22.refs_5_ = bf16[1024,256]{1,0:T(8,128)(2,1)} collective-permute-done((bf16[1024,256]{1,0:T(8,128)(2,1)}, bf16[1024,256]{1,0:T(8,128)(2,1)}, u32[]{:S(2)}, u32[]{:S(2)}) %collective-permute-start.22) | collective-permute-done | bytes 524320 | tf_op jit(solution)/shard_map/ppermute | solution.py:32
  184.4 17.0 %collective-permute-done.23.refs_6_ = bf16[1024,256]{1,0:T(8,128)(2,1)} collective-permute-done((bf16[1024,256]{1,0:T(8,128)(2,1)}, bf16[1024,256]{1,0:T(8,128)(2,1)}, u32[]{:S(2)}, u32[]{:S(2)}) %collective-permute-start.23) | collective-permute-done | bytes 524320 | tf_op jit(solution)/shard_map/ppermute | solution.py:32
  201.4 4.7 %make_targets.1 = (bf16[2,128,512]{2,1,0:T(8,128)(2,1)}, bf16[2,128,512]{2,1,0:T(8,128)(2,1)}, bf16[2,128,512]{2,1,0:T(8,128)(2,1)}, bf16[2,128,512]{2,1,0:T(8,128)(2,1)}) custom-call(s32[9]{0:T(128)} %pad_add_fusion.place_ref, bf16[1024,256]{1,0:T(8,128)(2,1)} %get-tuple-element.24.refs_0_, bf16[1024,256]{1,0:T(8,128)(2,1)} %copy-done.12, ...), custom_call_target="tpu_custom_call" | custom-call | tf_op jit(solution)/shard_map/make_targets/pallas_call | solution.py:170
  206.1 6.4 %gradient_term.1 = (f32[1024,256]{1,0:T(8,128)}, f32[1024,256]{1,0:T(8,128)}) custom-call(bf16[4,2,128,1024]{3,2,1,0:T(8,128)(2,1)} %pad_maximum_fusion.kept_ref, bf16[1024,512]{1,0:T(8,128)(2,1)} %pad_maximum_fusion.1.weight_ref, bf16[2,128,512]{2,1,0:T(8,128)(2,1)} %get-tuple-element.33.refs_0_, bf16[2,128,512]{2,1,0:T(8,128)(2,1)} %get-tuple-element.34.refs_1_, ...), custom_call_target="tpu_custom_call" | custom-call | tf_op jit(solution)/shard_map/gradient_term/pallas_call | solution.py:207
  212.4 2.9 %collective-permute-done.35 = f32[1024,256]{1,0:T(8,128)S(1)} collective-permute-done((f32[1024,256]{1,0:T(8,128)}, f32[1024,256]{1,0:T(8,128)S(1)}, u32[]{:S(2)}, u32[]{:S(2)}) %collective-permute-start.35) | collective-permute-done | bytes 1048608 | tf_op jit(solution)/shard_map/ppermute | solution.py:32
  215.3 2.5 add_bitcast_fusion
  217.8 8.3 %all-to-all-start.1 = ((f32[128,8,256]{2,1,0:T(8,128)}), f32[128,8,256]{2,1,0:T(8,128)S(1)}, u32[]{:S(2)}, u32[]{:S(2)}) async-start(f32[128,8,256]{2,1,0:T(8,128)} %add_bitcast_fusion), calls=%async_computation.1 | async-start | bytes 2097152 | tf_op jit(solution)/shard_map/all_to_all | solution.py:22
  226.1 2.9 %collective-permute-start.25 = (bf16[2,128,512]{2,1,0:T(8,128)(2,1)S(1)}, bf16[2,128,512]{2,1,0:T(8,128)(2,1)S(1)}, u32[]{:S(2)}, u32[]{:S(2)}) collective-permute-start(bf16[2,128,512]{2,1,0:T(8,128)(2,1)S(1)} %copy-done.15), channel_id=1, source_target_pairs={{0,12},{4,0},{8,4},{12,8},{1,13},{5,1},{9,5},{13,9},{2,14},{6,2},{... | collective-permute-start | bytes 786440 | tf_op jit(solution)/shard_map/ppermute | solution.py:27
  231.3 18.5 %collective-permute-done.25.refs_1_ = bf16[2,128,512]{2,1,0:T(8,128)(2,1)S(1)} collective-permute-done((bf16[2,128,512]{2,1,0:T(8,128)(2,1)S(1)}, bf16[2,128,512]{2,1,0:T(8,128)(2,1)S(1)}, u32[]{:S(2)}, u32[]{:S(2)}) %collective-permute-start.25) | collective-permute-done | bytes 262176 | tf_op jit(solution)/shard_map/ppermute | solution.py:27
  249.7 3.5 %collective-permute-done.27.refs_3_ = bf16[2,128,512]{2,1,0:T(8,128)(2,1)S(1)} collective-permute-done((bf16[2,128,512]{2,1,0:T(8,128)(2,1)S(1)}, bf16[2,128,512]{2,1,0:T(8,128)(2,1)S(1)}, u32[]{:S(2)}, u32[]{:S(2)}) %collective-permute-start.27) | collective-permute-done | bytes 262176 | tf_op jit(solution)/shard_map/ppermute | solution.py:27
  254.0 2.2 regroup.1
  256.1 2.7 collective-permute-start.28
  258.8 6.1 %fusion.27 = f32[128,4096]{1,0:T(8,128)} fusion(bf16[128,1024]{1,0:T(8,128)(2,1)S(1)} %get-tuple-element.52, bf16[1024,4096]{1,0:T(8,128)(2,1)} %param.17), kind=kOutput, calls=%fused_computation.72 | convolution fusion | flops 1073741824 | bytes 10747904 | tf_op jit(solution)/shard_map/dot_general | solution.py:401
  264.9 6.9 %collective-permute-done.28.refs_1_ = bf16[4,128,512]{2,1,0:T(8,128)(2,1)} collective-permute-done((bf16[4,128,512]{2,1,0:T(8,128)(2,1)}, bf16[4,128,512]{2,1,0:T(8,128)(2,1)}, u32[]{:S(2)}, u32[]{:S(2)}) %collective-permute-start.28) | collective-permute-done | bytes 524320 | tf_op jit(solution)/shard_map/ppermute | solution.py:32
  271.9 2.9 %place_columns.1 = bf16[128,4096]{1,0:T(8,128)(2,1)} custom-call(s32[16]{0:T(128)} %add_multiply_fusion.column_ref, bf16[4,128,512]{2,1,0:T(8,128)(2,1)} %get-tuple-element.37.refs_0_, bf16[4,128,512]{2,1,0:T(8,128)(2,1)} %collective-permute-done.28.refs_1_), custom_call_target="tpu_custom_call" | custom-call | tf_op jit(solution)/shard_map/place_columns/pallas_call | solution.py:243
  275.8 1.9 sum_rows.1
  (115 shorter events, 24.1 us)
Async XLA Ops:
  0.6 48.2 %copy-start = (bf16[1024,1024]{1,0:T(8,128)(2,1)S(1)}, bf16[1024,1024]{1,0:T(8,128)(2,1)}, u32[]{:S(2)}) copy-start(bf16[1024,1024]{1,0:T(8,128)(2,1)} %param.16) | copy-start | bytes 6291460
  0.6 29.8 %copy-start.7 = (bf16[128,1024]{1,0:T(8,128)(2,1)S(1)}, bf16[128,1024]{1,0:T(8,128)(2,1)}, u32[]{:S(2)}) copy-start(bf16[128,1024]{1,0:T(8,128)(2,1)} %param.13) | copy-start | bytes 786436
  1.9 21.1 %copy-start.9 = (bf16[512,256]{1,0:T(8,128)(2,1)}, bf16[512,256]{1,0:T(8,128)(2,1)S(1)}, u32[]{:S(2)}) copy-start(bf16[512,256]{1,0:T(8,128)(2,1)S(1)} %get-tuple-element.48.refs_0_) | copy-start | bytes 786436
  1.9 16.1 %collective-permute-start.3 = (bf16[512,256]{1,0:T(8,128)(2,1)S(1)}, bf16[512,256]{1,0:T(8,128)(2,1)}, u32[]{:S(2)}, u32[]{:S(2)}) collective-permute-start(bf16[512,256]{1,0:T(8,128)(2,1)S(1)} %get-tuple-element.47), channel_id=1, source_target_pairs={{0,4},{4,0},{1,5},{5,1},{2,6},{6,2},{3,7},{7,3},{8,12},{12,8},{9,1... | collective-permute-start | bytes 786440 | tf_op jit(solution)/shard_map/ppermute | solution.py:32
  4.0 19.0 %collective-permute-start.5 = (bf16[512,256]{1,0:T(8,128)(2,1)S(1)}, bf16[512,256]{1,0:T(8,128)(2,1)}, u32[]{:S(2)}, u32[]{:S(2)}) collective-permute-start(bf16[512,256]{1,0:T(8,128)(2,1)S(1)} %get-tuple-element.47), channel_id=1, source_target_pairs={{0,20},{4,16},{16,4},{20,0},{1,21},{5,17},{17,5},{21,1},{2,22},{6,... | collective-permute-start | bytes 786440 | tf_op jit(solution)/shard_map/ppermute | solution.py:32
  5.1 25.4 %collective-permute-start.30 = (bf16[128,1024]{1,0:T(8,128)(2,1)}, bf16[128,1024]{1,0:T(8,128)(2,1)S(1)}, u32[]{:S(2)}, u32[]{:S(2)}) collective-permute-start(bf16[128,1024]{1,0:T(8,128)(2,1)} %param.13), channel_id=1, source_target_pairs={{0,15},{1,0},{2,1},{3,2},{4,3},{5,4},{6,5},{7,6},{8,7},{9,8},{10,9... | collective-permute-start | bytes 786440 | tf_op jit(solution)/shard_map/ppermute | solution.py:27
  10.1 20.3 %collective-permute-start.29 = (bf16[128,1024]{1,0:T(8,128)(2,1)}, bf16[128,1024]{1,0:T(8,128)(2,1)S(1)}, u32[]{:S(2)}, u32[]{:S(2)}) collective-permute-start(bf16[128,1024]{1,0:T(8,128)(2,1)} %param.13), channel_id=1, source_target_pairs={{0,1},{1,2},{2,3},{3,4},{4,5},{5,6},{6,7},{7,8},{8,9},{9,10},{10,1... | collective-permute-start | bytes 786440 | tf_op jit(solution)/shard_map/ppermute | solution.py:27
  10.1 12.8 %collective-permute-start.4 = (bf16[512,256]{1,0:T(8,128)(2,1)S(1)}, bf16[512,256]{1,0:T(8,128)(2,1)}, u32[]{:S(2)}, u32[]{:S(2)}) collective-permute-start(bf16[512,256]{1,0:T(8,128)(2,1)S(1)} %get-tuple-element.48.refs_0_), channel_id=1, source_target_pairs={{0,16},{16,0},{1,17},{17,1},{2,18},{18,2},{3,19},{19,3},{4,20},{20... | collective-permute-start | bytes 786440 | tf_op jit(solution)/shard_map/ppermute | solution.py:32
  25.9 36.8 %collective-permute-start.6 = (bf16[2,2,512,128]{3,2,1,0:T(8,128)(2,1)}, bf16[2,2,512,128]{3,2,1,0:T(8,128)(2,1)S(1)}, u32[]{:S(2)}, u32[]{:S(2)}) collective-permute-start(bf16[2,2,512,128]{3,2,1,0:T(8,128)(2,1)} %get-tuple-element.22.refs_4_), channel_id=1, source_target_pairs={{0,96},{32,0},{64,32},{96,64},{1,97},{33,1},{65,33},{97,65},{2,98}... | collective-permute-start | bytes 1572872 | tf_op jit(solution)/shard_map/ppermute | solution.py:27
  28.9 33.9 %collective-permute-start.7 = (bf16[2,2,512,128]{3,2,1,0:T(8,128)(2,1)}, bf16[2,2,512,128]{3,2,1,0:T(8,128)(2,1)}, u32[]{:S(2)}, u32[]{:S(2)}) collective-permute-start(bf16[2,2,512,128]{3,2,1,0:T(8,128)(2,1)} %get-tuple-element.22.refs_4_), channel_id=1, source_target_pairs={{0,64},{32,96},{64,0},{96,32},{1,65},{33,97},{65,1},{97,33},{2,66}... | collective-permute-start | bytes 1572872 | tf_op jit(solution)/shard_map/ppermute | solution.py:27
  29.5 35.6 %collective-permute-start.8 = (bf16[2,2,512,128]{3,2,1,0:T(8,128)(2,1)}, bf16[2,2,512,128]{3,2,1,0:T(8,128)(2,1)}, u32[]{:S(2)}, u32[]{:S(2)}) collective-permute-start(bf16[2,2,512,128]{3,2,1,0:T(8,128)(2,1)} %get-tuple-element.22.refs_4_), channel_id=1, source_target_pairs={{0,32},{32,64},{64,96},{96,0},{1,33},{33,65},{65,97},{97,1},{2,34}... | collective-permute-start | bytes 1572872 | tf_op jit(solution)/shard_map/ppermute | solution.py:27
  38.9 34.4 %collective-permute-start.16 = (bf16[2,2,512,128]{3,2,1,0:T(8,128)(2,1)}, bf16[2,2,512,128]{3,2,1,0:T(8,128)(2,1)}, u32[]{:S(2)}, u32[]{:S(2)}) collective-permute-start(bf16[2,2,512,128]{3,2,1,0:T(8,128)(2,1)} %get-tuple-element.28.refs_4_), channel_id=1, source_target_pairs={{0,96},{32,0},{64,32},{96,64},{1,97},{33,1},{65,33},{97,65},{2,98}... | collective-permute-start | bytes 1572872 | tf_op jit(solution)/shard_map/ppermute | solution.py:27
  50.3 8.0 %collective-permute-start.31 = (bf16[128,1024]{1,0:T(8,128)(2,1)S(1)}, bf16[128,1024]{1,0:T(8,128)(2,1)S(1)}, u32[]{:S(2)}, u32[]{:S(2)}) collective-permute-start(bf16[128,1024]{1,0:T(8,128)(2,1)S(1)} %get-tuple-element.51), channel_id=1, source_target_pairs={{0,2},{2,0},{1,3},{3,1},{4,6},{6,4},{5,7},{7,5},{8,10},{10,8},{9,1... | collective-permute-start | bytes 786440 | tf_op jit(solution)/shard_map/ppermute | solution.py:32
  58.2 15.0 %collective-permute-start.17 = (bf16[2,2,512,128]{3,2,1,0:T(8,128)(2,1)}, bf16[2,2,512,128]{3,2,1,0:T(8,128)(2,1)}, u32[]{:S(2)}, u32[]{:S(2)}) collective-permute-start(bf16[2,2,512,128]{3,2,1,0:T(8,128)(2,1)} %get-tuple-element.28.refs_4_), channel_id=1, source_target_pairs={{0,64},{32,96},{64,0},{96,32},{1,65},{33,97},{65,1},{97,33},{2,66}... | collective-permute-start | bytes 1572872 | tf_op jit(solution)/shard_map/ppermute | solution.py:27
  62.6 55.6 %copy-start.2 = (bf16[8,1,128,512]{3,2,1,0:T(8,128)(2,1)}, bf16[8,1,128,512]{3,2,1,0:T(8,128)(2,1)S(1)}, u32[]{:S(2)}) copy-start(bf16[8,1,128,512]{3,2,1,0:T(8,128)(2,1)S(1)} %get-tuple-element.44) | copy-start | bytes 3145732
  62.7 27.2 %collective-permute-start = (bf16[1024,512]{1,0:T(8,128)(2,1)}, bf16[1024,512]{1,0:T(8,128)(2,1)S(1)}, u32[]{:S(2)}, u32[]{:S(2)}) collective-permute-start(bf16[1024,512]{1,0:T(8,128)(2,1)} %bitcast.3), channel_id=1, source_target_pairs={{0,1},{1,0},{2,3},{3,2},{4,5},{5,4},{6,7},{7,6},{8,9},{9,8},{10,11... | collective-permute-start | bytes 3145736 | tf_op jit(solution)/shard_map/ppermute | solution.py:32
  63.5 26.9 %collective-permute-start.1 = (bf16[1024,512]{1,0:T(8,128)(2,1)S(1)}, bf16[1024,512]{1,0:T(8,128)(2,1)S(1)}, u32[]{:S(2)}, u32[]{:S(2)}) collective-permute-start(bf16[1024,512]{1,0:T(8,128)(2,1)S(1)} %bitcast.25), channel_id=1, source_target_pairs={{0,4},{4,0},{1,5},{5,1},{2,6},{6,2},{3,7},{7,3},{8,12},{12,8},{9,1... | collective-permute-start | bytes 3145736 | tf_op jit(solution)/shard_map/ppermute | solution.py:32
  65.1 44.9 %collective-permute-start.2 = (bf16[1024,512]{1,0:T(8,128)(2,1)}, bf16[1024,512]{1,0:T(8,128)(2,1)}, u32[]{:S(2)}, u32[]{:S(2)}) collective-permute-start(bf16[1024,512]{1,0:T(8,128)(2,1)} %bitcast.3), channel_id=1, source_target_pairs={{0,5},{1,4},{4,1},{5,0},{2,7},{3,6},{6,3},{7,2},{8,13},{9,12},{12,... | collective-permute-start | bytes 3145736 | tf_op jit(solution)/shard_map/ppermute | solution.py:32
  73.2 37.5 %collective-permute-start.9 = (bf16[2,2,2,512,128]{4,3,2,1,0:T(8,128)(2,1)}, bf16[2,2,2,512,128]{4,3,2,1,0:T(8,128)(2,1)}, u32[]{:S(2)}, u32[]{:S(2)}) collective-permute-start(bf16[2,2,2,512,128]{4,3,2,1,0:T(8,128)(2,1)} %get-tuple-element.23), channel_id=1, source_target_pairs={{0,1},{1,0},{2,3},{3,2},{4,5},{5,4},{6,7},{7,6},{8,9},{9,8},{10,11... | collective-permute-start | bytes 3145736 | tf_op jit(solution)/shard_map/ppermute | solution.py:32
  73.3 16.6 %collective-permute-start.18 = (bf16[2,2,512,128]{3,2,1,0:T(8,128)(2,1)}, bf16[2,2,512,128]{3,2,1,0:T(8,128)(2,1)}, u32[]{:S(2)}, u32[]{:S(2)}) collective-permute-start(bf16[2,2,512,128]{3,2,1,0:T(8,128)(2,1)} %get-tuple-element.28.refs_4_), channel_id=1, source_target_pairs={{0,32},{32,64},{64,96},{96,0},{1,33},{33,65},{65,97},{97,1},{2,34}... | collective-permute-start | bytes 1572872 | tf_op jit(solution)/shard_map/ppermute | solution.py:27
  89.9 21.0 %collective-permute-start.10 = (bf16[2,2,512,128]{3,2,1,0:T(8,128)(2,1)}, bf16[2,2,512,128]{3,2,1,0:T(8,128)(2,1)}, u32[]{:S(2)}, u32[]{:S(2)}) collective-permute-start(bf16[2,2,512,128]{3,2,1,0:T(8,128)(2,1)} %copy-done.11), channel_id=1, source_target_pairs={{0,1},{1,0},{2,3},{3,2},{4,5},{5,4},{6,7},{7,6},{8,9},{9,8},{10,11... | collective-permute-start | bytes 1572872 | tf_op jit(solution)/shard_map/ppermute | solution.py:32
  89.9 28.4 %copy-start.3 = (bf16[1024,512]{1,0:T(8,128)(2,1)}, bf16[1024,512]{1,0:T(8,128)(2,1)S(1)}, u32[]{:S(2)}) copy-start(bf16[1024,512]{1,0:T(8,128)(2,1)S(1)} %collective-permute-done.refs_1_) | copy-start | bytes 3145732
  89.9 23.5 %collective-permute-start.11 = (bf16[2,2,512,128]{3,2,1,0:T(8,128)(2,1)}, bf16[2,2,512,128]{3,2,1,0:T(8,128)(2,1)}, u32[]{:S(2)}, u32[]{:S(2)}) collective-permute-start(bf16[2,2,512,128]{3,2,1,0:T(8,128)(2,1)} %collective-permute-done.7.refs_6_), channel_id=1, source_target_pairs={{0,1},{1,0},{2,3},{3,2},{4,5},{5,4},{6,7},{7,6},{8,9},{9,8},{10,11... | collective-permute-start | bytes 1572872 | tf_op jit(solution)/shard_map/ppermute | solution.py:32
  90.4 27.9 %copy-start.4 = (bf16[1024,512]{1,0:T(8,128)(2,1)}, bf16[1024,512]{1,0:T(8,128)(2,1)S(1)}, u32[]{:S(2)}) copy-start(bf16[1024,512]{1,0:T(8,128)(2,1)S(1)} %collective-permute-done.1.refs_2_) | copy-start | bytes 3145732
  90.4 27.9 %collective-permute-start.12 = (bf16[2,2,512,128]{3,2,1,0:T(8,128)(2,1)}, bf16[2,2,512,128]{3,2,1,0:T(8,128)(2,1)}, u32[]{:S(2)}, u32[]{:S(2)}) collective-permute-start(bf16[2,2,512,128]{3,2,1,0:T(8,128)(2,1)} %collective-permute-done.8.refs_7_), channel_id=1, source_target_pairs={{0,1},{1,0},{2,3},{3,2},{4,5},{5,4},{6,7},{7,6},{8,9},{9,8},{10,11... | collective-permute-start | bytes 1572872 | tf_op jit(solution)/shard_map/ppermute | solution.py:32
  110.1 19.5 %collective-permute-start.19 = (bf16[2,2,512,128]{3,2,1,0:T(8,128)(2,1)}, bf16[2,2,512,128]{3,2,1,0:T(8,128)(2,1)}, u32[]{:S(2)}, u32[]{:S(2)}) collective-permute-start(bf16[2,2,512,128]{3,2,1,0:T(8,128)(2,1)} %collective-permute-done.16.refs_5_), channel_id=1, source_target_pairs={{0,1},{1,0},{2,3},{3,2},{4,5},{5,4},{6,7},{7,6},{8,9},{9,8},{10,11... | collective-permute-start | bytes 1572872 | tf_op jit(solution)/shard_map/ppermute | solution.py:32
  110.7 20.0 %collective-permute-start.20 = (bf16[2,2,512,128]{3,2,1,0:T(8,128)(2,1)}, bf16[2,2,512,128]{3,2,1,0:T(8,128)(2,1)}, u32[]{:S(2)}, u32[]{:S(2)}) collective-permute-start(bf16[2,2,512,128]{3,2,1,0:T(8,128)(2,1)} %collective-permute-done.17.refs_6_), channel_id=1, source_target_pairs={{0,1},{1,0},{2,3},{3,2},{4,5},{5,4},{6,7},{7,6},{8,9},{9,8},{10,11... | collective-permute-start | bytes 1572872 | tf_op jit(solution)/shard_map/ppermute | solution.py:32
  110.8 31.2 %collective-permute-start.21 = (bf16[2,2,512,128]{3,2,1,0:T(8,128)(2,1)}, bf16[2,2,512,128]{3,2,1,0:T(8,128)(2,1)}, u32[]{:S(2)}, u32[]{:S(2)}) collective-permute-start(bf16[2,2,512,128]{3,2,1,0:T(8,128)(2,1)} %collective-permute-done.18.refs_7_), channel_id=1, source_target_pairs={{0,1},{1,0},{2,3},{3,2},{4,5},{5,4},{6,7},{7,6},{8,9},{9,8},{10,11... | collective-permute-start | bytes 1572872 | tf_op jit(solution)/shard_map/ppermute | solution.py:32
  113.4 43.5 %collective-permute-start.34 = (bf16[2,128,1024]{2,1,0:T(8,128)(2,1)}, bf16[2,128,1024]{2,1,0:T(8,128)(2,1)}, u32[]{:S(2)}, u32[]{:S(2)}) collective-permute-start(bf16[2,128,1024]{2,1,0:T(8,128)(2,1)} %get-tuple-element.46), channel_id=1, source_target_pairs={{0,12},{4,0},{8,4},{12,8},{1,13},{5,1},{9,5},{13,9},{2,14},{6,2},{... | collective-permute-start | bytes 1572872 | tf_op jit(solution)/shard_map/ppermute | solution.py:27
  118.3 41.7 %collective-permute-start.33 = (bf16[2,128,1024]{2,1,0:T(8,128)(2,1)}, bf16[2,128,1024]{2,1,0:T(8,128)(2,1)}, u32[]{:S(2)}, u32[]{:S(2)}) collective-permute-start(bf16[2,128,1024]{2,1,0:T(8,128)(2,1)} %get-tuple-element.46), channel_id=1, source_target_pairs={{0,8},{4,12},{8,0},{12,4},{1,9},{5,13},{9,1},{13,5},{2,10},{6,14},... | collective-permute-start | bytes 1572872 | tf_op jit(solution)/shard_map/ppermute | solution.py:27
  129.5 30.5 %collective-permute-start.32 = (bf16[2,128,1024]{2,1,0:T(8,128)(2,1)}, bf16[2,128,1024]{2,1,0:T(8,128)(2,1)S(1)}, u32[]{:S(2)}, u32[]{:S(2)}) collective-permute-start(bf16[2,128,1024]{2,1,0:T(8,128)(2,1)} %get-tuple-element.46), channel_id=1, source_target_pairs={{0,4},{4,8},{8,12},{12,0},{1,5},{5,9},{9,13},{13,1},{2,6},{6,10},{... | collective-permute-start | bytes 1572872 | tf_op jit(solution)/shard_map/ppermute | solution.py:27
  130.7 32.7 %collective-permute-start.13 = (bf16[1024,256]{1,0:T(8,128)(2,1)}, bf16[1024,256]{1,0:T(8,128)(2,1)S(1)}, u32[]{:S(2)}, u32[]{:S(2)}) collective-permute-start(bf16[1024,256]{1,0:T(8,128)(2,1)} %get-tuple-element.25), channel_id=1, source_target_pairs={{0,2},{2,0},{1,3},{3,1},{4,6},{6,4},{5,7},{7,5},{8,10},{10,8},{9,1... | collective-permute-start | bytes 1572872 | tf_op jit(solution)/shard_map/ppermute | solution.py:32
  138.1 34.2 %all-to-all-start = ((bf16[8,128,512]{2,1,0:T(8,128)(2,1)}), bf16[8,128,512]{2,1,0:T(8,128)(2,1)S(1)}, u32[]{:S(2)}, u32[]{:S(2)}) async-start(bf16[8,128,512]{2,1,0:T(8,128)(2,1)} %reshape.167), calls=%async_computation | async-start | bytes 2097152 | tf_op jit(solution)/shard_map/all_to_all | solution.py:22
  142.1 38.9 %collective-permute-start.14 = (bf16[1024,256]{1,0:T(8,128)(2,1)}, bf16[1024,256]{1,0:T(8,128)(2,1)}, u32[]{:S(2)}, u32[]{:S(2)}) collective-permute-start(bf16[1024,256]{1,0:T(8,128)(2,1)} %get-tuple-element.26), channel_id=1, source_target_pairs={{0,8},{8,0},{1,9},{9,1},{2,10},{10,2},{3,11},{11,3},{4,12},{12,4},... | collective-permute-start | bytes 1572872 | tf_op jit(solution)/shard_map/ppermute | solution.py:32
  156.9 24.1 %collective-permute-start.15 = (bf16[1024,256]{1,0:T(8,128)(2,1)}, bf16[1024,256]{1,0:T(8,128)(2,1)}, u32[]{:S(2)}, u32[]{:S(2)}) collective-permute-start(bf16[1024,256]{1,0:T(8,128)(2,1)} %get-tuple-element.27), channel_id=1, source_target_pairs={{0,10},{2,8},{8,2},{10,0},{1,11},{3,9},{9,3},{11,1},{4,14},{6,12},... | collective-permute-start | bytes 1572872 | tf_op jit(solution)/shard_map/ppermute | solution.py:32
  159.9 24.5 %collective-permute-start.22 = (bf16[1024,256]{1,0:T(8,128)(2,1)}, bf16[1024,256]{1,0:T(8,128)(2,1)}, u32[]{:S(2)}, u32[]{:S(2)}) collective-permute-start(bf16[1024,256]{1,0:T(8,128)(2,1)} %get-tuple-element.30), channel_id=1, source_target_pairs={{0,2},{2,0},{1,3},{3,1},{4,6},{6,4},{5,7},{7,5},{8,10},{10,8},{9,1... | collective-permute-start | bytes 1572872 | tf_op jit(solution)/shard_map/ppermute | solution.py:32
  160.0 41.3 %collective-permute-start.23 = (bf16[1024,256]{1,0:T(8,128)(2,1)}, bf16[1024,256]{1,0:T(8,128)(2,1)}, u32[]{:S(2)}, u32[]{:S(2)}) collective-permute-start(bf16[1024,256]{1,0:T(8,128)(2,1)} %get-tuple-element.31), channel_id=1, source_target_pairs={{0,8},{8,0},{1,9},{9,1},{2,10},{10,2},{3,11},{11,3},{4,12},{12,4},... | collective-permute-start | bytes 1572872 | tf_op jit(solution)/shard_map/ppermute | solution.py:32
  163.5 37.9 %collective-permute-start.24 = (bf16[1024,256]{1,0:T(8,128)(2,1)}, bf16[1024,256]{1,0:T(8,128)(2,1)}, u32[]{:S(2)}, u32[]{:S(2)}) collective-permute-start(bf16[1024,256]{1,0:T(8,128)(2,1)} %get-tuple-element.32), channel_id=1, source_target_pairs={{0,10},{2,8},{8,2},{10,0},{1,11},{3,9},{9,3},{11,1},{4,14},{6,12},... | collective-permute-start | bytes 1572872 | tf_op jit(solution)/shard_map/ppermute | solution.py:32
  172.3 29.1 %copy-start.6 = (bf16[8,128,512]{2,1,0:T(8,128)(2,1)}, bf16[8,128,512]{2,1,0:T(8,128)(2,1)S(1)}, u32[]{:S(2)}) copy-start(bf16[8,128,512]{2,1,0:T(8,128)(2,1)S(1)} %all-to-all-done.refs_8_) | copy-start | bytes 3145732
  212.4 2.9 %collective-permute-start.35 = (f32[1024,256]{1,0:T(8,128)}, f32[1024,256]{1,0:T(8,128)S(1)}, u32[]{:S(2)}, u32[]{:S(2)}) collective-permute-start(f32[1024,256]{1,0:T(8,128)} %get-tuple-element.40), channel_id=1, source_target_pairs={{0,1},{1,0},{2,3},{3,2},{4,5},{5,4},{6,7},{7,6},{8,9},{9,8},{10,11... | collective-permute-start | bytes 3145736 | tf_op jit(solution)/shard_map/ppermute | solution.py:32
  215.3 13.7 %copy-start.14 = (bf16[2,128,512]{2,1,0:T(8,128)(2,1)S(1)}, bf16[2,128,512]{2,1,0:T(8,128)(2,1)}, u32[]{:S(2)}) copy-start(bf16[2,128,512]{2,1,0:T(8,128)(2,1)} %get-tuple-element.35.refs_2_) | copy-start | bytes 786436
  215.3 14.0 %copy-start.13 = (bf16[2,128,512]{2,1,0:T(8,128)(2,1)S(1)}, bf16[2,128,512]{2,1,0:T(8,128)(2,1)}, u32[]{:S(2)}) copy-start(bf16[2,128,512]{2,1,0:T(8,128)(2,1)} %get-tuple-element.36.refs_3_) | copy-start | bytes 786436
  217.8 57.0 %all-to-all-start.1 = ((f32[128,8,256]{2,1,0:T(8,128)}), f32[128,8,256]{2,1,0:T(8,128)S(1)}, u32[]{:S(2)}, u32[]{:S(2)}) async-start(f32[128,8,256]{2,1,0:T(8,128)} %add_bitcast_fusion), calls=%async_computation.1 | async-start | bytes 2097152 | tf_op jit(solution)/shard_map/all_to_all | solution.py:22
  226.1 23.7 %collective-permute-start.25 = (bf16[2,128,512]{2,1,0:T(8,128)(2,1)S(1)}, bf16[2,128,512]{2,1,0:T(8,128)(2,1)S(1)}, u32[]{:S(2)}, u32[]{:S(2)}) collective-permute-start(bf16[2,128,512]{2,1,0:T(8,128)(2,1)S(1)} %copy-done.15), channel_id=1, source_target_pairs={{0,12},{4,0},{8,4},{12,8},{1,13},{5,1},{9,5},{13,9},{2,14},{6,2},{... | collective-permute-start | bytes 786440 | tf_op jit(solution)/shard_map/ppermute | solution.py:27
  229.0 20.8 %collective-permute-start.26 = (bf16[2,128,512]{2,1,0:T(8,128)(2,1)S(1)}, bf16[2,128,512]{2,1,0:T(8,128)(2,1)S(1)}, u32[]{:S(2)}, u32[]{:S(2)}) collective-permute-start(bf16[2,128,512]{2,1,0:T(8,128)(2,1)S(1)} %copy-done.14), channel_id=1, source_target_pairs={{0,8},{4,12},{8,0},{12,4},{1,9},{5,13},{9,1},{13,5},{2,10},{6,14},... | collective-permute-start | bytes 786440 | tf_op jit(solution)/shard_map/ppermute | solution.py:27
  229.3 23.9 %collective-permute-start.27 = (bf16[2,128,512]{2,1,0:T(8,128)(2,1)S(1)}, bf16[2,128,512]{2,1,0:T(8,128)(2,1)S(1)}, u32[]{:S(2)}, u32[]{:S(2)}) collective-permute-start(bf16[2,128,512]{2,1,0:T(8,128)(2,1)S(1)} %copy-done.13), channel_id=1, source_target_pairs={{0,4},{4,8},{8,12},{12,0},{1,5},{5,9},{9,13},{13,1},{2,6},{6,10},{... | collective-permute-start | bytes 786440 | tf_op jit(solution)/shard_map/ppermute | solution.py:27
  256.1 15.7 %collective-permute-start.28 = (bf16[4,128,512]{2,1,0:T(8,128)(2,1)}, bf16[4,128,512]{2,1,0:T(8,128)(2,1)}, u32[]{:S(2)}, u32[]{:S(2)}) collective-permute-start(bf16[4,128,512]{2,1,0:T(8,128)(2,1)} %get-tuple-element.38), channel_id=1, source_target_pairs={{0,2},{2,0},{1,3},{3,1},{4,6},{6,4},{5,7},{7,5},{8,10},{10,8},{9,1... | collective-permute-start | bytes 1572872 | tf_op jit(solution)/shard_map/ppermute | solution.py:32
  258.8 19.0 %copy-start.1 = (bf16[1024,1024]{1,0:T(8,128)(2,1)S(1)}, bf16[1024,1024]{1,0:T(8,128)(2,1)}, u32[]{:S(2)}) copy-start(bf16[1024,1024]{1,0:T(8,128)(2,1)} %param.16) | copy-start | bytes 6291460
  (10 other events, 45.6 us)
